TPU v7x, 32 devices: a whole 2x2x4 slice. The times are simulated.
32 devices in a mesh: ta: 2 (over y), ha: 4 (over z), wa: 4 (over x, core).
Axes of the slice: x: 2, y: 2, z: 4, core: 2. Of those that a mesh axis runs over, the one named last changes fastest.
Arguments:
- latents: bfloat16 [1, 8, 32, 32, 3072], P(None, 'ta', 'ha', 'wa'), may hold values from -6 to 6
- input_weight: bfloat16 [3072, 3, 16, 128], P(None, None, 'ta'), as said below
- norm_gains: float32 [2, 128], replicated, may hold values from 0.6 to 5
- output_weight: bfloat16 [16, 128, 3072], P('ta'), may hold values from -0.125 to 0.125
Outputs:
- mixed: bfloat16 [1, 8, 32, 32, 3072], P(None, 'ta', 'ha', 'wa')
Inputs may be any that keep to these rules, and one draw needn't show every extreme that they name: `input_weight`: every entry has magnitude at most 6.3 / sqrt(3072).
All inputs are finite; a program needn't handle non-finite values.
Results may differ from a plain program's by a relative error of at most 0.0077.
Values may be sent and summed in bfloat16 or wider, within the bound.
No kernel may reach another device: no remote copies, remote signals or barrier semaphores. Data moves between devices by JAX's collectives and lax.ppermute only.
A program may use at most 320 MiB of HBM per device.

v0:
```python
import math

import jax
import jax.numpy as jnp
from jax import lax
from jax.sharding import PartitionSpec as P

TILE_T = 4


EPSILON = 1e-06


def padded(cells, sides, width):
    for axis, dim in sides:
        count = lax.axis_size(axis)
        ends = count - 1
        head = lax.slice_in_dim(cells, 0, width, axis=dim)
        tail = lax.slice_in_dim(cells, cells.shape[dim] - width, cells.shape[dim], axis=dim)
        cells = jnp.concatenate(
            [
                lax.ppermute(tail, axis, [(i, (i + 1) % count) for i in range(ends)]),
                cells,
                lax.ppermute(head, axis, [((i + 1) % count, i) for i in range(ends)]),
            ],
            axis=dim,
        )
    return cells


def rms_norm(values, gain_row):
    mean_square = jnp.mean(values * values, axis=-1, keepdims=True)
    return values * lax.rsqrt(mean_square + EPSILON) * gain_row


def per_device(latents, input_weight, norm_gains, output_weight):
    clip_count = latents.shape[0]
    frames_local = latents.shape[1]
    tile_side = latents.shape[2]
    model_width = latents.shape[4]
    heads_local = input_weight.shape[2]
    head_dim = input_weight.shape[3]
    projected = jnp.einsum(
        "cfhwd,dsne->cfhwsne",
        lax.all_gather(latents, "ta", axis=1, tiled=True),
        input_weight,
        preferred_element_type=jnp.float32,
    )
    query_normed = rms_norm(projected[:, :, :, :, 0], norm_gains[0])
    key_normed = rms_norm(projected[:, :, :, :, 1], norm_gains[1])
    stacked = jnp.stack([query_normed, key_normed, projected[:, :, :, :, 2]], axis=4).astype(
        jnp.bfloat16
    )
    frames = stacked.shape[1]
    query_all = stacked[:, :, :, :, 0]
    key_value = stacked[:, :, :, :, 1:]
    beside_all = padded(key_value, (("ha", 2), ("wa", 3)), tile_side)
    height_index = lax.axis_index("ha")
    width_index = lax.axis_index("wa")
    band_rows = jnp.stack(
        [height_index > 0, height_index >= 0, height_index < lax.axis_size("ha") - 1]
    )
    band_cols = jnp.stack(
        [width_index > 0, width_index >= 0, width_index < lax.axis_size("wa") - 1]
    )
    rows_valid = jnp.repeat(band_rows, tile_side)
    cols_valid = jnp.repeat(band_cols, tile_side)
    around_mask = (rows_valid[:, None] & cols_valid[None, :]).reshape(-1)
    spatial = tile_side * tile_side
    around_len = 9 * spatial
    queries = query_all.reshape(clip_count, frames, spatial, heads_local, head_dim)
    keys_all = beside_all[:, :, :, :, 0].reshape(
        clip_count, frames, around_len, heads_local, head_dim
    )
    values_all = beside_all[:, :, :, :, 1].reshape(
        clip_count, frames, around_len, heads_local, head_dim
    )
    inv_root = 1.0 / math.sqrt(head_dim)
    tile_count = -(-frames // TILE_T)
    pieces = []
    for tile_at in range(tile_count):
        query_low = tile_at * TILE_T
        query_high = min(query_low + TILE_T, frames)
        key_low = max(query_low - TILE_T, 0)
        key_high = min(query_low + 2 * TILE_T, frames)
        query_block = queries[:, query_low:query_high].reshape(
            clip_count, (query_high - query_low) * spatial, heads_local, head_dim
        )
        key_block = keys_all.reshape(
            clip_count, (key_high - key_low) * around_len, heads_local, head_dim
        )
        value_block = values_all.reshape(
            clip_count, (key_high - key_low) * around_len, heads_local, head_dim
        )
        key_mask = jnp.tile(around_mask, key_high - key_low)
        scores = (
            jnp.einsum(
                "cqnd,cknd->ncqk", query_block, key_block, preferred_element_type=jnp.float32
            )
            * inv_root
        )
        scores = jnp.where(key_mask, scores, -1e30)
        row_peak = jnp.max(scores, axis=-1, keepdims=True)
        weights = jnp.exp(scores - row_peak)
        probability = (weights / jnp.sum(weights, axis=-1, keepdims=True)).astype(jnp.bfloat16)
        pieces.append(
            jnp.einsum(
                "ncqk,cknd->ncqd", probability, value_block, preferred_element_type=jnp.float32
            ).astype(jnp.bfloat16)
        )
    attended = jnp.concatenate(pieces, axis=2).reshape(
        heads_local, clip_count, frames, spatial, head_dim
    )
    own_rows = lax.psum_scatter(
        jnp.einsum("ncfqd,nde->fcqe", attended, output_weight, preferred_element_type=jnp.float32),
        "ta",
        scatter_dimension=0,
        tiled=True,
    )
    result = own_rows.transpose(1, 0, 2, 3).reshape(
        clip_count, frames_local, tile_side, tile_side, model_width
    )
    return result.astype(jnp.bfloat16)


def solution(mesh):
    in_specs = (
        P(None, "ta", "ha", "wa", None),
        P(None, None, "ta", None),
        P(),
        P("ta", None, None),
    )
    out_specs = P(None, "ta", "ha", "wa", None)
    return jax.shard_map(
        per_device, mesh=mesh, in_specs=in_specs, out_specs=out_specs, check_vma=False
    )
```

profile of v0, /device:TPU:16, one launch (start us, length us, event | category | flops | bytes accessed | tf_op | source)
XLA Modules:
  0.0 482.1 jit_solution(83558213477799190)
XLA Ops:
  6.5 0.7 all-gather.2.cloned.1.call-update
  7.3 0.0 reduce-scatter.2.cloned.1.call-start
  7.3 1.4 slice_bitcast_fusion.1
  8.7 46.2 %all-gather.2.cloned.1.call-done = bf16[1,8,8,8,3072]{4,3,2,0,1:T(8,128)(2,1)} async-done(((bf16[1,4,8,8,3072]{4,3,2,0,1:T(8,128)(2,1)}), bf16[1,8,8,8,3072]{4,3,2,0,1:T(8,128)(2,1)}) %all-gather.2.cloned.1.call-update) | async-done | bytes 3145744 | tf_op jit(solution)/shard_map/all_gather | solution.py:45
  54.9 14.1 %fusion.26 = f32[1,8,8,8,3,8,128]{6,3,5,4,2,1,0:T(8,128)S(1)} fusion(bf16[3072,3,8,128,1,1]{3,2,1,0,5,4:T(8,128)(2,1)} %bitcast.62, bf16[1,8,8,8,3072]{4,3,2,0,1:T(8,128)(2,1)} %all-gather.2.cloned.1.call-done), kind=kOutput, calls=%fused_computation.32 | convolution fusion | flops 9663676416 | bytes 28311552 | tf_op jit(solution)/shard_map/cfhwd,dsne->cfhwsne/dot_general | solution.py:43
  69.0 1.2 multiply_reduce_fusion.1
  70.2 0.2 slice.58
  70.4 0.1 add_rsqrt_fusion
  70.5 1.3 multiply_convert_fusion.1
  71.8 0.2 pad_maximum_fusion.2
  72.0 2.4 collective-permute-start.1
  74.4 3.5 collective-permute-start
  77.9 43.1 %collective-permute-done.1 = bf16[1,8,8,8,2,8,128]{6,3,5,4,2,1,0:T(8,128)(2,1)S(1)} collective-permute-done((bf16[1,8,8,8,2,8,128]{6,3,5,4,2,1,0:T(8,128)(2,1)S(1)}, bf16[1,8,8,8,2,8,128]{6,3,5,4,2,1,0:T(8,128)(2,1)S(1)}, u32[]{:S(2)}, u32[]{:S(2)}) %collective-permute-start.1) | collective-permute-done | bytes 2097184 | tf_op jit(solution)/shard_map/ppermute | solution.py:24
  121.1 2.2 collective-permute-done
  123.2 5.4 %pad_maximum_fusion.1 = bf16[1,8,24,8,2,8,128]{6,3,5,4,2,1,0:T(8,128)(2,1)} fusion(bf16[1,8,8,8,2,8,128]{6,3,5,4,2,1,0:T(8,128)(2,1)S(1)} %collective-permute-done.1, bf16[1,8,8,8,1,8,128]{6,3,5,4,2,1,0:T(8,128)(2,1)S(1)} %slice.58, bf16[1,8,8,8,1,8,128]{6,3,5,4,2,1,0:T(8,128)(2,1)S(1)} %get-tuple-element.10, ...), kind=kLoop, calls=%fused_computation.27 | loop fusion | flops 9437184 | bytes 12582912 | tf_op jit(solution)/shard_map/concatenate | solution.py:20
  128.6 0.0 copy-done.1
  128.6 1.3 collective-permute-start.3
  129.9 5.7 %collective-permute-start.2 = (bf16[1,8,24,8,2,8,128]{6,3,5,4,2,1,0:T(8,128)(2,1)}, bf16[1,8,24,8,2,8,128]{6,3,5,4,2,1,0:T(8,128)(2,1)}, u32[]{:S(2)}, u32[]{:S(2)}) collective-permute-start(bf16[1,8,24,8,2,8,128]{6,3,5,4,2,1,0:T(8,128)(2,1)} %pad_maximum_fusion.1), channel_id=1, source_target_pairs={{0,1},{1,2},{2,3},{4,5},{5,6},{6,7},{8,9},{9,10},{10,11},{12,13},{... | collective-permute-start | bytes 18874376 | tf_op jit(solution)/shard_map/ppermute | solution.py:22
  135.6 0.1 pad_add_fusion.1
  135.7 0.1 broadcast_in_dim.23
  135.8 0.1 and.28
  135.8 0.1 pad_add_fusion
  135.9 0.1 broadcast_in_dim.22
  136.0 0.1 and.26
  136.1 0.1 broadcast_and_fusion
  136.2 0.1 and.31
  136.3 0.1 tile.5
  136.4 0.3 copy.20
  136.7 0.1 fusion.48
  136.8 0.1 copy.21
  136.9 0.1 copy.26
  137.0 4.0 collective-permute-done.3
  141.0 2.1 collective-permute-done.2
  143.1 9.3 %pad_maximum_fusion = bf16[1,8,24,24,2,8,128]{6,3,5,4,2,1,0:T(8,128)(2,1)S(1)} fusion(bf16[1,8,24,8,2,8,128]{6,3,5,4,2,1,0:T(8,128)(2,1)} %collective-permute-done.3, bf16[1,8,8,8,2,8,128]{6,3,5,4,2,1,0:T(8,128)(2,1)} %copy-done, bf16[1,8,8,8,1,8,128]{6,3,5,4,2,1,0:T(8,128)(2,1)S(1)} %slice.58, bf16[1,8,8,8,1,8,128]{6,3,5,4,2,1,0:T(8,128)(2,1)S(1)} %get-tuple-element.10, ...), kind=kLoop, calls=%fused_computation.10 | loop fusion | flops 113246208 | bytes 37748736 | tf_op jit(solution)/shard_map/concatenate | solution.py:20
  152.4 7.5 %fusion.47 = (bf16[1,8,24,24,1,8,128]{6,3,5,4,2,1,0:T(8,128)(2,1)}, bf16[1,8,24,24,1,8,128]{6,3,5,4,2,1,0:T(8,128)(2,1)}) fusion(bf16[1,8,24,24,2,8,128]{6,3,5,4,2,1,0:T(8,128)(2,1)S(1)} %pad_maximum_fusion), kind=kLoop, calls=%fused_computation.56 | loop fusion | bytes 37748736 | tf_op jit(solution)/shard_map/slice | solution.py:72
  159.9 10.6 %copy.22 = bf16[1,8,24,24,1,8,128]{6,5,3,2,1,4,0:T(8,128)(2,1)} copy(bf16[1,8,24,24,1,8,128]{6,3,5,4,2,1,0:T(8,128)(2,1)} %get-tuple-element.7) | data formatting | bytes 18874368 | tf_op jit(solution)/shard_map/slice | solution.py:72
  170.4 10.4 %copy.24 = bf16[1,8,24,24,1,8,128]{6,5,3,2,1,4,0:T(8,128)(2,1)} copy(bf16[1,8,24,24,1,8,128]{6,3,5,4,2,1,0:T(8,128)(2,1)} %get-tuple-element.8) | data formatting | bytes 18874368 | tf_op jit(solution)/shard_map/slice | solution.py:75
  180.9 17.4 %fusion.16 = f32[8,256,4608]{2,1,0:T(8,128)} fusion(bf16[256,8,128]{2,0,1:T(8,128)(2,1)S(1)} %bitcast.59, bf16[4608,8,128]{2,1,0:T(8,128)(2,1)} %bitcast.53), kind=kOutput, calls=%fused_computation.23 | convolution fusion | flops 2415919104 | bytes 47710208 | tf_op jit(solution)/shard_map/cqnd,cknd->ncqk/dot_general | solution.py:97
  198.3 17.4 %fusion.18 = f32[8,256,4608]{2,1,0:T(8,128)} fusion(bf16[256,8,128]{2,0,1:T(8,128)(2,1)S(1)} %bitcast.58, bf16[4608,8,128]{2,1,0:T(8,128)(2,1)} %bitcast.54), kind=kOutput, calls=%fused_computation.25 | convolution fusion | flops 2415919104 | bytes 47710208 | tf_op jit(solution)/shard_map/cqnd,cknd->ncqk/dot_general | solution.py:97
  215.7 37.6 %fusion.49 = (f32[8,256]{1,0:T(8,128)S(1)}, f32[8,256,4608]{2,1,0:T(8,128)}) fusion(f32[8,256,4608]{2,1,0:T(8,128)} %fusion.16, pred[4608]{0:T(1024)(128)(4,1)S(1)} %tile.5), kind=kOutput, calls=%fused_computation.58 | output fusion | flops 56627712 | bytes 75510272 | tf_op jit(solution)/shard_map/sub | solution.py:104
  253.3 37.6 %fusion.50 = (f32[8,256]{1,0:T(8,128)S(1)}, f32[8,256,4608]{2,1,0:T(8,128)}) fusion(f32[8,256,4608]{2,1,0:T(8,128)} %fusion.18, pred[4608]{0:T(1024)(128)(4,1)S(1)} %tile.5), kind=kOutput, calls=%fused_computation.59 | output fusion | flops 56627712 | bytes 75510272 | tf_op jit(solution)/shard_map/sub | solution.py:104
  291.0 18.0 %fusion.40 = bf16[8,1,256,128]{3,2,0,1:T(8,128)(2,1)S(1)} fusion(bf16[4608,8,128]{2,1,0:T(8,128)(2,1)} %bitcast.55, f32[8,256,4608]{2,1,0:T(8,128)} %get-tuple-element.16, f32[8,256]{1,0:T(8,128)S(1)} %get-tuple-element.15), kind=kOutput, calls=%fused_computation.43 | convolution fusion | flops 2435055616 | bytes 47718400 | tf_op jit(solution)/shard_map/ncqk,cknd->ncqd/dot_general | solution.py:107
  309.0 18.2 %fusion.37 = bf16[8,1,256,128]{3,2,0,1:T(8,128)(2,1)S(1)} fusion(bf16[4608,8,128]{2,1,0:T(8,128)(2,1)} %bitcast.56, f32[8,256,4608]{2,1,0:T(8,128)} %get-tuple-element.18, f32[8,256]{1,0:T(8,128)S(1)} %get-tuple-element.17), kind=kOutput, calls=%fused_computation.42 | convolution fusion | flops 2435055616 | bytes 47718400 | tf_op jit(solution)/shard_map/ncqk,cknd->ncqd/dot_general | solution.py:107
  327.1 0.1 pad_maximum_fusion.3
  327.2 7.2 %fusion.22 = f32[8,1,64,3072]{3,2,0,1:T(8,128)} fusion(bf16[8,8,64,128]{3,2,1,0:T(8,128)(2,1)S(1)} %bitcast.61, bf16[8,128,3072]{2,1,0:T(8,128)(2,1)} %param.7), kind=kOutput, calls=%fused_computation.30 | convolution fusion | flops 3221225472 | bytes 13631488 | tf_op jit(solution)/shard_map/ncfqd,nde->fcqe/dot_general | solution.py:115
  334.4 0.0 reduce-scatter.2.cloned.1.call-update
  334.5 137.5 %reduce-scatter.2.cloned.1.call-done = f32[4,1,64,3072]{3,2,0,1:T(8,128)} async-done(((f32[8,1,64,3072]{3,2,0,1:T(8,128)}), f32[4,1,64,3072]{3,2,0,1:T(8,128)}) %reduce-scatter.2.cloned.1.call-update) | async-done | bytes 3145744 | tf_op jit(solution)/shard_map/reduce_scatter | solution.py:114
  472.0 3.2 convert_bitcast_fusion
  (9 shorter events, 0.0 us)
Async XLA Ops:
  6.5 48.4 %all-gather.2.cloned.1.call-start = ((), (), s32[]{:S(2)}) async-start(), calls=%async_computation.1 | async-start | bytes 4718592 | tf_op jit(solution)/shard_map/all_gather | solution.py:45
  7.3 464.7 %reduce-scatter.2.cloned.1.call-start = ((), (), s32[]{:S(2)}) async-start(), calls=%async_computation.2 | async-start | bytes 9437184 | tf_op jit(solution)/shard_map/reduce_scatter | solution.py:114
  54.9 15.6 %copy-start.2 = (f32[128]{0:T(128)S(1)}, f32[128]{0:T(128)}, u32[]{:S(2)}) copy-start(f32[128]{0:T(128)} %get-tuple-element.13) | copy-start | bytes 1540
  54.9 15.6 %copy-start.3 = (f32[128]{0:T(128)S(1)}, f32[128]{0:T(128)}, u32[]{:S(2)}) copy-start(f32[128]{0:T(128)} %get-tuple-element.14) | copy-start | bytes 1540
  72.0 49.1 %collective-permute-start.1 = (bf16[1,8,8,8,2,8,128]{6,3,5,4,2,1,0:T(8,128)(2,1)S(1)}, bf16[1,8,8,8,2,8,128]{6,3,5,4,2,1,0:T(8,128)(2,1)S(1)}, u32[]{:S(2)}, u32[]{:S(2)}) collective-permute-start(bf16[1,8,8,8,2,8,128]{6,3,5,4,2,1,0:T(8,128)(2,1)S(1)} %pad_maximum_fusion.2), channel_id=1, source_target_pairs={{4,0},{8,4},{12,8},{5,1},{9,5},{13,9},{6,2},{10,6},{14,10},{7,3},{... | collective-permute-start | bytes 6291464 | tf_op jit(solution)/shard_map/ppermute | solution.py:24
  74.4 48.8 %collective-permute-start = (bf16[1,8,8,8,2,8,128]{6,3,5,4,2,1,0:T(8,128)(2,1)S(1)}, bf16[1,8,8,8,2,8,128]{6,3,5,4,2,1,0:T(8,128)(2,1)S(1)}, u32[]{:S(2)}, u32[]{:S(2)}) collective-permute-start(bf16[1,8,8,8,2,8,128]{6,3,5,4,2,1,0:T(8,128)(2,1)S(1)} %pad_maximum_fusion.2), channel_id=1, source_target_pairs={{0,4},{4,8},{8,12},{1,5},{5,9},{9,13},{2,6},{6,10},{10,14},{3,7},{... | collective-permute-start | bytes 6291464 | tf_op jit(solution)/shard_map/ppermute | solution.py:22
  121.1 2.2 copy-start
  123.2 5.4 %copy-start.1 = (bf16[1,8,8,8,2,8,128]{6,3,5,4,2,1,0:T(8,128)(2,1)}, bf16[1,8,8,8,2,8,128]{6,3,5,4,2,1,0:T(8,128)(2,1)S(1)}, u32[]{:S(2)}) copy-start(bf16[1,8,8,8,2,8,128]{6,3,5,4,2,1,0:T(8,128)(2,1)S(1)} %collective-permute-done) | copy-start | bytes 6291460
  128.6 12.4 %collective-permute-start.3 = (bf16[1,8,24,8,2,8,128]{6,3,5,4,2,1,0:T(8,128)(2,1)}, bf16[1,8,24,8,2,8,128]{6,3,5,4,2,1,0:T(8,128)(2,1)}, u32[]{:S(2)}, u32[]{:S(2)}) collective-permute-start(bf16[1,8,24,8,2,8,128]{6,3,5,4,2,1,0:T(8,128)(2,1)} %pad_maximum_fusion.1), channel_id=1, source_target_pairs={{1,0},{2,1},{3,2},{5,4},{6,5},{7,6},{9,8},{10,9},{11,10},{13,12},{... | collective-permute-start | bytes 18874376 | tf_op jit(solution)/shard_map/ppermute | solution.py:24
  129.9 13.2 %collective-permute-start.2 = (bf16[1,8,24,8,2,8,128]{6,3,5,4,2,1,0:T(8,128)(2,1)}, bf16[1,8,24,8,2,8,128]{6,3,5,4,2,1,0:T(8,128)(2,1)}, u32[]{:S(2)}, u32[]{:S(2)}) collective-permute-start(bf16[1,8,24,8,2,8,128]{6,3,5,4,2,1,0:T(8,128)(2,1)} %pad_maximum_fusion.1), channel_id=1, source_target_pairs={{0,1},{1,2},{2,3},{4,5},{5,6},{6,7},{8,9},{9,10},{10,11},{12,13},{... | collective-permute-start | bytes 18874376 | tf_op jit(solution)/shard_map/ppermute | solution.py:22
Sparse Core Ops, SparseCore 0:
  8.9 45.9 all-gather.1
  334.6 137.3 reduce-scatter.1
where the time goes:
time: 484 us; the launch traced here: 482 us
  waiting for transfers between devices  236 us (49%)
  other arithmetic  96.2 us (20%)
  matrix products  92.3 us (19%)
  local copies, waits for them, and re-layouts  31.2 us (6%)
  between operations  13.6 us (3%)
  starting transfers between devices  13 us (3%)
    reduce_scatter x1, waiting for transfers between devices, per_device(): lax.psum_scatter(jnp.einsum('ncfqd,nde->fcqe', attended, output_weight, p...  138 us
    sub x2, other arithmetic, per_device(): weights = jnp.exp(scores - row_peak)  75.3 us
    ppermute x2, waiting for transfers between devices, padded(): lax.ppermute(head, axis, [((i + 1) % count, i) for i in range(ends)])  47.1 us
    all_gather x1, waiting for transfers between devices, per_device(): lax.all_gather(latents, 'ta', axis=1, tiled=True)  46.2 us
    dot_general x2, matrix products, per_device(): jnp.einsum('ncqk,cknd->ncqd', probability, value_block, preferred_element...  36.1 us
    dot_general x2, matrix products, per_device(): jnp.einsum('cqnd,cknd->ncqk', query_block, key_block, preferred_element_t...  34.8 us
    slice x2, local copies, waits for them, and re-layouts, per_device(): beside_all[:, :, :, :, 0]  18.1 us
    concatenate x2, other arithmetic, padded(): jnp.concatenate([lax.ppermute(tail, axis, [(i, (i + 1) % count) for i in...  14.7 us
  transfers between devices with their start and end apart: 6, of which 6 were waited for; matrix products, arithmetic and copies ran while one was open for 1% of the time, Pallas kernels for 0%

commit v1 on v0

--- a/solution.py
+++ b/solution.py
@@ -1,8 +1,11 @@
+import functools
 import math
 
 import jax
 import jax.numpy as jnp
 from jax import lax
+from jax.experimental import pallas as pl
+from jax.experimental.pallas import tpu as pltpu
 from jax.sharding import PartitionSpec as P
 
 TILE_T = 4
@@ -33,7 +36,7 @@
     return values * lax.rsqrt(mean_square + EPSILON) * gain_row
 
 
-def per_device(latents, input_weight, norm_gains, output_weight):
+def halo_plan(latents, input_weight, norm_gains, output_weight):
     clip_count = latents.shape[0]
     frames_local = latents.shape[1]
     tile_side = latents.shape[2]
@@ -123,6 +126,149 @@
     return result.astype(jnp.bfloat16)
 
 
+def shift_perm(count, by):
+    return [(i, (i + by) % count) for i in range(count)]
+
+
+def attention_kernel(groups, columns, scale, valid_ref, query_ref, *refs):
+    kv_refs, out_ref, peak_ref, total_ref, sum_ref = refs[:-4], refs[-4], refs[-3], refs[-2], refs[-1]
+    column = pl.program_id(1)
+    edge = (column == 0) | (column == columns - 1)
+    to_exp2 = scale * math.log2(math.e)
+
+    def one_row(row, start, width):
+        query = query_ref[0, 0, 0]
+        scores, values = [], []
+        for group in range(groups):
+            ref = kv_refs[row * groups + group]
+            tokens = ref.shape[3]
+            first = ref.shape[2] - 2
+            key = ref[pl.ds(start, width), 0, first].reshape(width * tokens, -1)
+            values.append(ref[pl.ds(start, width), 0, first + 1].reshape(width * tokens, -1))
+            scores.append(
+                lax.dot_general(
+                    query, key, (((1,), (1,)), ((), ())), preferred_element_type=jnp.float32
+                )
+            )
+        peak = scores[0].max(axis=1, keepdims=True)
+        for score in scores[1:]:
+            peak = jnp.maximum(peak, score.max(axis=1, keepdims=True))
+        if row > 0:
+            before = peak_ref[...]
+            peak = jnp.maximum(peak, before)
+            fade = jnp.exp2((before - peak) * to_exp2)
+        offset = peak * to_exp2
+        total, summed = 0.0, 0.0
+        for score, value in zip(scores, values):
+            weight = jnp.exp2(score * to_exp2 - offset)
+            total = total + weight.sum(axis=1, keepdims=True)
+            summed = summed + jnp.dot(
+                weight.astype(jnp.bfloat16), value, preferred_element_type=jnp.float32
+            )
+        if row > 0:
+            total = total + total_ref[...] * fade
+            summed = summed + sum_ref[...] * fade
+        peak_ref[...] = peak
+        total_ref[...] = total
+        sum_ref[...] = summed
+
+    def all_rows(start, width):
+        one_row(0, start, width)
+        for row in (1, 2):
+            pl.when(valid_ref[row - 1] > 0)(lambda row=row: one_row(row, start, width))
+
+    pl.when(edge)(lambda: all_rows(jnp.where(column == 0, 0, columns - 2), 2))
+    pl.when(jnp.logical_not(edge))(lambda: all_rows(column - 1, 3))
+    out_ref[0, 0] = (sum_ref[...] / total_ref[...]).astype(out_ref.dtype)
+
+
+def attend(valid, stream, rows, scale):
+    columns, heads, _, tokens, head_dim = stream.shape
+    groups = len(rows) // 3
+    keys = sum(kv.shape[3] for kv in rows) * 10 // 4
+
+    def kv_spec(kv):
+        return pl.BlockSpec(
+            (columns, 1, kv.shape[2], kv.shape[3], head_dim), lambda h, c, v: (0, h, 0, 0, 0)
+        )
+
+    pairs = heads * columns * tokens * keys
+    return pl.pallas_call(
+        functools.partial(attention_kernel, groups, columns, scale),
+        grid_spec=pltpu.PrefetchScalarGridSpec(
+            num_scalar_prefetch=1,
+            grid=(heads, columns),
+            in_specs=[
+                pl.BlockSpec((1, 1, 1, tokens, head_dim), lambda h, c, v: (c, h, 0, 0, 0))
+            ]
+            + [kv_spec(kv) for kv in rows],
+            out_specs=pl.BlockSpec((1, 1, tokens, head_dim), lambda h, c, v: (c, h, 0, 0)),
+            scratch_shapes=[
+                pltpu.VMEM((tokens, 1), jnp.float32),
+                pltpu.VMEM((tokens, 1), jnp.float32),
+                pltpu.VMEM((tokens, head_dim), jnp.float32),
+            ],
+        ),
+        out_shape=jax.ShapeDtypeStruct((columns, heads, tokens, head_dim), jnp.bfloat16),
+        cost_estimate=pl.CostEstimate(
+            flops=pairs * head_dim * 8, bytes_accessed=pairs * 4, transcendentals=pairs
+        ),
+        name="tile_attention",
+    )(valid, stream, *rows)
+
+
+def row_plan(latents, input_weight, norm_gains, output_weight):
+    frame_parts = lax.axis_size("ta")
+    row_parts = lax.axis_size("ha")
+    col_parts = lax.axis_size("wa")
+    model_width = latents.shape[-1]
+    tokens = math.prod(latents.shape[:-1])
+    heads_local, head_dim = input_weight.shape[2:]
+    heads_each = heads_local // col_parts
+    own = latents.reshape(tokens, model_width)
+    groups = [own]
+    for by in range(1, frame_parts):
+        groups.append(lax.ppermute(own, "ta", shift_perm(frame_parts, by)))
+    gains = jnp.concatenate([norm_gains, jnp.ones_like(norm_gains[:1])])[:, None, :]
+    is_value = jnp.arange(3).reshape(3, 1, 1) == 2
+
+    def project(group):
+        projected = jnp.einsum(
+            "td,dsne->nste", group, input_weight, preferred_element_type=jnp.float32
+        )
+        mean_square = jnp.mean(projected * projected, axis=-1, keepdims=True)
+        factor = jnp.where(is_value, 1.0, lax.rsqrt(mean_square + EPSILON))
+        normed = (projected * factor * gains).astype(jnp.bfloat16)
+        dealt = normed.reshape(col_parts, heads_each, 3, tokens, head_dim)
+        return lax.all_to_all(dealt, "wa", 0, 0)
+
+    streams = [project(group) for group in groups]
+    down = [(i, i + 1) for i in range(row_parts - 1)]
+    up = [(i + 1, i) for i in range(row_parts - 1)]
+    rows = list(streams)
+    for perm in (down, up):
+        rows += [lax.ppermute(stream[:, :, 1:], "ha", perm) for stream in streams]
+    height_index = lax.axis_index("ha")
+    valid = jnp.stack([height_index > 0, height_index < row_parts - 1]).astype(jnp.int32)
+    scale = 1.0 / math.sqrt(head_dim)
+
+    def shares(stream):
+        attended = lax.all_to_all(attend(valid, stream, rows, scale), "wa", 0, 0)
+        attended = attended.reshape(heads_local, tokens, head_dim)
+        return jnp.einsum(
+            "nte,ned->td", attended, output_weight, preferred_element_type=jnp.float32
+        )
+
+    arrived = []
+    for by in range(1, frame_parts):
+        share = shares(streams[by]).astype(jnp.bfloat16)
+        arrived.append(lax.ppermute(share, "ta", shift_perm(frame_parts, -by)))
+    result = shares(streams[0])
+    for share in arrived:
+        result = result + share.astype(jnp.float32)
+    return result.astype(jnp.bfloat16).reshape(latents.shape)
+
+
 def solution(mesh):
     in_specs = (
         P(None, "ta", "ha", "wa", None),
@@ -131,6 +277,14 @@
         P("ta", None, None),
     )
     out_specs = P(None, "ta", "ha", "wa", None)
+
+    def per_device(latents, input_weight, norm_gains, output_weight):
+        frames = latents.shape[1] * lax.axis_size("ta")
+        dealt_heads = input_weight.shape[2] % lax.axis_size("wa") == 0
+        if latents.shape[0] == 1 and dealt_heads and frames <= 2 * TILE_T:
+            return row_plan(latents, input_weight, norm_gains, output_weight)
+        return halo_plan(latents, input_weight, norm_gains, output_weight)
+
     return jax.shard_map(
         per_device, mesh=mesh, in_specs=in_specs, out_specs=out_specs, check_vma=False
     )

time: 484 us -> 238 us (0.49)
  waiting for transfers between devices: 236 us -> 77 us
  other arithmetic: 96.2 us -> 3.78 us
  matrix products: 92.3 us -> 27.7 us
  Pallas kernels: 0 us -> 51.4 us
  blocking collectives: 0 us -> 24.5 us
  between operations: 13.6 us -> 0.12 us
  starting transfers between devices: 13 us -> 22 us
    reduce_scatter x1 -> x0, waiting for transfers between devices: 138 us -> none  [per_device(): lax.psum_scatter(jnp.einsum('ncfqd,nde->fcqe', attended, output_weight, p...]
    sub x2 -> x0, other arithmetic: 75.3 us -> none  [per_device(): weights = jnp.exp(scores - row_peak)]
    dot_general x6 -> x4, matrix products: 92.3 us -> 27.7 us  [the longest x2 17.2 us: project(): jnp.einsum('td,dsne->nste', group, input_weight, preferred_element_type=j...]
    pallas_call x0 -> x2, Pallas kernels: none -> 51.4 us  [attend(): pl.pallas_call(functools.partial(attention_kernel, groups, columns, scale...]
    all_gather x1 -> x0, waiting for transfers between devices: 46.2 us -> none  [per_device(): lax.all_gather(latents, 'ta', axis=1, tiled=True)]
    all_to_all x0 -> x2, waiting for transfers between devices: none -> 33.8 us  [project(): return lax.all_to_all(dealt, 'wa', 0, 0)]
    slice x8 -> x2, local copies, waits for them, and re-layouts: 29.3 us -> 2.24 us  [row_plan(): rows += [lax.ppermute(stream[:, :, 1:], 'ha', perm) for stream in streams]]
    unnamed x8 -> x13, local copies, waits for them, and re-layouts: 0.01 us -> 25.2 us
  transfers between devices with their start and end apart: 6 -> 8, of which waited for: 6 -> 6; matrix products, arithmetic and copies ran while one was open for 1% -> 16% of each run, Pallas kernels for 0% -> 11%
where the time goes in v1:
time: 238 us; the launch traced here: 237 us
  waiting for transfers between devices  77 us (32%)
  Pallas kernels  51.4 us (22%)
  local copies, waits for them, and re-layouts  30.6 us (13%)
  matrix products  27.7 us (12%)
  blocking collectives  24.5 us (10%)
  starting transfers between devices  22 us (9%)
  other arithmetic  3.78 us (2%)
    pallas_call x2, Pallas kernels, attend(): pl.pallas_call(functools.partial(attention_kernel, groups, columns, scale...  51.4 us
    ppermute x4, waiting for transfers between devices, row_plan(): rows += [lax.ppermute(stream[:, :, 1:], 'ha', perm) for stream in streams]  42.6 us
    all_to_all x2, waiting for transfers between devices, project(): return lax.all_to_all(dealt, 'wa', 0, 0)  33.8 us
    unnamed x13, local copies, waits for them, and re-layouts  25.2 us
    all_to_all x2, blocking collectives, shares(): attended = lax.all_to_all(attend(valid, stream, rows, scale), 'wa', 0, 0)  24.5 us
    dot_general x2, matrix products, project(): jnp.einsum('td,dsne->nste', group, input_weight, preferred_element_type=j...  17.2 us
    ppermute x4, starting transfers between devices, row_plan(): rows += [lax.ppermute(stream[:, :, 1:], 'ha', perm) for stream in streams]  12.8 us
    dot_general x2, matrix products, shares(): jnp.einsum('nte,ned->td', attended, output_weight, preferred_element_type...  10.5 us
  transfers between devices with their start and end apart: 8, of which 6 were waited for; matrix products, arithmetic and copies ran while one was open for 16% of the time, Pallas kernels for 11%

profile of v1, /device:TPU:16, one launch (start us, length us, event | category | flops | bytes accessed | tf_op | source)
XLA Modules:
  0.0 237.1 jit_solution(11881612399733488076)
XLA Ops:
  0.0 0.0 copy-start.3
  0.0 0.0 copy-start.4
  0.0 1.5 collective-permute-start
  1.5 24.1 %copy.5 = bf16[3072,3,8,128]{0,3,2,1:T(8,128)(2,1)} copy(bf16[3072,3,8,128]{3,2,1,0:T(8,128)(2,1)} %param.5) | data formatting | bytes 37748736 | tf_op args[1]
  25.6 0.0 copy-done.3
  25.7 0.0 copy-done.4
  25.7 0.0 copy-start
  25.7 10.1 %fusion.6 = (f32[8,3,256]{2,0,1:T(8,128)S(1)}, f32[3,8,128,256]{3,2,1,0:T(8,128)S(1)}) fusion(bf16[3072,3,8,128]{0,3,2,1:T(8,128)(2,1)} %copy.5, bf16[256,3072,1,1]{1,0,3,2:T(8,128)(2,1)S(1)} %bitcast.57), kind=kOutput, calls=%fused_computation.12 | convolution fusion | flops 4833404928 | bytes 23617536 | tf_op jit(solution)/shard_map/td,dsne->nste/dot_general | solution.py:236
  35.8 0.5 collective-permute-done
  36.4 1.1 copy-done
  37.4 7.1 %fusion.3 = (f32[8,3,256]{2,0,1:T(8,128)S(1)}, f32[3,8,128,256]{3,2,1,0:T(8,128)}) fusion(bf16[3072,3,8,128]{0,3,2,1:T(8,128)(2,1)S(1)} %copy-done, bf16[256,3072]{1,0:T(8,128)(2,1)S(1)} %collective-permute-done), kind=kOutput, calls=%fused_computation.7 | convolution fusion | flops 4833404928 | bytes 23617536 | tf_op jit(solution)/shard_map/td,dsne->nste/dot_general | solution.py:236
  44.5 0.1 rsqrt_select_fusion
  44.6 3.0 %fusion.5 = (bf16[8,3,256,128]{2,3,0,1:T(8,128)(2,1)S(1)}, bf16[8,3,256,128]{2,3,0,1:T(8,128)(2,1)S(1)}) fusion(f32[3,8,128,256]{3,2,1,0:T(8,128)} %get-tuple-element.10, f32[8,3,256]{2,0,1:T(8,128)S(1)} %get-tuple-element.7, f32[3,128]{1,0:T(4,128)S(1)} %concatenate.3, f32[8,3,256]{2,0,1:T(8,128)S(1)} %get-tuple-element.8, ...), kind=kLoop, calls=%fused_computation.9 | loop fusion | flops 4718592 | bytes 9487872 | tf_op jit(solution)/shard_map/convert_element_type | solution.py:241
  47.6 1.6 copy.6
  49.2 3.6 %all-to-all-start = ((bf16[4,2,3,256,128]{4,3,2,1,0:T(8,128)(2,1)}), bf16[4,2,3,256,128]{4,3,2,1,0:T(8,128)(2,1)S(1)}, u32[]{:S(2)}, u32[]{:S(2)}) async-start(bf16[4,2,3,256,128]{4,3,2,1,0:T(8,128)(2,1)} %bitcast.6), calls=%async_computation | async-start | bytes 3145728 | tf_op jit(solution)/shard_map/all_to_all | solution.py:243
  52.8 1.6 copy.8
  54.4 18.4 %all-to-all-done.query_ref.refs_0_ = bf16[4,2,3,256,128]{4,3,2,1,0:T(8,128)(2,1)S(1)} async-done(((bf16[4,2,3,256,128]{4,3,2,1,0:T(8,128)(2,1)}), bf16[4,2,3,256,128]{4,3,2,1,0:T(8,128)(2,1)S(1)}, u32[]{:S(2)}, u32[]{:S(2)}) %all-to-all-start) | async-done | bytes 1572896 | tf_op jit(solution)/shard_map/all_to_all | solution.py:243
  72.8 0.0 copy-start.1
  72.8 3.6 %all-to-all-start.1 = ((bf16[4,2,3,256,128]{4,3,2,1,0:T(8,128)(2,1)}), bf16[4,2,3,256,128]{4,3,2,1,0:T(8,128)(2,1)S(1)}, u32[]{:S(2)}, u32[]{:S(2)}) async-start(bf16[4,2,3,256,128]{4,3,2,1,0:T(8,128)(2,1)} %bitcast.10), calls=%async_computation.1 | async-start | bytes 3145728 | tf_op jit(solution)/shard_map/all_to_all | solution.py:243
  76.4 1.1 slice.10
  77.5 3.5 %collective-permute-start.1 = (bf16[4,2,2,256,128]{4,3,2,1,0:T(8,128)(2,1)}, bf16[4,2,2,256,128]{4,3,2,1,0:T(8,128)(2,1)}, u32[]{:S(2)}, u32[]{:S(2)}) collective-permute-start(bf16[4,2,2,256,128]{4,3,2,1,0:T(8,128)(2,1)} %slice.10), channel_id=1, source_target_pairs={{0,4},{4,8},{8,12},{1,5},{5,9},{9,13},{2,6},{6,10},{10,14},{3,7},{... | collective-permute-start | bytes 3145736 | tf_op jit(solution)/shard_map/ppermute | solution.py:250
  80.9 15.4 %all-to-all-done.1.refs_1_.query_ref = bf16[4,2,3,256,128]{4,3,2,1,0:T(8,128)(2,1)S(1)} async-done(((bf16[4,2,3,256,128]{4,3,2,1,0:T(8,128)(2,1)}), bf16[4,2,3,256,128]{4,3,2,1,0:T(8,128)(2,1)S(1)}, u32[]{:S(2)}, u32[]{:S(2)}) %all-to-all-start.1) | async-done | bytes 1572896 | tf_op jit(solution)/shard_map/all_to_all | solution.py:243
  96.4 0.0 copy-start.2
  96.4 1.2 slice.11
  97.5 0.0 copy-done.1
  97.5 3.5 %collective-permute-start.2 = (bf16[4,2,2,256,128]{4,3,2,1,0:T(8,128)(2,1)}, bf16[4,2,2,256,128]{4,3,2,1,0:T(8,128)(2,1)}, u32[]{:S(2)}, u32[]{:S(2)}) collective-permute-start(bf16[4,2,2,256,128]{4,3,2,1,0:T(8,128)(2,1)} %slice.11), channel_id=1, source_target_pairs={{0,4},{4,8},{8,12},{1,5},{5,9},{9,13},{2,6},{6,10},{10,14},{3,7},{... | collective-permute-start | bytes 3145736 | tf_op jit(solution)/shard_map/ppermute | solution.py:250
  101.0 2.4 collective-permute-start.3
  103.4 3.5 %collective-permute-start.4 = (bf16[4,2,2,256,128]{4,3,2,1,0:T(8,128)(2,1)}, bf16[4,2,2,256,128]{4,3,2,1,0:T(8,128)(2,1)}, u32[]{:S(2)}, u32[]{:S(2)}) collective-permute-start(bf16[4,2,2,256,128]{4,3,2,1,0:T(8,128)(2,1)} %slice.11), channel_id=1, source_target_pairs={{4,0},{8,4},{12,8},{5,1},{9,5},{13,9},{6,2},{10,6},{14,10},{7,3},{... | collective-permute-start | bytes 3145736 | tf_op jit(solution)/shard_map/ppermute | solution.py:250
  106.9 0.7 add_convert_fusion.valid_ref
  107.6 0.0 collective-permute-done.1.refs_2_
  107.6 20.1 %collective-permute-done.2.refs_3_ = bf16[4,2,2,256,128]{4,3,2,1,0:T(8,128)(2,1)} collective-permute-done((bf16[4,2,2,256,128]{4,3,2,1,0:T(8,128)(2,1)}, bf16[4,2,2,256,128]{4,3,2,1,0:T(8,128)(2,1)}, u32[]{:S(2)}, u32[]{:S(2)}) %collective-permute-start.2) | collective-permute-done | bytes 1048608 | tf_op jit(solution)/shard_map/ppermute | solution.py:250
  127.7 1.5 collective-permute-done.3.refs_4_
  129.2 0.0 copy-start.5
  129.2 21.0 %collective-permute-done.4.refs_5_ = bf16[4,2,2,256,128]{4,3,2,1,0:T(8,128)(2,1)} collective-permute-done((bf16[4,2,2,256,128]{4,3,2,1,0:T(8,128)(2,1)}, bf16[4,2,2,256,128]{4,3,2,1,0:T(8,128)(2,1)}, u32[]{:S(2)}, u32[]{:S(2)}) %collective-permute-start.4) | collective-permute-done | bytes 1048608 | tf_op jit(solution)/shard_map/ppermute | solution.py:250
  150.1 0.0 copy-done.2
  150.1 0.0 copy-done.5
  150.1 25.7 %tile_attention.3 = bf16[4,2,256,128]{3,2,1,0:T(8,128)(2,1)} custom-call(s32[2]{0:T(128)} %add_convert_fusion.valid_ref, bf16[4,2,3,256,128]{4,3,2,1,0:T(8,128)(2,1)} %copy-done.2, bf16[4,2,3,256,128]{4,3,2,1,0:T(8,128)(2,1)} %copy-done.1, bf16[4,2,3,256,128]{4,3,2,1,0:T(8,128)(2,1)} %copy-done.2, ...), custom_call_target="tpu_custom_call" | custom-call | flops 8053063680 | bytes 31457280 | tf_op jit(solution)/shard_map/tile_attention/pallas_call | solution.py:196
  175.8 12.3 %all_to_all.20 = bf16[4,2,256,128]{3,2,1,0:T(8,128)(2,1)S(1)} all-to-all(bf16[4,2,256,128]{3,2,1,0:T(8,128)(2,1)} %tile_attention.3), channel_id=1, replica_groups=mesh['ta'=2,'ha'=4,'wa'=4] {'wa'}, dimensions={0} | all-to-all | bytes 1048576 | tf_op jit(solution)/shard_map/all_to_all | solution.py:256
  188.1 4.7 %fusion.1 = bf16[256,3072]{1,0:T(8,128)(2,1)S(1)} fusion(bf16[8,256,128]{2,1,0:T(8,128)(2,1)S(1)} %bitcast.55, bf16[8,128,3072]{2,1,0:T(8,128)(2,1)} %param.7), kind=kOutput, calls=%fused_computation.3 | convolution fusion | flops 1611399168 | bytes 8388608 | tf_op jit(solution)/shard_map/nte,ned->td/dot_general | solution.py:258
  192.8 0.6 collective-permute-start.5
  193.3 25.7 %tile_attention.2 = bf16[4,2,256,128]{3,2,1,0:T(8,128)(2,1)} custom-call(s32[2]{0:T(128)} %add_convert_fusion.valid_ref, bf16[4,2,3,256,128]{4,3,2,1,0:T(8,128)(2,1)} %copy-done.1, bf16[4,2,3,256,128]{4,3,2,1,0:T(8,128)(2,1)} %copy-done.1, bf16[4,2,3,256,128]{4,3,2,1,0:T(8,128)(2,1)} %copy-done.2, ...), custom_call_target="tpu_custom_call" | custom-call | flops 8053063680 | bytes 31457280 | tf_op jit(solution)/shard_map/tile_attention/pallas_call | solution.py:196
  219.1 12.3 %all_to_all.21 = bf16[4,2,256,128]{3,2,1,0:T(8,128)(2,1)S(1)} all-to-all(bf16[4,2,256,128]{3,2,1,0:T(8,128)(2,1)} %tile_attention.2), channel_id=1, replica_groups=mesh['ta'=2,'ha'=4,'wa'=4] {'wa'}, dimensions={0} | all-to-all | bytes 1048576 | tf_op jit(solution)/shard_map/all_to_all | solution.py:256
  231.3 0.0 collective-permute-done.5
  231.3 5.8 %fusion.2 = bf16[256,3072]{1,0:T(8,128)(2,1)} fusion(bf16[8,256,128]{2,1,0:T(8,128)(2,1)S(1)} %bitcast.54, bf16[8,128,3072]{2,1,0:T(8,128)(2,1)} %param.7, bf16[256,3072]{1,0:T(8,128)(2,1)S(1)} %collective-permute-done.5), kind=kOutput, calls=%fused_computation.4 | convolution fusion | flops 1612972032 | bytes 9961472 | tf_op jit(solution)/shard_map/nte,ned->td/dot_general | solution.py:258
  (2 shorter events, 0.0 us)
Async XLA Ops:
  0.0 25.6 %copy-start.3 = (f32[2,128]{1,0:T(2,128)S(1)}, f32[2,128]{1,0:T(2,128)}, u32[]{:S(2)}) copy-start(f32[2,128]{1,0:T(2,128)} %param.6) | copy-start | bytes 3076
  0.0 25.7 %copy-start.4 = (bf16[1,4,8,8,3072]{4,3,2,1,0:T(8,128)(2,1)S(1)}, bf16[1,4,8,8,3072]{4,3,2,1,0:T(8,128)(2,1)}, u32[]{:S(2)}) copy-start(bf16[1,4,8,8,3072]{4,3,2,1,0:T(8,128)(2,1)} %param.4) | copy-start | bytes 4718596
  0.0 36.3 %collective-permute-start = (bf16[256,3072]{1,0:T(8,128)(2,1)}, bf16[256,3072]{1,0:T(8,128)(2,1)S(1)}, u32[]{:S(2)}, u32[]{:S(2)}) collective-permute-start(bf16[256,3072]{1,0:T(8,128)(2,1)} %bitcast.56), channel_id=1, source_target_pairs={{0,16},{16,0},{1,17},{17,1},{2,18},{18,2},{3,19},{19,3},{4,20},{20... | collective-permute-start | bytes 4718600 | tf_op jit(solution)/shard_map/ppermute | solution.py:231
  25.7 11.7 %copy-start = (bf16[3072,3,8,128]{0,3,2,1:T(8,128)(2,1)S(1)}, bf16[3072,3,8,128]{0,3,2,1:T(8,128)(2,1)}, u32[]{:S(2)}) copy-start(bf16[3072,3,8,128]{0,3,2,1:T(8,128)(2,1)} %copy.5) | copy-start | bytes 56623108
  49.2 23.6 %all-to-all-start = ((bf16[4,2,3,256,128]{4,3,2,1,0:T(8,128)(2,1)}), bf16[4,2,3,256,128]{4,3,2,1,0:T(8,128)(2,1)S(1)}, u32[]{:S(2)}, u32[]{:S(2)}) async-start(bf16[4,2,3,256,128]{4,3,2,1,0:T(8,128)(2,1)} %bitcast.6), calls=%async_computation | async-start | bytes 3145728 | tf_op jit(solution)/shard_map/all_to_all | solution.py:243
  72.8 24.7 %copy-start.1 = (bf16[4,2,3,256,128]{4,3,2,1,0:T(8,128)(2,1)}, bf16[4,2,3,256,128]{4,3,2,1,0:T(8,128)(2,1)S(1)}, u32[]{:S(2)}) copy-start(bf16[4,2,3,256,128]{4,3,2,1,0:T(8,128)(2,1)S(1)} %all-to-all-done.query_ref.refs_0_) | copy-start | bytes 4718596
  72.8 23.6 %all-to-all-start.1 = ((bf16[4,2,3,256,128]{4,3,2,1,0:T(8,128)(2,1)}), bf16[4,2,3,256,128]{4,3,2,1,0:T(8,128)(2,1)S(1)}, u32[]{:S(2)}, u32[]{:S(2)}) async-start(bf16[4,2,3,256,128]{4,3,2,1,0:T(8,128)(2,1)} %bitcast.10), calls=%async_computation.1 | async-start | bytes 3145728 | tf_op jit(solution)/shard_map/all_to_all | solution.py:243
  77.5 30.1 %collective-permute-start.1 = (bf16[4,2,2,256,128]{4,3,2,1,0:T(8,128)(2,1)}, bf16[4,2,2,256,128]{4,3,2,1,0:T(8,128)(2,1)}, u32[]{:S(2)}, u32[]{:S(2)}) collective-permute-start(bf16[4,2,2,256,128]{4,3,2,1,0:T(8,128)(2,1)} %slice.10), channel_id=1, source_target_pairs={{0,4},{4,8},{8,12},{1,5},{5,9},{9,13},{2,6},{6,10},{10,14},{3,7},{... | collective-permute-start | bytes 3145736 | tf_op jit(solution)/shard_map/ppermute | solution.py:250
  96.4 53.7 %copy-start.2 = (bf16[4,2,3,256,128]{4,3,2,1,0:T(8,128)(2,1)}, bf16[4,2,3,256,128]{4,3,2,1,0:T(8,128)(2,1)S(1)}, u32[]{:S(2)}) copy-start(bf16[4,2,3,256,128]{4,3,2,1,0:T(8,128)(2,1)S(1)} %all-to-all-done.1.refs_1_.query_ref) | copy-start | bytes 4718596
  97.5 30.1 %collective-permute-start.2 = (bf16[4,2,2,256,128]{4,3,2,1,0:T(8,128)(2,1)}, bf16[4,2,2,256,128]{4,3,2,1,0:T(8,128)(2,1)}, u32[]{:S(2)}, u32[]{:S(2)}) collective-permute-start(bf16[4,2,2,256,128]{4,3,2,1,0:T(8,128)(2,1)} %slice.11), channel_id=1, source_target_pairs={{0,4},{4,8},{8,12},{1,5},{5,9},{9,13},{2,6},{6,10},{10,14},{3,7},{... | collective-permute-start | bytes 3145736 | tf_op jit(solution)/shard_map/ppermute | solution.py:250
  101.0 28.1 %collective-permute-start.3 = (bf16[4,2,2,256,128]{4,3,2,1,0:T(8,128)(2,1)}, bf16[4,2,2,256,128]{4,3,2,1,0:T(8,128)(2,1)S(1)}, u32[]{:S(2)}, u32[]{:S(2)}) collective-permute-start(bf16[4,2,2,256,128]{4,3,2,1,0:T(8,128)(2,1)} %slice.10), channel_id=1, source_target_pairs={{4,0},{8,4},{12,8},{5,1},{9,5},{13,9},{6,2},{10,6},{14,10},{7,3},{... | collective-permute-start | bytes 3145736 | tf_op jit(solution)/shard_map/ppermute | solution.py:250
  103.4 46.7 %collective-permute-start.4 = (bf16[4,2,2,256,128]{4,3,2,1,0:T(8,128)(2,1)}, bf16[4,2,2,256,128]{4,3,2,1,0:T(8,128)(2,1)}, u32[]{:S(2)}, u32[]{:S(2)}) collective-permute-start(bf16[4,2,2,256,128]{4,3,2,1,0:T(8,128)(2,1)} %slice.11), channel_id=1, source_target_pairs={{4,0},{8,4},{12,8},{5,1},{9,5},{13,9},{6,2},{10,6},{14,10},{7,3},{... | collective-permute-start | bytes 3145736 | tf_op jit(solution)/shard_map/ppermute | solution.py:250
  129.2 21.0 %copy-start.5 = (bf16[4,2,2,256,128]{4,3,2,1,0:T(8,128)(2,1)}, bf16[4,2,2,256,128]{4,3,2,1,0:T(8,128)(2,1)S(1)}, u32[]{:S(2)}) copy-start(bf16[4,2,2,256,128]{4,3,2,1,0:T(8,128)(2,1)S(1)} %collective-permute-done.3.refs_4_) | copy-start | bytes 3145732
  192.8 38.5 %collective-permute-start.5 = (bf16[256,3072]{1,0:T(8,128)(2,1)S(1)}, bf16[256,3072]{1,0:T(8,128)(2,1)S(1)}, u32[]{:S(2)}, u32[]{:S(2)}) collective-permute-start(bf16[256,3072]{1,0:T(8,128)(2,1)S(1)} %fusion.1), channel_id=1, source_target_pairs={{0,16},{16,0},{1,17},{17,1},{2,18},{18,2},{3,19},{19,3},{4,20},{20... | collective-permute-start | bytes 4718600 | tf_op jit(solution)/shard_map/ppermute | solution.py:265

commit v2 on v1

--- a/solution.py
+++ b/solution.py
@@ -7,6 +7,7 @@
 from jax.experimental import pallas as pl
 from jax.experimental.pallas import tpu as pltpu
 from jax.sharding import PartitionSpec as P
+
 
 TILE_T = 4
 
@@ -130,21 +131,32 @@
     return [(i, (i + by) % count) for i in range(count)]
 
 
-def attention_kernel(groups, columns, scale, valid_ref, query_ref, *refs):
-    kv_refs, out_ref, peak_ref, total_ref, sum_ref = refs[:-4], refs[-4], refs[-3], refs[-2], refs[-1]
+def after(value, earlier):
+    return lax.optimization_barrier((value, earlier))[0]
+
+
+def attention_kernel(parts, columns, scale, first, last, valid_ref, *refs):
+    queries = refs[: parts]
+    rest = refs[parts:]
+    if not first:
+        before_ref, rest = rest[0], rest[1:]
+    kv_refs, out_ref, state_ref = rest[:-2], rest[-2], rest[-1]
+    groups = len(kv_refs) // 3
+    head_dim = queries[0].shape[-1]
     column = pl.program_id(1)
     edge = (column == 0) | (column == columns - 1)
     to_exp2 = scale * math.log2(math.e)
+    state_ref = state_ref if last else out_ref.at[0, 0]
 
     def one_row(row, start, width):
-        query = query_ref[0, 0, 0]
+        query = jnp.concatenate([ref[0, 0, 0] for ref in queries], axis=0)
         scores, values = [], []
         for group in range(groups):
             ref = kv_refs[row * groups + group]
             tokens = ref.shape[3]
-            first = ref.shape[2] - 2
-            key = ref[pl.ds(start, width), 0, first].reshape(width * tokens, -1)
-            values.append(ref[pl.ds(start, width), 0, first + 1].reshape(width * tokens, -1))
+            at = ref.shape[2] - 2
+            key = ref[pl.ds(start, width), 0, at].reshape(width * tokens, head_dim)
+            values.append(ref[pl.ds(start, width), 0, at + 1].reshape(width * tokens, head_dim))
             scores.append(
                 lax.dot_general(
                     query, key, (((1,), (1,)), ((), ())), preferred_element_type=jnp.float32
@@ -153,10 +165,12 @@
         peak = scores[0].max(axis=1, keepdims=True)
         for score in scores[1:]:
             peak = jnp.maximum(peak, score.max(axis=1, keepdims=True))
-        if row > 0:
-            before = peak_ref[...]
-            peak = jnp.maximum(peak, before)
-            fade = jnp.exp2((before - peak) * to_exp2)
+        fresh = first and row == 0
+        old_ref = state_ref if row > 0 or first else before_ref.at[0, 0]
+        if not fresh:
+            old_peak = old_ref[:, head_dim : head_dim + 1]
+            peak = jnp.maximum(peak, old_peak)
+            fade = jnp.exp2((old_peak - peak) * to_exp2)
         offset = peak * to_exp2
         total, summed = 0.0, 0.0
         for score, value in zip(scores, values):
@@ -165,12 +179,12 @@
             summed = summed + jnp.dot(
                 weight.astype(jnp.bfloat16), value, preferred_element_type=jnp.float32
             )
-        if row > 0:
-            total = total + total_ref[...] * fade
-            summed = summed + sum_ref[...] * fade
-        peak_ref[...] = peak
-        total_ref[...] = total
-        sum_ref[...] = summed
+        if not fresh:
+            total = total + old_ref[:, head_dim + 1 : head_dim + 2] * fade
+            summed = summed + old_ref[:, :head_dim] * fade
+        state_ref[:, :head_dim] = summed
+        state_ref[:, head_dim : head_dim + 1] = peak
+        state_ref[:, head_dim + 1 : head_dim + 2] = total
 
     def all_rows(start, width):
         one_row(0, start, width)
@@ -179,94 +193,191 @@
 
     pl.when(edge)(lambda: all_rows(jnp.where(column == 0, 0, columns - 2), 2))
     pl.when(jnp.logical_not(edge))(lambda: all_rows(column - 1, 3))
-    out_ref[0, 0] = (sum_ref[...] / total_ref[...]).astype(out_ref.dtype)
-
-
-def attend(valid, stream, rows, scale):
-    columns, heads, _, tokens, head_dim = stream.shape
-    groups = len(rows) // 3
+    if last:
+        out = state_ref[:, :head_dim] / state_ref[:, head_dim + 1 : head_dim + 2]
+        places, each = out_ref.shape[0], out_ref.shape[3]
+        for by in range(places):
+            out_ref[valid_ref[2 + by], 0, 0] = out[by * each : (by + 1) * each].astype(out_ref.dtype)
+
+
+def attend(valid, streams, before, rows, scale, last, places):
+    columns, heads, _, _, head_dim = streams[0].shape
+    tokens = sum(stream.shape[3] for stream in streams)
     keys = sum(kv.shape[3] for kv in rows) * 10 // 4
+    first = before is None
+
+    def at_query(h, c, v):
+        return (c, h, 0, 0)
 
     def kv_spec(kv):
         return pl.BlockSpec(
             (columns, 1, kv.shape[2], kv.shape[3], head_dim), lambda h, c, v: (0, h, 0, 0, 0)
         )
 
+    if last:
+        each = tokens // places
+        out_spec = pl.BlockSpec((places, 1, 1, each, head_dim), lambda h, c, v: (0, c, h, 0, 0))
+        out_shape = jax.ShapeDtypeStruct((places, columns, heads, each, head_dim), jnp.bfloat16)
+    else:
+        out_spec = pl.BlockSpec((1, 1, tokens, 2 * head_dim), at_query)
+        out_shape = jax.ShapeDtypeStruct((columns, heads, tokens, 2 * head_dim), jnp.float32)
     pairs = heads * columns * tokens * keys
+    state = [] if first else [before]
     return pl.pallas_call(
-        functools.partial(attention_kernel, groups, columns, scale),
+        functools.partial(attention_kernel, len(streams), columns, scale, first, last),
         grid_spec=pltpu.PrefetchScalarGridSpec(
             num_scalar_prefetch=1,
             grid=(heads, columns),
             in_specs=[
-                pl.BlockSpec((1, 1, 1, tokens, head_dim), lambda h, c, v: (c, h, 0, 0, 0))
+                pl.BlockSpec((1, 1, 1, stream.shape[3], head_dim), lambda h, c, v: (c, h, 0, 0, 0))
+                for stream in streams
             ]
+            + [pl.BlockSpec((1, 1, tokens, 2 * head_dim), at_query) for _ in state]
             + [kv_spec(kv) for kv in rows],
-            out_specs=pl.BlockSpec((1, 1, tokens, head_dim), lambda h, c, v: (c, h, 0, 0)),
-            scratch_shapes=[
-                pltpu.VMEM((tokens, 1), jnp.float32),
-                pltpu.VMEM((tokens, 1), jnp.float32),
-                pltpu.VMEM((tokens, head_dim), jnp.float32),
-            ],
+            out_specs=out_spec,
+            scratch_shapes=[pltpu.VMEM((tokens, 2 * head_dim), jnp.float32)],
         ),
-        out_shape=jax.ShapeDtypeStruct((columns, heads, tokens, head_dim), jnp.bfloat16),
+        out_shape=out_shape,
         cost_estimate=pl.CostEstimate(
             flops=pairs * head_dim * 8, bytes_accessed=pairs * 4, transcendentals=pairs
         ),
         name="tile_attention",
-    )(valid, stream, *rows)
+    )(valid, *streams, *state, *rows)
+
+
+def mix_kernel(at_ref, attended_ref, *refs):
+    weight_refs, out_ref = refs[:-1], refs[-1]
+    places = []
+    for ref in weight_refs:
+        for k in range(ref.shape[0]):
+            places.append((ref, k))
+    total = 0.0
+    for at in range(0, len(places), 2):
+        pair = places[at : at + 2]
+        left = jnp.concatenate([attended_ref[at_ref[at + i]] for i in range(len(pair))], axis=1)
+        right = jnp.concatenate([ref[k] for ref, k in pair], axis=0)
+        total = total + jnp.dot(left, right, preferred_element_type=jnp.float32)
+    out_ref[...] = total.astype(out_ref.dtype)
+
+
+def mix(order, attended, weights):
+    heads, tokens, head_dim = attended.shape
+    width = weights[0].shape[-1]
+    step = math.gcd(width, 768)
+    return pl.pallas_call(
+        mix_kernel,
+        grid_spec=pltpu.PrefetchScalarGridSpec(
+            num_scalar_prefetch=1,
+            grid=(width // step,),
+            in_specs=[pl.BlockSpec(attended.shape, lambda i, o: (0, 0, 0))]
+            + [
+                pl.BlockSpec((weight.shape[0], head_dim, step), lambda i, o: (0, 0, i))
+                for weight in weights
+            ],
+            out_specs=pl.BlockSpec((tokens, step), lambda i, o: (0, i)),
+        ),
+        out_shape=jax.ShapeDtypeStruct((tokens, width), jnp.bfloat16),
+        cost_estimate=pl.CostEstimate(
+            flops=2 * heads * tokens * head_dim * width,
+            bytes_accessed=2 * heads * head_dim * width,
+            transcendentals=0,
+        ),
+        name="mix_heads",
+    )(order, attended, *weights)
 
 
 def row_plan(latents, input_weight, norm_gains, output_weight):
     frame_parts = lax.axis_size("ta")
     row_parts = lax.axis_size("ha")
     col_parts = lax.axis_size("wa")
-    model_width = latents.shape[-1]
-    tokens = math.prod(latents.shape[:-1])
+    frames = latents.shape[1]
     heads_local, head_dim = input_weight.shape[2:]
     heads_each = heads_local // col_parts
-    own = latents.reshape(tokens, model_width)
-    groups = [own]
+    here, column_at = lax.axis_index("ta"), lax.axis_index("wa")
+    cuts = 2 if frames % 2 == 0 else 1
+    step = frames // cuts
+    own = [lax.slice_in_dim(latents, i * step, (i + 1) * step, axis=1) for i in range(cuts)]
+    chunks = [latents]
     for by in range(1, frame_parts):
-        groups.append(lax.ppermute(own, "ta", shift_perm(frame_parts, by)))
-    gains = jnp.concatenate([norm_gains, jnp.ones_like(norm_gains[:1])])[:, None, :]
-    is_value = jnp.arange(3).reshape(3, 1, 1) == 2
-
-    def project(group):
+        for chunk in own:
+            chunks.append(lax.ppermute(chunk, "ta", shift_perm(frame_parts, by)))
+
+    fetched = []
+    for by in range(1, frame_parts):
+        for k in range(heads_each):
+            share = lax.dynamic_slice_in_dim(output_weight, column_at * heads_each + k, 1, axis=0)
+            share = lax.ppermute(after(share, chunks[-1]), "ta", shift_perm(frame_parts, by))
+            fetched.append((by, k, share))
+
+    def project(chunk):
         projected = jnp.einsum(
-            "td,dsne->nste", group, input_weight, preferred_element_type=jnp.float32
-        )
-        mean_square = jnp.mean(projected * projected, axis=-1, keepdims=True)
-        factor = jnp.where(is_value, 1.0, lax.rsqrt(mean_square + EPSILON))
-        normed = (projected * factor * gains).astype(jnp.bfloat16)
-        dealt = normed.reshape(col_parts, heads_each, 3, tokens, head_dim)
-        return lax.all_to_all(dealt, "wa", 0, 0)
-
-    streams = [project(group) for group in groups]
+            "cfhwd,dsne->cfhwsne", chunk, input_weight, preferred_element_type=jnp.float32
+        )
+        normed = jnp.stack(
+            [
+                rms_norm(projected[:, :, :, :, 0], norm_gains[0]),
+                rms_norm(projected[:, :, :, :, 1], norm_gains[1]),
+                projected[:, :, :, :, 2],
+            ]
+        ).astype(jnp.bfloat16)
+        return normed.transpose(5, 0, 1, 2, 3, 4, 6)
+
+    streams = []
+    ready = None
+    for at, chunk in enumerate(chunks):
+        if ready is not None:
+            chunk = after(chunk, ready)
+        ready = project(chunk)
+        for part in range(cuts if at == 0 else 1):
+            dealt = lax.slice_in_dim(ready, part * step, (part + 1) * step, axis=3)
+            dealt = dealt.reshape(col_parts, heads_each, 3, -1, head_dim)
+            streams.append(lax.all_to_all(dealt, "wa", 0, 0))
     down = [(i, i + 1) for i in range(row_parts - 1)]
     up = [(i + 1, i) for i in range(row_parts - 1)]
-    rows = list(streams)
-    for perm in (down, up):
-        rows += [lax.ppermute(stream[:, :, 1:], "ha", perm) for stream in streams]
+    above, below = [], []
+    for stream in streams:
+        above.append(lax.ppermute(stream[:, :, 1:], "ha", down))
+        below.append(lax.ppermute(stream[:, :, 1:], "ha", up))
     height_index = lax.axis_index("ha")
-    valid = jnp.stack([height_index > 0, height_index < row_parts - 1]).astype(jnp.int32)
+    places = [lax.rem(here + (frame_parts - by), frame_parts) for by in range(frame_parts)]
+    scalars = jnp.stack(
+        [(height_index > 0).astype(jnp.int32), (height_index < row_parts - 1).astype(jnp.int32)]
+        + places
+    )
     scale = 1.0 / math.sqrt(head_dim)
 
-    def shares(stream):
-        attended = lax.all_to_all(attend(valid, stream, rows, scale), "wa", 0, 0)
-        attended = attended.reshape(heads_local, tokens, head_dim)
-        return jnp.einsum(
-            "nte,ned->td", attended, output_weight, preferred_element_type=jnp.float32
-        )
-
-    arrived = []
-    for by in range(1, frame_parts):
-        share = shares(streams[by]).astype(jnp.bfloat16)
-        arrived.append(lax.ppermute(share, "ta", shift_perm(frame_parts, -by)))
-    result = shares(streams[0])
-    for share in arrived:
-        result = result + share.astype(jnp.float32)
-    return result.astype(jnp.bfloat16).reshape(latents.shape)
+    def spread(block):
+        held = [(0, block)]
+        distance = col_parts // 2
+        while distance:
+            perm = [(i, i ^ distance) for i in range(col_parts)]
+            got = lax.ppermute(jnp.concatenate([b for _, b in held], axis=0), "wa", perm)
+            held = held + [
+                (mask ^ distance, got[i : i + 1]) for i, (mask, _) in enumerate(held)
+            ]
+            distance //= 2
+        return held
+
+    state = attend(
+        scalars, streams, None, streams[:cuts] + above[:cuts] + below[:cuts], scale, False, 1
+    )
+    attended = attend(
+        scalars, streams, state, streams[cuts:] + above[cuts:] + below[cuts:], scale, True,
+        frame_parts,
+    )
+    sent = attended.reshape(frame_parts * col_parts, heads_each, -1, head_dim)
+    got = lax.all_to_all(sent, ("ta", "wa"), 0, 0)
+    got = got.reshape(frame_parts * heads_local, -1, head_dim)
+    order = [here * heads_local + k for k in range(heads_local)]
+    weights = [output_weight]
+    for by, k, block in fetched:
+        for mask, part in spread(block):
+            weights.append(part)
+            order.append(
+                places[by] * heads_local + (column_at ^ mask) * heads_each + k
+            )
+    result = mix(jnp.stack(order).astype(jnp.int32), got, weights)
+    return result.reshape(latents.shape)
 
 
 def solution(mesh):
@@ -280,7 +391,8 @@
 
     def per_device(latents, input_weight, norm_gains, output_weight):
         frames = latents.shape[1] * lax.axis_size("ta")
-        dealt_heads = input_weight.shape[2] % lax.axis_size("wa") == 0
+        width = lax.axis_size("wa")
+        dealt_heads = input_weight.shape[2] % width == 0 and width & (width - 1) == 0
         if latents.shape[0] == 1 and dealt_heads and frames <= 2 * TILE_T:
             return row_plan(latents, input_weight, norm_gains, output_weight)
         return halo_plan(latents, input_weight, norm_gains, output_weight)

time: 238 us -> 232 us (0.975)
  waiting for transfers between devices: 77 us -> 45.3 us
  starting transfers between devices: 22 us -> 52.3 us
  blocking collectives: 24.5 us -> 0 us
  Pallas kernels: 51.4 us -> 72.3 us
  local copies, waits for them, and re-layouts: 30.6 us -> 23.1 us
  other arithmetic: 3.78 us -> 7.62 us
    ppermute x6 -> x16, waiting for transfers between devices: 43.1 us -> 11.7 us  [the longest x4 7.06 us: spread(): lax.ppermute(jnp.concatenate([b for _, b in held], axis=0), 'wa', perm)]
    all_to_all x2 -> x0, blocking collectives: 24.5 us -> none  [shares(): attended = lax.all_to_all(attend(valid, stream, rows, scale), 'wa', 0, 0)]
    unnamed x13 -> x22, local copies, waits for them, and re-layouts: 25.2 us -> 2.78 us
    pallas_call x2 -> x3, Pallas kernels: 51.4 us -> 72.3 us  [the longest x2 62.5 us: attend(): pl.pallas_call(functools.partial(attention_kernel, len(streams), columns,...]
    ppermute x6 -> x16, starting transfers between devices: 14.9 us -> 32.6 us  [the longest x4 14.8 us: row_plan(): above.append(lax.ppermute(stream[:, :, 1:], 'ha', down))]
    all_to_all x2 -> x5, starting transfers between devices: 7.13 us -> 19.6 us  [the longest x4 16.1 us: row_plan(): streams.append(lax.all_to_all(dealt, 'wa', 0, 0))]
    slice x2 -> x10, local copies, waits for them, and re-layouts: 2.24 us -> 14.6 us  [the longest x4 6.65 us: row_plan(): above.append(lax.ppermute(stream[:, :, 1:], 'ha', down))]
    concatenate x0 -> x2, other arithmetic: none -> 3.8 us  [spread(): jnp.concatenate([b for _, b in held], axis=0)]
  transfers between devices with their start and end apart: 8 -> 21, of which waited for: 6 -> 6; matrix products, arithmetic and copies ran while one was open for 16% -> 24% of each run, Pallas kernels for 11% -> 27%
where the time goes in v2:
time: 232 us; the launch traced here: 231 us
  Pallas kernels  72.3 us (31%)
  starting transfers between devices  52.3 us (23%)
  waiting for transfers between devices  45.3 us (20%)
  matrix products  29.6 us (13%)
  local copies, waits for them, and re-layouts  23.1 us (10%)
  other arithmetic  7.62 us (3%)
    pallas_call x2, Pallas kernels, attend(): pl.pallas_call(functools.partial(attention_kernel, len(streams), columns,...  62.5 us
    dot_general x3, matrix products, project(): jnp.einsum('cfhwd,dsne->cfhwsne', chunk, input_weight, preferred_element_...  29.6 us
    all_to_all x4, waiting for transfers between devices, row_plan(): streams.append(lax.all_to_all(dealt, 'wa', 0, 0))  22.3 us
    all_to_all x4, starting transfers between devices, row_plan(): streams.append(lax.all_to_all(dealt, 'wa', 0, 0))  16.1 us
    ppermute x4, starting transfers between devices, row_plan(): above.append(lax.ppermute(stream[:, :, 1:], 'ha', down))  14.8 us
    all_to_all x1, waiting for transfers between devices, row_plan(): got = lax.all_to_all(sent, ('ta', 'wa'), 0, 0)  11.4 us
    pallas_call x1, Pallas kernels, mix(): pl.pallas_call(mix_kernel, grid_spec=pltpu.PrefetchScalarGridSpec(num_sca...  9.81 us
    ppermute x4, starting transfers between devices, row_plan(): below.append(lax.ppermute(stream[:, :, 1:], 'ha', up))  9.55 us
  transfers between devices with their start and end apart: 21, of which 6 were waited for; matrix products, arithmetic and copies ran while one was open for 24% of the time, Pallas kernels for 27%

profile of v2, /device:TPU:16, one launch (start us, length us, event | category | flops | bytes accessed | tf_op | source)
XLA Modules:
  0.0 230.7 jit_solution(14661619408028435492)
XLA Ops:
  0.0 1.6 fusion.29
  1.6 1.6 collective-permute-start
  3.2 9.3 %fusion.6 = f32[1,4,8,8,3,8,128]{6,3,5,4,2,1,0:T(8,128)S(1)} fusion(bf16[3072,3,8,128,1,1]{3,2,1,0,5,4:T(8,128)(2,1)} %bitcast.145, bf16[1,4,8,8,3072]{4,3,2,1,0:T(8,128)(2,1)S(1)} %copy-done.5), kind=kOutput, calls=%fused_computation.6 | convolution fusion | flops 4831838208 | bytes 23592960 | tf_op jit(solution)/shard_map/cfhwd,dsne->cfhwsne/dot_general | solution.py:313
  13.2 0.7 fusion.18
  14.3 1.1 copy.8
  15.4 4.2 %all-to-all-start = ((bf16[4,2,3,128,128]{4,3,2,1,0:T(8,128)(2,1)}), bf16[4,2,3,128,128]{4,3,2,1,0:T(8,128)(2,1)}, u32[]{:S(2)}, u32[]{:S(2)}) async-start(bf16[4,2,3,128,128]{4,3,2,1,0:T(8,128)(2,1)} %bitcast.33), calls=%async_computation | async-start | bytes 1572864 | tf_op jit(solution)/shard_map/all_to_all | solution.py:334
  20.1 1.2 copy.9
  21.3 2.6 %constant_dynamic-slice_fusion = (bf16[1,128,3072]{2,1,0:T(8,128)(2,1)}, bf16[1,128,3072]{2,1,0:T(8,128)(2,1)}) fusion(bf16[8,128,3072]{2,1,0:T(8,128)(2,1)} %refs_0_.1, s32[]{:T(128)S(6)} %select_n.7, s32[]{:T(128)S(6)} %select_n.6), kind=kLoop, calls=%fused_computation.56 | loop fusion | bytes 3145736 | tf_op jit(solution)/shard_map/dynamic_slice | solution.py:308
  24.0 10.2 %fusion.13 = f32[1,2,8,8,3,8,128]{6,3,5,4,2,1,0:T(8,128)S(1)} fusion(bf16[3072,3,8,128,1,1]{3,2,1,0,5,4:T(8,128)(2,1)} %bitcast.146, bf16[1,2,8,8,3072]{4,3,2,1,0:T(8,128)(2,1)} %collective-permute-done), kind=kOutput, calls=%fused_computation.12 | convolution fusion | flops 2415919104 | bytes 21233664 | tf_op jit(solution)/shard_map/cfhwd,dsne->cfhwsne/dot_general | solution.py:313
  35.0 4.6 %collective-permute-done.1 = bf16[1,2,8,8,3072]{4,3,2,1,0:T(8,128)(2,1)} collective-permute-done((bf16[1,2,8,8,3072]{4,3,2,1,0:T(8,128)(2,1)S(1)}, bf16[1,2,8,8,3072]{4,3,2,1,0:T(8,128)(2,1)}, u32[]{:S(2)}, u32[]{:S(2)}) %collective-permute-start.1) | collective-permute-done | bytes 786464 | tf_op jit(solution)/shard_map/ppermute | solution.py:303
  39.6 10.2 %fusion.10 = f32[1,2,8,8,3,8,128]{6,3,5,2,1,4,0:T(8,128)S(1)} fusion(bf16[3072,3,8,128,1,1]{3,2,1,0,5,4:T(8,128)(2,1)} %bitcast.147, bf16[1,2,8,8,3072]{4,3,2,1,0:T(8,128)(2,1)} %collective-permute-done.1), kind=kOutput, calls=%fused_computation.11 | convolution fusion | flops 2415919104 | bytes 21233664 | tf_op jit(solution)/shard_map/cfhwd,dsne->cfhwsne/dot_general | solution.py:313
  49.8 1.1 copy.13
  51.4 1.5 collective-permute-start.13
  52.9 4.2 %all-to-all-start.1 = ((bf16[4,2,3,128,128]{4,3,2,1,0:T(8,128)(2,1)}), bf16[4,2,3,128,128]{4,3,2,1,0:T(8,128)(2,1)}, u32[]{:S(2)}, u32[]{:S(2)}) async-start(bf16[4,2,3,128,128]{4,3,2,1,0:T(8,128)(2,1)} %bitcast.142), calls=%async_computation.1 | async-start | bytes 1572864 | tf_op jit(solution)/shard_map/all_to_all | solution.py:334
  57.5 11.3 %all-to-all-done.1.refs_1_.refs_5_ = bf16[4,2,3,128,128]{4,3,2,1,0:T(8,128)(2,1)} async-done(((bf16[4,2,3,128,128]{4,3,2,1,0:T(8,128)(2,1)}), bf16[4,2,3,128,128]{4,3,2,1,0:T(8,128)(2,1)}, u32[]{:S(2)}, u32[]{:S(2)}) %all-to-all-start.1) | async-done | bytes 786464 | tf_op jit(solution)/shard_map/all_to_all | solution.py:334
  68.8 4.2 %all-to-all-start.2 = ((bf16[4,2,3,128,128]{4,3,2,1,0:T(8,128)(2,1)}), bf16[4,2,3,128,128]{4,3,2,1,0:T(8,128)(2,1)}, u32[]{:S(2)}, u32[]{:S(2)}) async-start(bf16[4,2,3,128,128]{4,3,2,1,0:T(8,128)(2,1)} %bitcast.143), calls=%async_computation.2 | async-start | bytes 1572864 | tf_op jit(solution)/shard_map/all_to_all | solution.py:334
  73.4 2.0 collective-permute-start.11
  75.6 1.1 copy.16
  76.7 8.6 %all-to-all-done.2.refs_2_.refs_5_ = bf16[4,2,3,128,128]{4,3,2,1,0:T(8,128)(2,1)} async-done(((bf16[4,2,3,128,128]{4,3,2,1,0:T(8,128)(2,1)}), bf16[4,2,3,128,128]{4,3,2,1,0:T(8,128)(2,1)}, u32[]{:S(2)}, u32[]{:S(2)}) %all-to-all-start.2) | async-done | bytes 786464 | tf_op jit(solution)/shard_map/all_to_all | solution.py:334
  85.3 3.5 %all-to-all-start.3 = ((bf16[4,2,3,128,128]{4,3,2,1,0:T(8,128)(2,1)}), bf16[4,2,3,128,128]{4,3,2,1,0:T(8,128)(2,1)S(1)}, u32[]{:S(2)}, u32[]{:S(2)}) async-start(bf16[4,2,3,128,128]{4,3,2,1,0:T(8,128)(2,1)} %bitcast.58), calls=%async_computation.3 | async-start | bytes 1572864 | tf_op jit(solution)/shard_map/all_to_all | solution.py:334
  88.8 1.9 slice.114
  90.7 3.5 %collective-permute-start.2 = (bf16[4,2,2,128,128]{4,3,2,1,0:T(8,128)(2,1)}, bf16[4,2,2,128,128]{4,3,2,1,0:T(8,128)(2,1)}, u32[]{:S(2)}, u32[]{:S(2)}) collective-permute-start(bf16[4,2,2,128,128]{4,3,2,1,0:T(8,128)(2,1)} %slice.114), channel_id=1, source_target_pairs={{0,4},{4,8},{8,12},{1,5},{5,9},{9,13},{2,6},{6,10},{10,14},{3,7},{... | collective-permute-start | bytes 1572872 | tf_op jit(solution)/shard_map/ppermute | solution.py:339
  94.2 2.0 collective-permute-start.14
  96.3 0.7 stack.121.at_ref
  97.6 2.3 %collective-permute-start.4 = (bf16[4,2,2,128,128]{4,3,2,1,0:T(8,128)(2,1)}, bf16[4,2,2,128,128]{4,3,2,1,0:T(8,128)(2,1)}, u32[]{:S(2)}, u32[]{:S(2)}) collective-permute-start(bf16[4,2,2,128,128]{4,3,2,1,0:T(8,128)(2,1)} %slice.114), channel_id=1, source_target_pairs={{4,0},{8,4},{12,8},{5,1},{9,5},{13,9},{6,2},{10,6},{14,10},{7,3},{... | collective-permute-start | bytes 1572872 | tf_op jit(solution)/shard_map/ppermute | solution.py:340
  100.0 1.9 slice.115
  101.9 4.3 %collective-permute-start.3 = (bf16[4,2,2,128,128]{4,3,2,1,0:T(8,128)(2,1)}, bf16[4,2,2,128,128]{4,3,2,1,0:T(8,128)(2,1)}, u32[]{:S(2)}, u32[]{:S(2)}) collective-permute-start(bf16[4,2,2,128,128]{4,3,2,1,0:T(8,128)(2,1)} %slice.115), channel_id=1, source_target_pairs={{0,4},{4,8},{8,12},{1,5},{5,9},{9,13},{2,6},{6,10},{10,14},{3,7},{... | collective-permute-start | bytes 1572872 | tf_op jit(solution)/shard_map/ppermute | solution.py:339
  106.1 1.9 slice.116
  108.0 2.4 %all-to-all-done.3.refs_3_.refs_6_ = bf16[4,2,3,128,128]{4,3,2,1,0:T(8,128)(2,1)S(1)} async-done(((bf16[4,2,3,128,128]{4,3,2,1,0:T(8,128)(2,1)}), bf16[4,2,3,128,128]{4,3,2,1,0:T(8,128)(2,1)S(1)}, u32[]{:S(2)}, u32[]{:S(2)}) %all-to-all-start.3) | async-done | bytes 786464 | tf_op jit(solution)/shard_map/all_to_all | solution.py:334
  110.4 0.9 slice.117
  111.4 2.3 %collective-permute-start.5 = (bf16[4,2,2,128,128]{4,3,2,1,0:T(8,128)(2,1)}, bf16[4,2,2,128,128]{4,3,2,1,0:T(8,128)(2,1)S(1)}, u32[]{:S(2)}, u32[]{:S(2)}) collective-permute-start(bf16[4,2,2,128,128]{4,3,2,1,0:T(8,128)(2,1)} %slice.115), channel_id=1, source_target_pairs={{4,0},{8,4},{12,8},{5,1},{9,5},{13,9},{6,2},{10,6},{14,10},{7,3},{... | collective-permute-start | bytes 1572872 | tf_op jit(solution)/shard_map/ppermute | solution.py:340
  113.7 3.5 %collective-permute-start.6 = (bf16[4,2,2,128,128]{4,3,2,1,0:T(8,128)(2,1)}, bf16[4,2,2,128,128]{4,3,2,1,0:T(8,128)(2,1)}, u32[]{:S(2)}, u32[]{:S(2)}) collective-permute-start(bf16[4,2,2,128,128]{4,3,2,1,0:T(8,128)(2,1)} %slice.116), channel_id=1, source_target_pairs={{0,4},{4,8},{8,12},{1,5},{5,9},{9,13},{2,6},{6,10},{10,14},{3,7},{... | collective-permute-start | bytes 1572872 | tf_op jit(solution)/shard_map/ppermute | solution.py:339
  117.2 2.4 %pad_maximum_fusion = bf16[2,128,3072]{2,1,0:T(8,128)(2,1)} fusion(bf16[1,128,3072]{2,1,0:T(8,128)(2,1)} %collective-permute-done.11.refs_2_, bf16[1,128,3072]{2,1,0:T(8,128)(2,1)S(1)} %collective-permute-done.10.refs_1_), kind=kLoop, calls=%fused_computation.8 | loop fusion | flops 786432 | bytes 3145728 | tf_op jit(solution)/shard_map/concatenate | solution.py:354
  119.7 7.0 %collective-permute-done.14.refs_6_ = bf16[1,128,3072]{2,1,0:T(8,128)(2,1)S(1)} collective-permute-done((bf16[1,128,3072]{2,1,0:T(8,128)(2,1)S(1)}, bf16[1,128,3072]{2,1,0:T(8,128)(2,1)S(1)}, u32[]{:S(2)}, u32[]{:S(2)}) %collective-permute-start.14) | collective-permute-done | bytes 786464 | tf_op jit(solution)/shard_map/ppermute | solution.py:354
  126.7 1.4 pad_maximum_fusion.1
  128.1 2.3 %collective-permute-start.8 = (bf16[4,2,2,128,128]{4,3,2,1,0:T(8,128)(2,1)}, bf16[4,2,2,128,128]{4,3,2,1,0:T(8,128)(2,1)S(1)}, u32[]{:S(2)}, u32[]{:S(2)}) collective-permute-start(bf16[4,2,2,128,128]{4,3,2,1,0:T(8,128)(2,1)} %slice.116), channel_id=1, source_target_pairs={{4,0},{8,4},{12,8},{5,1},{9,5},{13,9},{6,2},{10,6},{14,10},{7,3},{... | collective-permute-start | bytes 1572872 | tf_op jit(solution)/shard_map/ppermute | solution.py:340
  130.5 3.5 %collective-permute-start.7 = (bf16[4,2,2,128,128]{4,3,2,1,0:T(8,128)(2,1)}, bf16[4,2,2,128,128]{4,3,2,1,0:T(8,128)(2,1)S(1)}, u32[]{:S(2)}, u32[]{:S(2)}) collective-permute-start(bf16[4,2,2,128,128]{4,3,2,1,0:T(8,128)(2,1)} %slice.117), channel_id=1, source_target_pairs={{0,4},{4,8},{8,12},{1,5},{5,9},{9,13},{2,6},{6,10},{10,14},{3,7},{... | collective-permute-start | bytes 1572872 | tf_op jit(solution)/shard_map/ppermute | solution.py:339
  134.0 2.5 %collective-permute-start.9 = (bf16[4,2,2,128,128]{4,3,2,1,0:T(8,128)(2,1)}, bf16[4,2,2,128,128]{4,3,2,1,0:T(8,128)(2,1)S(1)}, u32[]{:S(2)}, u32[]{:S(2)}) collective-permute-start(bf16[4,2,2,128,128]{4,3,2,1,0:T(8,128)(2,1)} %slice.117), channel_id=1, source_target_pairs={{4,0},{8,4},{12,8},{5,1},{9,5},{13,9},{6,2},{10,6},{14,10},{7,3},{... | collective-permute-start | bytes 1572872 | tf_op jit(solution)/shard_map/ppermute | solution.py:340
  136.6 29.2 %tile_attention.2.refs_4_ = f32[4,2,512,256]{3,2,1,0:T(8,128)} custom-call(s32[4]{0:T(128)} %pad_add_fusion.valid_ref, bf16[4,2,3,128,128]{4,3,2,1,0:T(8,128)(2,1)} %all-to-all-done.refs_0_.refs_4_, bf16[4,2,3,128,128]{4,3,2,1,0:T(8,128)(2,1)} %all-to-all-done.1.refs_1_.refs_5_, bf16[4,2,3,128,128]{4,3,2,1,0:T(8,128)(2,1)} %all-to-all-done.2.refs_2_.refs_5_, ...), custom_call_target="tpu_custom_call" | custom-call | flops 8053063680 | bytes 31457280 | tf_op jit(solution)/shard_map/tile_attention/pallas_call | solution.py:226
  165.9 0.7 copy-done.9
  166.9 0.8 copy-done.10
  167.7 33.3 %tile_attention.3 = bf16[2,4,2,256,128]{4,3,2,1,0:T(8,128)(2,1)} custom-call(s32[4]{0:T(128)} %pad_add_fusion.valid_ref, bf16[4,2,3,128,128]{4,3,2,1,0:T(8,128)(2,1)} %all-to-all-done.refs_0_.refs_4_, bf16[4,2,3,128,128]{4,3,2,1,0:T(8,128)(2,1)} %all-to-all-done.1.refs_1_.refs_5_, bf16[4,2,3,128,128]{4,3,2,1,0:T(8,128)(2,1)} %all-to-all-done.2.refs_2_.refs_5_, ...), custom_call_target="tpu_custom_call" | custom-call | flops 8053063680 | bytes 31457280 | tf_op jit(solution)/shard_map/tile_attention/pallas_call | solution.py:226
  201.0 3.6 %all-to-all-start.4 = ((bf16[8,2,256,128]{3,2,1,0:T(8,128)(2,1)}), bf16[8,2,256,128]{3,2,1,0:T(8,128)(2,1)S(1)}, u32[]{:S(2)}, u32[]{:S(2)}) async-start(bf16[8,2,256,128]{3,2,1,0:T(8,128)(2,1)} %bitcast.144), calls=%async_computation.4 | async-start | bytes 2097152 | tf_op jit(solution)/shard_map/all_to_all | solution.py:369
  204.6 2.7 %fusion.28 = (bf16[1,128,3072]{2,1,0:T(8,128)(2,1)}, bf16[1,128,3072]{2,1,0:T(8,128)(2,1)}) fusion(bf16[2,128,3072]{2,1,0:T(8,128)(2,1)} %collective-permute-done.12), kind=kLoop, calls=%fused_computation.59 | loop fusion | bytes 3145728 | tf_op jit(solution)/shard_map/slice | solution.py:356
  207.2 1.3 fusion.27
  208.5 11.4 %all-to-all-done.4 = bf16[8,2,256,128]{3,2,1,0:T(8,128)(2,1)S(1)} async-done(((bf16[8,2,256,128]{3,2,1,0:T(8,128)(2,1)}), bf16[8,2,256,128]{3,2,1,0:T(8,128)(2,1)S(1)}, u32[]{:S(2)}, u32[]{:S(2)}) %all-to-all-start.4) | async-done | bytes 1048608 | tf_op jit(solution)/shard_map/all_to_all | solution.py:369
  219.9 1.0 copy-done
  220.8 9.8 %mix_heads.1 = bf16[256,3072]{1,0:T(8,128)(2,1)} custom-call(s32[16]{0:T(128)} %stack.121.at_ref, bf16[16,256,128]{2,1,0:T(8,128)(2,1)} %bitcast.141, bf16[8,128,3072]{2,1,0:T(8,128)(2,1)} %refs_0_.1, bf16[1,128,3072]{2,1,0:T(8,128)(2,1)} %copy-done.1, bf16[1,128,3072]{2,1,0:T(8,128)(2,1)} %collective-permute-done.11.refs_2_, ...), custom_call_target="tpu_custom_call" | custom-call | flops 3221225472 | bytes 12582912 | tf_op jit(solution)/shard_map/mix_heads/pallas_call | solution.py:267
  (57 shorter events, 4.8 us)
Async XLA Ops:
  0.0 3.2 %copy-start.5 = (bf16[1,4,8,8,3072]{4,3,2,1,0:T(8,128)(2,1)S(1)}, bf16[1,4,8,8,3072]{4,3,2,1,0:T(8,128)(2,1)}, u32[]{:S(2)}) copy-start(bf16[1,4,8,8,3072]{4,3,2,1,0:T(8,128)(2,1)} %param.4) | copy-start | bytes 4718596
  1.6 22.4 %collective-permute-start = (bf16[1,2,8,8,3072]{4,3,2,1,0:T(8,128)(2,1)S(1)}, bf16[1,2,8,8,3072]{4,3,2,1,0:T(8,128)(2,1)}, u32[]{:S(2)}, u32[]{:S(2)}) collective-permute-start(bf16[1,2,8,8,3072]{4,3,2,1,0:T(8,128)(2,1)S(1)} %get-tuple-element.30), channel_id=1, source_target_pairs={{0,16},{16,0},{1,17},{17,1},{2,18},{18,2},{3,19},{19,3},{4,20},{20... | collective-permute-start | bytes 2359304 | tf_op jit(solution)/shard_map/ppermute | solution.py:303
  12.4 0.7 copy-start.6
  15.4 37.6 %all-to-all-start = ((bf16[4,2,3,128,128]{4,3,2,1,0:T(8,128)(2,1)}), bf16[4,2,3,128,128]{4,3,2,1,0:T(8,128)(2,1)}, u32[]{:S(2)}, u32[]{:S(2)}) async-start(bf16[4,2,3,128,128]{4,3,2,1,0:T(8,128)(2,1)} %bitcast.33), calls=%async_computation | async-start | bytes 1572864 | tf_op jit(solution)/shard_map/all_to_all | solution.py:334
  19.6 20.0 %collective-permute-start.1 = (bf16[1,2,8,8,3072]{4,3,2,1,0:T(8,128)(2,1)S(1)}, bf16[1,2,8,8,3072]{4,3,2,1,0:T(8,128)(2,1)}, u32[]{:S(2)}, u32[]{:S(2)}) collective-permute-start(bf16[1,2,8,8,3072]{4,3,2,1,0:T(8,128)(2,1)S(1)} %get-tuple-element.29), channel_id=1, source_target_pairs={{0,16},{16,0},{1,17},{17,1},{2,18},{18,2},{3,19},{19,3},{4,20},{20... | collective-permute-start | bytes 2359304 | tf_op jit(solution)/shard_map/ppermute | solution.py:303
  50.9 22.5 %collective-permute-start.10 = (bf16[1,128,3072]{2,1,0:T(8,128)(2,1)}, bf16[1,128,3072]{2,1,0:T(8,128)(2,1)S(1)}, u32[]{:S(2)}, u32[]{:S(2)}) collective-permute-start(bf16[1,128,3072]{2,1,0:T(8,128)(2,1)} %get-tuple-element.11), channel_id=1, source_target_pairs={{0,16},{16,0},{1,17},{17,1},{2,18},{18,2},{3,19},{19,3},{4,20},{20... | collective-permute-start | bytes 2359304 | tf_op jit(solution)/shard_map/ppermute | solution.py:309
  51.4 42.8 %collective-permute-start.13 = (bf16[1,128,3072]{2,1,0:T(8,128)(2,1)}, bf16[1,128,3072]{2,1,0:T(8,128)(2,1)S(1)}, u32[]{:S(2)}, u32[]{:S(2)}) collective-permute-start(bf16[1,128,3072]{2,1,0:T(8,128)(2,1)} %get-tuple-element.12), channel_id=1, source_target_pairs={{0,16},{16,0},{1,17},{17,1},{2,18},{18,2},{3,19},{19,3},{4,20},{20... | collective-permute-start | bytes 2359304 | tf_op jit(solution)/shard_map/ppermute | solution.py:309
  52.9 15.9 %all-to-all-start.1 = ((bf16[4,2,3,128,128]{4,3,2,1,0:T(8,128)(2,1)}), bf16[4,2,3,128,128]{4,3,2,1,0:T(8,128)(2,1)}, u32[]{:S(2)}, u32[]{:S(2)}) async-start(bf16[4,2,3,128,128]{4,3,2,1,0:T(8,128)(2,1)} %bitcast.142), calls=%async_computation.1 | async-start | bytes 1572864 | tf_op jit(solution)/shard_map/all_to_all | solution.py:334
  68.8 16.4 %all-to-all-start.2 = ((bf16[4,2,3,128,128]{4,3,2,1,0:T(8,128)(2,1)}), bf16[4,2,3,128,128]{4,3,2,1,0:T(8,128)(2,1)}, u32[]{:S(2)}, u32[]{:S(2)}) async-start(bf16[4,2,3,128,128]{4,3,2,1,0:T(8,128)(2,1)} %bitcast.143), calls=%async_computation.2 | async-start | bytes 1572864 | tf_op jit(solution)/shard_map/all_to_all | solution.py:334
  73.4 43.9 %copy-start.1 = (bf16[1,128,3072]{2,1,0:T(8,128)(2,1)}, bf16[1,128,3072]{2,1,0:T(8,128)(2,1)S(1)}, u32[]{:S(2)}) copy-start(bf16[1,128,3072]{2,1,0:T(8,128)(2,1)S(1)} %collective-permute-done.10.refs_1_) | copy-start | bytes 2359300
  73.4 40.3 %collective-permute-start.11 = (bf16[1,128,3072]{2,1,0:T(8,128)(2,1)S(1)}, bf16[1,128,3072]{2,1,0:T(8,128)(2,1)}, u32[]{:S(2)}, u32[]{:S(2)}) collective-permute-start(bf16[1,128,3072]{2,1,0:T(8,128)(2,1)S(1)} %collective-permute-done.10.refs_1_), channel_id=1, source_target_pairs={{0,2},{1,3},{2,0},{3,1},{4,6},{5,7},{6,4},{7,5},{8,10},{9,11},{10,... | collective-permute-start | bytes 2359304 | tf_op jit(solution)/shard_map/ppermute | solution.py:354
  85.3 25.2 %all-to-all-start.3 = ((bf16[4,2,3,128,128]{4,3,2,1,0:T(8,128)(2,1)}), bf16[4,2,3,128,128]{4,3,2,1,0:T(8,128)(2,1)S(1)}, u32[]{:S(2)}, u32[]{:S(2)}) async-start(bf16[4,2,3,128,128]{4,3,2,1,0:T(8,128)(2,1)} %bitcast.58), calls=%async_computation.3 | async-start | bytes 1572864 | tf_op jit(solution)/shard_map/all_to_all | solution.py:334
  90.7 20.6 %collective-permute-start.2 = (bf16[4,2,2,128,128]{4,3,2,1,0:T(8,128)(2,1)}, bf16[4,2,2,128,128]{4,3,2,1,0:T(8,128)(2,1)}, u32[]{:S(2)}, u32[]{:S(2)}) collective-permute-start(bf16[4,2,2,128,128]{4,3,2,1,0:T(8,128)(2,1)} %slice.114), channel_id=1, source_target_pairs={{0,4},{4,8},{8,12},{1,5},{5,9},{9,13},{2,6},{6,10},{10,14},{3,7},{... | collective-permute-start | bytes 1572872 | tf_op jit(solution)/shard_map/ppermute | solution.py:339
  94.2 32.5 %copy-start.2 = (bf16[1,128,3072]{2,1,0:T(8,128)(2,1)}, bf16[1,128,3072]{2,1,0:T(8,128)(2,1)S(1)}, u32[]{:S(2)}) copy-start(bf16[1,128,3072]{2,1,0:T(8,128)(2,1)S(1)} %collective-permute-done.13.refs_5_) | copy-start | bytes 2359300
  94.2 32.5 %collective-permute-start.14 = (bf16[1,128,3072]{2,1,0:T(8,128)(2,1)S(1)}, bf16[1,128,3072]{2,1,0:T(8,128)(2,1)S(1)}, u32[]{:S(2)}, u32[]{:S(2)}) collective-permute-start(bf16[1,128,3072]{2,1,0:T(8,128)(2,1)S(1)} %collective-permute-done.13.refs_5_), channel_id=1, source_target_pairs={{0,2},{1,3},{2,0},{3,1},{4,6},{5,7},{6,4},{7,5},{8,10},{9,11},{10,... | collective-permute-start | bytes 2359304 | tf_op jit(solution)/shard_map/ppermute | solution.py:354
  97.6 32.9 %collective-permute-start.4 = (bf16[4,2,2,128,128]{4,3,2,1,0:T(8,128)(2,1)}, bf16[4,2,2,128,128]{4,3,2,1,0:T(8,128)(2,1)}, u32[]{:S(2)}, u32[]{:S(2)}) collective-permute-start(bf16[4,2,2,128,128]{4,3,2,1,0:T(8,128)(2,1)} %slice.114), channel_id=1, source_target_pairs={{4,0},{8,4},{12,8},{5,1},{9,5},{13,9},{6,2},{10,6},{14,10},{7,3},{... | collective-permute-start | bytes 1572872 | tf_op jit(solution)/shard_map/ppermute | solution.py:340
  101.9 26.3 %collective-permute-start.3 = (bf16[4,2,2,128,128]{4,3,2,1,0:T(8,128)(2,1)}, bf16[4,2,2,128,128]{4,3,2,1,0:T(8,128)(2,1)}, u32[]{:S(2)}, u32[]{:S(2)}) collective-permute-start(bf16[4,2,2,128,128]{4,3,2,1,0:T(8,128)(2,1)} %slice.115), channel_id=1, source_target_pairs={{0,4},{4,8},{8,12},{1,5},{5,9},{9,13},{2,6},{6,10},{10,14},{3,7},{... | collective-permute-start | bytes 1572872 | tf_op jit(solution)/shard_map/ppermute | solution.py:339
  110.4 9.2 %copy-start.4 = (bf16[4,2,3,128,128]{4,3,2,1,0:T(8,128)(2,1)}, bf16[4,2,3,128,128]{4,3,2,1,0:T(8,128)(2,1)S(1)}, u32[]{:S(2)}) copy-start(bf16[4,2,3,128,128]{4,3,2,1,0:T(8,128)(2,1)S(1)} %all-to-all-done.3.refs_3_.refs_6_) | copy-start | bytes 2359300
  111.4 22.7 %collective-permute-start.5 = (bf16[4,2,2,128,128]{4,3,2,1,0:T(8,128)(2,1)}, bf16[4,2,2,128,128]{4,3,2,1,0:T(8,128)(2,1)S(1)}, u32[]{:S(2)}, u32[]{:S(2)}) collective-permute-start(bf16[4,2,2,128,128]{4,3,2,1,0:T(8,128)(2,1)} %slice.115), channel_id=1, source_target_pairs={{4,0},{8,4},{12,8},{5,1},{9,5},{13,9},{6,2},{10,6},{14,10},{7,3},{... | collective-permute-start | bytes 1572872 | tf_op jit(solution)/shard_map/ppermute | solution.py:340
  113.7 22.8 %collective-permute-start.6 = (bf16[4,2,2,128,128]{4,3,2,1,0:T(8,128)(2,1)}, bf16[4,2,2,128,128]{4,3,2,1,0:T(8,128)(2,1)}, u32[]{:S(2)}, u32[]{:S(2)}) collective-permute-start(bf16[4,2,2,128,128]{4,3,2,1,0:T(8,128)(2,1)} %slice.116), channel_id=1, source_target_pairs={{0,4},{4,8},{8,12},{1,5},{5,9},{9,13},{2,6},{6,10},{10,14},{3,7},{... | collective-permute-start | bytes 1572872 | tf_op jit(solution)/shard_map/ppermute | solution.py:339
  126.7 1.4 copy-start.3
  126.7 77.8 %collective-permute-start.12 = (bf16[2,128,3072]{2,1,0:T(8,128)(2,1)}, bf16[2,128,3072]{2,1,0:T(8,128)(2,1)}, u32[]{:S(2)}, u32[]{:S(2)}) collective-permute-start(bf16[2,128,3072]{2,1,0:T(8,128)(2,1)} %pad_maximum_fusion), channel_id=1, source_target_pairs={{0,1},{1,0},{2,3},{3,2},{4,5},{5,4},{6,7},{7,6},{8,9},{9,8},{10,11... | collective-permute-start | bytes 4718600 | tf_op jit(solution)/shard_map/ppermute | solution.py:354
  128.1 37.8 %collective-permute-start.8 = (bf16[4,2,2,128,128]{4,3,2,1,0:T(8,128)(2,1)}, bf16[4,2,2,128,128]{4,3,2,1,0:T(8,128)(2,1)S(1)}, u32[]{:S(2)}, u32[]{:S(2)}) collective-permute-start(bf16[4,2,2,128,128]{4,3,2,1,0:T(8,128)(2,1)} %slice.116), channel_id=1, source_target_pairs={{4,0},{8,4},{12,8},{5,1},{9,5},{13,9},{6,2},{10,6},{14,10},{7,3},{... | collective-permute-start | bytes 1572872 | tf_op jit(solution)/shard_map/ppermute | solution.py:340
  130.5 35.4 %collective-permute-start.7 = (bf16[4,2,2,128,128]{4,3,2,1,0:T(8,128)(2,1)}, bf16[4,2,2,128,128]{4,3,2,1,0:T(8,128)(2,1)S(1)}, u32[]{:S(2)}, u32[]{:S(2)}) collective-permute-start(bf16[4,2,2,128,128]{4,3,2,1,0:T(8,128)(2,1)} %slice.117), channel_id=1, source_target_pairs={{0,4},{4,8},{8,12},{1,5},{5,9},{9,13},{2,6},{6,10},{10,14},{3,7},{... | collective-permute-start | bytes 1572872 | tf_op jit(solution)/shard_map/ppermute | solution.py:339
  134.0 2.5 %copy-start.7 = (bf16[4,2,2,128,128]{4,3,2,1,0:T(8,128)(2,1)}, bf16[4,2,2,128,128]{4,3,2,1,0:T(8,128)(2,1)S(1)}, u32[]{:S(2)}) copy-start(bf16[4,2,2,128,128]{4,3,2,1,0:T(8,128)(2,1)S(1)} %collective-permute-done.5.refs_9_) | copy-start | bytes 1572868
  134.0 31.9 %collective-permute-start.9 = (bf16[4,2,2,128,128]{4,3,2,1,0:T(8,128)(2,1)}, bf16[4,2,2,128,128]{4,3,2,1,0:T(8,128)(2,1)S(1)}, u32[]{:S(2)}, u32[]{:S(2)}) collective-permute-start(bf16[4,2,2,128,128]{4,3,2,1,0:T(8,128)(2,1)} %slice.117), channel_id=1, source_target_pairs={{4,0},{8,4},{12,8},{5,1},{9,5},{13,9},{6,2},{10,6},{14,10},{7,3},{... | collective-permute-start | bytes 1572872 | tf_op jit(solution)/shard_map/ppermute | solution.py:340
  136.6 70.7 %collective-permute-start.15 = (bf16[2,128,3072]{2,1,0:T(8,128)(2,1)}, bf16[2,128,3072]{2,1,0:T(8,128)(2,1)S(1)}, u32[]{:S(2)}, u32[]{:S(2)}) collective-permute-start(bf16[2,128,3072]{2,1,0:T(8,128)(2,1)} %pad_maximum_fusion.1), channel_id=1, source_target_pairs={{0,1},{1,0},{2,3},{3,2},{4,5},{5,4},{6,7},{7,6},{8,9},{9,8},{10,11... | collective-permute-start | bytes 4718600 | tf_op jit(solution)/shard_map/ppermute | solution.py:354
  165.9 0.8 copy-start.9
  165.9 1.0 copy-start.8
  166.9 0.8 copy-start.10
  201.0 18.9 %all-to-all-start.4 = ((bf16[8,2,256,128]{3,2,1,0:T(8,128)(2,1)}), bf16[8,2,256,128]{3,2,1,0:T(8,128)(2,1)S(1)}, u32[]{:S(2)}, u32[]{:S(2)}) async-start(bf16[8,2,256,128]{3,2,1,0:T(8,128)(2,1)} %bitcast.144), calls=%async_computation.4 | async-start | bytes 2097152 | tf_op jit(solution)/shard_map/all_to_all | solution.py:369
  219.9 1.0 copy-start

commit v3 on v2

--- a/solution.py
+++ b/solution.py
@@ -127,6 +127,9 @@
     return result.astype(jnp.bfloat16)
 
 
+REMOTE_CUTS = 2
+
+
 def shift_perm(count, by):
     return [(i, (i + by) % count) for i in range(count)]
 
@@ -135,69 +138,83 @@
     return lax.optimization_barrier((value, earlier))[0]
 
 
-def attention_kernel(parts, columns, scale, first, last, valid_ref, *refs):
-    queries = refs[: parts]
+def attention_kernel(parts, columns, scale, first, last, scalar_ref, *refs):
+    queries = refs[:parts]
     rest = refs[parts:]
     if not first:
         before_ref, rest = rest[0], rest[1:]
-    kv_refs, out_ref, state_ref = rest[:-2], rest[-2], rest[-1]
+    kv_refs, out_ref = rest[:-1], rest[-1]
     groups = len(kv_refs) // 3
     head_dim = queries[0].shape[-1]
+    at_peak = 2 * head_dim - 1
+    to_exp2 = scale * math.log2(math.e)
     column = pl.program_id(1)
     edge = (column == 0) | (column == columns - 1)
-    to_exp2 = scale * math.log2(math.e)
-    state_ref = state_ref if last else out_ref.at[0, 0]
-
-    def one_row(row, start, width):
+    both = scalar_ref[0] > 0
+
+    def block(start, width, rows):
         query = jnp.concatenate([ref[0, 0, 0] for ref in queries], axis=0)
-        scores, values = [], []
-        for group in range(groups):
-            ref = kv_refs[row * groups + group]
+        keys, values = [], []
+        for ref in kv_refs[: rows * groups]:
             tokens = ref.shape[3]
             at = ref.shape[2] - 2
             key = ref[pl.ds(start, width), 0, at].reshape(width * tokens, head_dim)
-            values.append(ref[pl.ds(start, width), 0, at + 1].reshape(width * tokens, head_dim))
-            scores.append(
-                lax.dot_general(
-                    query, key, (((1,), (1,)), ((), ())), preferred_element_type=jnp.float32
-                )
+            value = ref[pl.ds(start, width), 0, at + 1].reshape(width * tokens, head_dim)
+            keys.append(key)
+            values.append(jnp.concatenate([value, jnp.ones_like(value)], axis=1))
+        halves = 2
+        each = query.shape[0] // halves
+
+        def score(half, key):
+            return lax.dot_general(
+                query[half * each : (half + 1) * each],
+                key,
+                (((1,), (1,)), ((), ())),
+                preferred_element_type=jnp.float32,
             )
-        peak = scores[0].max(axis=1, keepdims=True)
-        for score in scores[1:]:
-            peak = jnp.maximum(peak, score.max(axis=1, keepdims=True))
-        fresh = first and row == 0
-        old_ref = state_ref if row > 0 or first else before_ref.at[0, 0]
-        if not fresh:
-            old_peak = old_ref[:, head_dim : head_dim + 1]
-            peak = jnp.maximum(peak, old_peak)
-            fade = jnp.exp2((old_peak - peak) * to_exp2)
-        offset = peak * to_exp2
-        total, summed = 0.0, 0.0
-        for score, value in zip(scores, values):
-            weight = jnp.exp2(score * to_exp2 - offset)
-            total = total + weight.sum(axis=1, keepdims=True)
-            summed = summed + jnp.dot(
-                weight.astype(jnp.bfloat16), value, preferred_element_type=jnp.float32
-            )
-        if not fresh:
-            total = total + old_ref[:, head_dim + 1 : head_dim + 2] * fade
-            summed = summed + old_ref[:, :head_dim] * fade
-        state_ref[:, :head_dim] = summed
-        state_ref[:, head_dim : head_dim + 1] = peak
-        state_ref[:, head_dim + 1 : head_dim + 2] = total
-
-    def all_rows(start, width):
-        one_row(0, start, width)
-        for row in (1, 2):
-            pl.when(valid_ref[row - 1] > 0)(lambda row=row: one_row(row, start, width))
-
-    pl.when(edge)(lambda: all_rows(jnp.where(column == 0, 0, columns - 2), 2))
-    pl.when(jnp.logical_not(edge))(lambda: all_rows(column - 1, 3))
-    if last:
-        out = state_ref[:, :head_dim] / state_ref[:, head_dim + 1 : head_dim + 2]
-        places, each = out_ref.shape[0], out_ref.shape[3]
-        for by in range(places):
-            out_ref[valid_ref[2 + by], 0, 0] = out[by * each : (by + 1) * each].astype(out_ref.dtype)
+
+        scores = [score(0, key) for key in keys]
+        for half in range(halves):
+            here = slice(half * each, (half + 1) * each)
+            peak = None
+            for part in scores:
+                for low in range(0, part.shape[1], head_dim):
+                    piece = part[:, low : low + head_dim]
+                    peak = piece if peak is None else jnp.maximum(peak, piece)
+            peak = peak.max(axis=1, keepdims=True)
+            if not first:
+                old_peak = before_ref[0, 0, here, at_peak:]
+                peak = jnp.maximum(peak, old_peak)
+            offset = peak * to_exp2
+            summed = None
+            ahead = []
+            for key, value, part in zip(keys, values, scores):
+                if half + 1 < halves:
+                    ahead.append(score(half + 1, key))
+                weight = jnp.exp2(part * to_exp2 - offset).astype(jnp.bfloat16)
+                term = jnp.dot(weight, value, preferred_element_type=jnp.float32)
+                summed = term if summed is None else summed + term
+            if not first:
+                fade = jnp.exp2(old_peak * to_exp2 - offset)
+                summed = summed + before_ref[0, 0, here, :] * fade
+            if last:
+                out = summed[:, :head_dim] / summed[:, head_dim : head_dim + 1]
+                out = out.astype(out_ref.dtype)
+                piece = out_ref.shape[3]
+                size = min(piece, each)
+                for low in range(0, each, size):
+                    place, at = divmod(half * each + low, piece)
+                    out_ref[scalar_ref[1 + place], 0, 0, at : at + size] = out[low : low + size]
+            else:
+                out_ref[0, 0, here, :] = summed
+                out_ref[0, 0, here, at_peak:] = peak
+            scores = ahead
+
+    for at_edge in (True, False):
+        for rows in (2, 3):
+            start = jnp.where(column == 0, 0, columns - 2) if at_edge else column - 1
+            case = (edge == at_edge) & (both == (rows == 3))
+            pl.when(case)(functools.partial(block, start, 2 if at_edge else 3, rows))
 
 
 def attend(valid, streams, before, rows, scale, last, places):
@@ -235,7 +252,6 @@
             + [pl.BlockSpec((1, 1, tokens, 2 * head_dim), at_query) for _ in state]
             + [kv_spec(kv) for kv in rows],
             out_specs=out_spec,
-            scratch_shapes=[pltpu.VMEM((tokens, 2 * head_dim), jnp.float32)],
         ),
         out_shape=out_shape,
         cost_estimate=pl.CostEstimate(
@@ -294,7 +310,7 @@
     heads_local, head_dim = input_weight.shape[2:]
     heads_each = heads_local // col_parts
     here, column_at = lax.axis_index("ta"), lax.axis_index("wa")
-    cuts = 2 if frames % 2 == 0 else 1
+    cuts = REMOTE_CUTS if frames % REMOTE_CUTS == 0 else 1
     step = frames // cuts
     own = [lax.slice_in_dim(latents, i * step, (i + 1) * step, axis=1) for i in range(cuts)]
     chunks = [latents]
@@ -324,26 +340,24 @@
 
     streams = []
     ready = None
-    for at, chunk in enumerate(chunks):
+    for chunk in chunks:
         if ready is not None:
             chunk = after(chunk, ready)
         ready = project(chunk)
-        for part in range(cuts if at == 0 else 1):
-            dealt = lax.slice_in_dim(ready, part * step, (part + 1) * step, axis=3)
-            dealt = dealt.reshape(col_parts, heads_each, 3, -1, head_dim)
-            streams.append(lax.all_to_all(dealt, "wa", 0, 0))
-    down = [(i, i + 1) for i in range(row_parts - 1)]
-    up = [(i + 1, i) for i in range(row_parts - 1)]
-    above, below = [], []
+        dealt = ready.reshape(col_parts, heads_each, 3, -1, head_dim)
+        streams.append(lax.all_to_all(dealt, "wa", 0, 0))
+    pair = [(i, i ^ 1) for i in range(row_parts)]
+    side = [(i, ((i + 1) ^ 1) - 1) for i in range(1, row_parts - 1)]
+    side += [(i, i) for i in {0, row_parts - 1}]
+    paired, beside = [], []
     for stream in streams:
-        above.append(lax.ppermute(stream[:, :, 1:], "ha", down))
-        below.append(lax.ppermute(stream[:, :, 1:], "ha", up))
+        keys_values = stream[:, :, 1:]
+        paired.append(lax.ppermute(keys_values, "ha", pair))
+        beside.append(lax.ppermute(keys_values, "ha", sorted(side)))
     height_index = lax.axis_index("ha")
+    inside = (height_index > 0) & (height_index < row_parts - 1)
     places = [lax.rem(here + (frame_parts - by), frame_parts) for by in range(frame_parts)]
-    scalars = jnp.stack(
-        [(height_index > 0).astype(jnp.int32), (height_index < row_parts - 1).astype(jnp.int32)]
-        + places
-    )
+    scalars = jnp.stack([inside.astype(jnp.int32)] + places)
     scale = 1.0 / math.sqrt(head_dim)
 
     def spread(block):
@@ -351,18 +365,16 @@
         distance = col_parts // 2
         while distance:
             perm = [(i, i ^ distance) for i in range(col_parts)]
-            got = lax.ppermute(jnp.concatenate([b for _, b in held], axis=0), "wa", perm)
-            held = held + [
-                (mask ^ distance, got[i : i + 1]) for i, (mask, _) in enumerate(held)
-            ]
+            got = []
+            for mask, part in held:
+                got.append((mask ^ distance, lax.ppermute(part, "wa", perm)))
+            held = held + got
             distance //= 2
         return held
 
-    state = attend(
-        scalars, streams, None, streams[:cuts] + above[:cuts] + below[:cuts], scale, False, 1
-    )
+    state = attend(scalars, streams, None, [streams[0], paired[0], beside[0]], scale, False, 1)
     attended = attend(
-        scalars, streams, state, streams[cuts:] + above[cuts:] + below[cuts:], scale, True,
+        scalars, streams, state, streams[1:] + paired[1:] + beside[1:], scale, True,
         frame_parts,
     )
     sent = attended.reshape(frame_parts * col_parts, heads_each, -1, head_dim)
@@ -393,6 +405,7 @@
         frames = latents.shape[1] * lax.axis_size("ta")
         width = lax.axis_size("wa")
         dealt_heads = input_weight.shape[2] % width == 0 and width & (width - 1) == 0
+        dealt_heads &= lax.axis_size("ha") % 2 == 0
         if latents.shape[0] == 1 and dealt_heads and frames <= 2 * TILE_T:
             return row_plan(latents, input_weight, norm_gains, output_weight)
         return halo_plan(latents, input_weight, norm_gains, output_weight)

time: 232 us -> 172 us (0.74)
  the two profiles are of different devices: /device:TPU:16 before, /device:TPU:0 now
where the time goes in v3:
time: 172 us; the launch traced here: 170 us
  starting transfers between devices  45 us (26%)
  waiting for transfers between devices  39.5 us (23%)
  Pallas kernels  37.8 us (22%)
  matrix products  29.6 us (17%)
  local copies, waits for them, and re-layouts  13.8 us (8%)
  other arithmetic  3.84 us (2%)
    dot_general x3, matrix products, project(): jnp.einsum('cfhwd,dsne->cfhwsne', chunk, input_weight, preferred_element_...  29.6 us
    pallas_call x2, Pallas kernels, attend(): pl.pallas_call(functools.partial(attention_kernel, len(streams), columns,...  28 us
    ppermute x3, starting transfers between devices, row_plan(): beside.append(lax.ppermute(keys_values, 'ha', sorted(side)))  20.2 us
    ppermute x6, waiting for transfers between devices, spread(): got.append((mask ^ distance, lax.ppermute(part, 'wa', perm)))  15.9 us
    all_to_all x3, starting transfers between devices, row_plan(): streams.append(lax.all_to_all(dealt, 'wa', 0, 0))  11.3 us
    all_to_all x1, waiting for transfers between devices, row_plan(): got = lax.all_to_all(sent, ('ta', 'wa'), 0, 0)  10.1 us
    pallas_call x1, Pallas kernels, mix(): pl.pallas_call(mix_kernel, grid_spec=pltpu.PrefetchScalarGridSpec(num_sca...  9.81 us
    all_to_all x3, waiting for transfers between devices, row_plan(): streams.append(lax.all_to_all(dealt, 'wa', 0, 0))  7.4 us
  transfers between devices with their start and end apart: 20, of which 4 were waited for; matrix products, arithmetic and copies ran while one was open for 26% of the time, Pallas kernels for 16%

profile of v3, /device:TPU:0, one launch (start us, length us, event | category | flops | bytes accessed | tf_op | source)
XLA Modules:
  0.0 169.8 jit_solution(901103041382042314)
XLA Ops:
  0.0 1.6 fusion.27
  1.6 3.1 %collective-permute-start = (bf16[1,2,8,8,3072]{4,3,2,1,0:T(8,128)(2,1)S(1)}, bf16[1,2,8,8,3072]{4,3,2,1,0:T(8,128)(2,1)}, u32[]{:S(2)}, u32[]{:S(2)}) collective-permute-start(bf16[1,2,8,8,3072]{4,3,2,1,0:T(8,128)(2,1)S(1)} %get-tuple-element.26), channel_id=1, source_target_pairs={{0,16},{16,0},{1,17},{17,1},{2,18},{18,2},{3,19},{19,3},{4,20},{20... | collective-permute-start | bytes 2359304 | tf_op jit(solution)/shard_map/ppermute | solution.py:319
  4.7 9.3 %fusion.6 = f32[1,4,8,8,3,8,128]{6,3,5,4,2,1,0:T(8,128)S(1)} fusion(bf16[3072,3,8,128,1,1]{3,2,1,0,5,4:T(8,128)(2,1)} %bitcast.142, bf16[1,4,8,8,3072]{4,3,2,1,0:T(8,128)(2,1)S(1)} %copy-done.3), kind=kOutput, calls=%fused_computation.6 | convolution fusion | flops 4831838208 | bytes 23592960 | tf_op jit(solution)/shard_map/cfhwd,dsne->cfhwsne/dot_general | solution.py:329
  14.0 0.6 multiply_reduce_fusion.1
  14.6 0.7 fusion.18
  15.4 0.1 fusion.20
  15.5 0.2 maximum_bitcast_fusion
  15.6 1.6 copy.8
  17.2 3.6 %all-to-all-start = ((bf16[4,2,3,256,128]{4,3,2,1,0:T(8,128)(2,1)}), bf16[4,2,3,256,128]{4,3,2,1,0:T(8,128)(2,1)S(1)}, u32[]{:S(2)}, u32[]{:S(2)}) async-start(bf16[4,2,3,256,128]{4,3,2,1,0:T(8,128)(2,1)} %bitcast.32), calls=%async_computation | async-start | bytes 3145728 | tf_op jit(solution)/shard_map/all_to_all | solution.py:348
  20.8 0.3 collective-permute-start.1
  21.1 2.7 %constant_dynamic-slice_fusion = (bf16[1,128,3072]{2,1,0:T(8,128)(2,1)}, bf16[1,128,3072]{2,1,0:T(8,128)(2,1)}) fusion(bf16[8,128,3072]{2,1,0:T(8,128)(2,1)} %refs_0_.1, s32[]{:T(128)S(6)} %select_n.7, s32[]{:T(128)S(6)} %select_n.6), kind=kLoop, calls=%fused_computation.54 | loop fusion | bytes 3145736 | tf_op jit(solution)/shard_map/dynamic_slice | solution.py:324
  23.7 10.2 %fusion.13 = f32[1,2,8,8,3,8,128]{6,3,5,4,2,1,0:T(8,128)S(1)} fusion(bf16[3072,3,8,128,1,1]{3,2,1,0,5,4:T(8,128)(2,1)} %bitcast.143, bf16[1,2,8,8,3072]{4,3,2,1,0:T(8,128)(2,1)} %collective-permute-done), kind=kOutput, calls=%fused_computation.10 | convolution fusion | flops 2415919104 | bytes 21233664 | tf_op jit(solution)/shard_map/cfhwd,dsne->cfhwsne/dot_general | solution.py:329
  33.9 0.3 multiply_reduce_fusion.5
  34.4 0.3 fusion.21
  34.7 0.1 maximum_bitcast_fusion.1
  34.8 6.0 %collective-permute-done.1 = bf16[1,2,8,8,3072]{4,3,2,1,0:T(8,128)(2,1)} collective-permute-done((bf16[1,2,8,8,3072]{4,3,2,1,0:T(8,128)(2,1)S(1)}, bf16[1,2,8,8,3072]{4,3,2,1,0:T(8,128)(2,1)}, u32[]{:S(2)}, u32[]{:S(2)}) %collective-permute-start.1) | collective-permute-done | bytes 786464 | tf_op jit(solution)/shard_map/ppermute | solution.py:319
  40.8 10.2 %fusion.10 = f32[1,2,8,8,3,8,128]{6,3,5,2,1,4,0:T(8,128)S(1)} fusion(bf16[3072,3,8,128,1,1]{3,2,1,0,5,4:T(8,128)(2,1)} %bitcast.144, bf16[1,2,8,8,3072]{4,3,2,1,0:T(8,128)(2,1)} %collective-permute-done.1), kind=kOutput, calls=%fused_computation.9 | convolution fusion | flops 2415919104 | bytes 21233664 | tf_op jit(solution)/shard_map/cfhwd,dsne->cfhwsne/dot_general | solution.py:329
  51.0 1.1 copy.12
  52.1 0.3 collective-permute-start.8
  52.4 0.3 multiply_reduce_fusion.3
  52.8 4.2 %all-to-all-start.1 = ((bf16[4,2,3,128,128]{4,3,2,1,0:T(8,128)(2,1)}), bf16[4,2,3,128,128]{4,3,2,1,0:T(8,128)(2,1)}, u32[]{:S(2)}, u32[]{:S(2)}) async-start(bf16[4,2,3,128,128]{4,3,2,1,0:T(8,128)(2,1)} %bitcast.140), calls=%async_computation.1 | async-start | bytes 1572864 | tf_op jit(solution)/shard_map/all_to_all | solution.py:348
  57.0 1.1 slice.80
  58.1 1.8 %collective-permute-start.2 = (bf16[4,2,2,256,128]{4,3,2,1,0:T(8,128)(2,1)}, bf16[4,2,2,256,128]{4,3,2,1,0:T(8,128)(2,1)}, u32[]{:S(2)}, u32[]{:S(2)}) collective-permute-start(bf16[4,2,2,256,128]{4,3,2,1,0:T(8,128)(2,1)} %slice.80), channel_id=1, source_target_pairs={{0,4},{4,0},{8,12},{12,8},{1,5},{5,1},{9,13},{13,9},{2,6},{6,2},{1... | collective-permute-start | bytes 3145736 | tf_op jit(solution)/shard_map/ppermute | solution.py:355
  59.9 9.5 %collective-permute-start.3 = (bf16[4,2,2,256,128]{4,3,2,1,0:T(8,128)(2,1)}, bf16[4,2,2,256,128]{4,3,2,1,0:T(8,128)(2,1)}, u32[]{:S(2)}, u32[]{:S(2)}) collective-permute-start(bf16[4,2,2,256,128]{4,3,2,1,0:T(8,128)(2,1)} %slice.80), channel_id=1, source_target_pairs={{0,0},{4,8},{8,4},{12,12},{1,1},{5,9},{9,5},{13,13},{2,2},{6,10},{... | collective-permute-start | bytes 3145736 | tf_op jit(solution)/shard_map/ppermute | solution.py:356
  69.3 0.3 fusion.23
  69.7 0.1 maximum_bitcast_fusion.2
  69.8 1.1 copy.15
  71.0 3.5 %all-to-all-start.2 = ((bf16[4,2,3,128,128]{4,3,2,1,0:T(8,128)(2,1)}), bf16[4,2,3,128,128]{4,3,2,1,0:T(8,128)(2,1)S(1)}, u32[]{:S(2)}, u32[]{:S(2)}) async-start(bf16[4,2,3,128,128]{4,3,2,1,0:T(8,128)(2,1)} %bitcast.56), calls=%async_computation.2 | async-start | bytes 1572864 | tf_op jit(solution)/shard_map/all_to_all | solution.py:348
  74.5 1.6 collective-permute-start.12
  76.1 0.7 pad_add_fusion.scalar_ref
  76.7 1.9 %slice.81 = bf16[4,2,2,128,128]{4,3,2,1,0:T(8,128)(2,1)} slice(bf16[4,2,3,128,128]{4,3,2,1,0:T(8,128)(2,1)} %all-to-all-done.1.refs_1_.refs_4_), slice={[0:4], [0:2], [1:3], [0:128], [0:128]} | slice | bytes 1048576 | tf_op jit(solution)/shard_map/slice | solution.py:354
  78.7 7.4 %all-to-all-done.2.refs_2_.refs_5_ = bf16[4,2,3,128,128]{4,3,2,1,0:T(8,128)(2,1)S(1)} async-done(((bf16[4,2,3,128,128]{4,3,2,1,0:T(8,128)(2,1)}), bf16[4,2,3,128,128]{4,3,2,1,0:T(8,128)(2,1)S(1)}, u32[]{:S(2)}, u32[]{:S(2)}) %all-to-all-start.2) | async-done | bytes 786464 | tf_op jit(solution)/shard_map/all_to_all | solution.py:348
  86.1 0.9 slice.82
  86.9 5.4 %collective-permute-start.6 = (bf16[4,2,2,128,128]{4,3,2,1,0:T(8,128)(2,1)}, bf16[4,2,2,128,128]{4,3,2,1,0:T(8,128)(2,1)}, u32[]{:S(2)}, u32[]{:S(2)}) collective-permute-start(bf16[4,2,2,128,128]{4,3,2,1,0:T(8,128)(2,1)} %slice.81), channel_id=1, source_target_pairs={{0,0},{4,8},{8,4},{12,12},{1,1},{5,9},{9,5},{13,13},{2,2},{6,10},{... | collective-permute-start | bytes 1572872 | tf_op jit(solution)/shard_map/ppermute | solution.py:356
  92.3 5.4 %collective-permute-start.7 = (bf16[4,2,2,128,128]{4,3,2,1,0:T(8,128)(2,1)}, bf16[4,2,2,128,128]{4,3,2,1,0:T(8,128)(2,1)}, u32[]{:S(2)}, u32[]{:S(2)}) collective-permute-start(bf16[4,2,2,128,128]{4,3,2,1,0:T(8,128)(2,1)} %slice.82), channel_id=1, source_target_pairs={{0,0},{4,8},{8,4},{12,12},{1,1},{5,9},{9,5},{13,13},{2,2},{6,10},{... | collective-permute-start | bytes 1572872 | tf_op jit(solution)/shard_map/ppermute | solution.py:356
  97.7 12.9 %tile_attention.2.refs_3_ = f32[4,2,512,256]{3,2,1,0:T(8,128)} custom-call(s32[3]{0:T(128)} %pad_add_fusion.scalar_ref, bf16[4,2,3,256,128]{4,3,2,1,0:T(8,128)(2,1)} %copy-done, bf16[4,2,3,128,128]{4,3,2,1,0:T(8,128)(2,1)} %all-to-all-done.1.refs_1_.refs_4_, bf16[4,2,3,128,128]{4,3,2,1,0:T(8,128)(2,1)} %copy-done.2, bf16[4,2,3,256,128]{4,3,2,1,0:T(8,128)(2,1)} %copy-done, ...), custom_call_target="tpu_custom_call" | custom-call | flops 8053063680 | bytes 31457280 | tf_op jit(solution)/shard_map/tile_attention/pallas_call | solution.py:243
  110.6 0.5 collective-permute-start.9
  111.0 1.6 collective-permute-start.13
  112.7 15.0 %tile_attention.3 = bf16[2,4,2,256,128]{4,3,2,1,0:T(8,128)(2,1)} custom-call(s32[3]{0:T(128)} %pad_add_fusion.scalar_ref, bf16[4,2,3,256,128]{4,3,2,1,0:T(8,128)(2,1)} %copy-done, bf16[4,2,3,128,128]{4,3,2,1,0:T(8,128)(2,1)} %all-to-all-done.1.refs_1_.refs_4_, bf16[4,2,3,128,128]{4,3,2,1,0:T(8,128)(2,1)} %copy-done.2, ...), custom_call_target="tpu_custom_call" | custom-call | flops 8053063680 | bytes 31457280 | tf_op jit(solution)/shard_map/tile_attention/pallas_call | solution.py:243
  127.7 3.6 %all-to-all-start.3 = ((bf16[8,2,256,128]{3,2,1,0:T(8,128)(2,1)}), bf16[8,2,256,128]{3,2,1,0:T(8,128)(2,1)S(1)}, u32[]{:S(2)}, u32[]{:S(2)}) async-start(bf16[8,2,256,128]{3,2,1,0:T(8,128)(2,1)} %bitcast.141), calls=%async_computation.3 | async-start | bytes 2097152 | tf_op jit(solution)/shard_map/all_to_all | solution.py:381
  131.3 0.4 collective-permute-start.10
  131.7 0.2 collective-permute-start.14
  131.9 0.3 collective-permute-start.11
  132.2 15.9 %collective-permute-done.13.refs_6_ = bf16[1,128,3072]{2,1,0:T(8,128)(2,1)S(1)} collective-permute-done((bf16[1,128,3072]{2,1,0:T(8,128)(2,1)S(1)}, bf16[1,128,3072]{2,1,0:T(8,128)(2,1)S(1)}, u32[]{:S(2)}, u32[]{:S(2)}) %collective-permute-start.13) | collective-permute-done | bytes 786464 | tf_op jit(solution)/shard_map/ppermute | solution.py:370
  148.1 0.7 stack.115.at_ref
  148.9 10.1 %all-to-all-done.3 = bf16[8,2,256,128]{3,2,1,0:T(8,128)(2,1)S(1)} async-done(((bf16[8,2,256,128]{3,2,1,0:T(8,128)(2,1)}), bf16[8,2,256,128]{3,2,1,0:T(8,128)(2,1)S(1)}, u32[]{:S(2)}, u32[]{:S(2)}) %all-to-all-start.3) | async-done | bytes 1048608 | tf_op jit(solution)/shard_map/all_to_all | solution.py:381
  159.0 1.0 copy-done.1
  160.0 9.8 %mix_heads.1 = bf16[256,3072]{1,0:T(8,128)(2,1)} custom-call(s32[16]{0:T(128)} %stack.115.at_ref, bf16[16,256,128]{2,1,0:T(8,128)(2,1)} %bitcast.139, bf16[8,128,3072]{2,1,0:T(8,128)(2,1)} %refs_0_.1, bf16[1,128,3072]{2,1,0:T(8,128)(2,1)} %collective-permute-done.8.refs_1_, bf16[1,128,3072]{2,1,0:T(8,128)(2,1)} %copy-done.5, ...), custom_call_target="tpu_custom_call" | custom-call | flops 3221225472 | bytes 12582912 | tf_op jit(solution)/shard_map/mix_heads/pallas_call | solution.py:283
  (44 shorter events, 0.3 us)
Async XLA Ops:
  0.0 4.7 %copy-start.3 = (bf16[1,4,8,8,3072]{4,3,2,1,0:T(8,128)(2,1)S(1)}, bf16[1,4,8,8,3072]{4,3,2,1,0:T(8,128)(2,1)}, u32[]{:S(2)}) copy-start(bf16[1,4,8,8,3072]{4,3,2,1,0:T(8,128)(2,1)} %param.4) | copy-start | bytes 4718596
  1.6 22.1 %collective-permute-start = (bf16[1,2,8,8,3072]{4,3,2,1,0:T(8,128)(2,1)S(1)}, bf16[1,2,8,8,3072]{4,3,2,1,0:T(8,128)(2,1)}, u32[]{:S(2)}, u32[]{:S(2)}) collective-permute-start(bf16[1,2,8,8,3072]{4,3,2,1,0:T(8,128)(2,1)S(1)} %get-tuple-element.26), channel_id=1, source_target_pairs={{0,16},{16,0},{1,17},{17,1},{2,18},{18,2},{3,19},{19,3},{4,20},{20... | collective-permute-start | bytes 2359304 | tf_op jit(solution)/shard_map/ppermute | solution.py:319
  4.7 9.3 %copy-start.8 = (f32[2,128]{1,0:T(2,128)S(1)}, f32[2,128]{1,0:T(2,128)}, u32[]{:S(2)}) copy-start(f32[2,128]{1,0:T(2,128)} %param.6) | copy-start | bytes 3076
  17.2 35.5 %all-to-all-start = ((bf16[4,2,3,256,128]{4,3,2,1,0:T(8,128)(2,1)}), bf16[4,2,3,256,128]{4,3,2,1,0:T(8,128)(2,1)S(1)}, u32[]{:S(2)}, u32[]{:S(2)}) async-start(bf16[4,2,3,256,128]{4,3,2,1,0:T(8,128)(2,1)} %bitcast.32), calls=%async_computation | async-start | bytes 3145728 | tf_op jit(solution)/shard_map/all_to_all | solution.py:348
  20.8 20.0 %collective-permute-start.1 = (bf16[1,2,8,8,3072]{4,3,2,1,0:T(8,128)(2,1)S(1)}, bf16[1,2,8,8,3072]{4,3,2,1,0:T(8,128)(2,1)}, u32[]{:S(2)}, u32[]{:S(2)}) collective-permute-start(bf16[1,2,8,8,3072]{4,3,2,1,0:T(8,128)(2,1)S(1)} %get-tuple-element.25), channel_id=1, source_target_pairs={{0,16},{16,0},{1,17},{17,1},{2,18},{18,2},{3,19},{19,3},{4,20},{20... | collective-permute-start | bytes 2359304 | tf_op jit(solution)/shard_map/ppermute | solution.py:319
  52.1 34.8 %collective-permute-start.8 = (bf16[1,128,3072]{2,1,0:T(8,128)(2,1)}, bf16[1,128,3072]{2,1,0:T(8,128)(2,1)}, u32[]{:S(2)}, u32[]{:S(2)}) collective-permute-start(bf16[1,128,3072]{2,1,0:T(8,128)(2,1)} %get-tuple-element.11), channel_id=1, source_target_pairs={{0,16},{16,0},{1,17},{17,1},{2,18},{18,2},{3,19},{19,3},{4,20},{20... | collective-permute-start | bytes 2359304 | tf_op jit(solution)/shard_map/ppermute | solution.py:325
  52.8 5.3 %copy-start = (bf16[4,2,3,256,128]{4,3,2,1,0:T(8,128)(2,1)}, bf16[4,2,3,256,128]{4,3,2,1,0:T(8,128)(2,1)S(1)}, u32[]{:S(2)}) copy-start(bf16[4,2,3,256,128]{4,3,2,1,0:T(8,128)(2,1)S(1)} %all-to-all-done.refs_0_.refs_3_) | copy-start | bytes 4718596
  52.8 18.2 %all-to-all-start.1 = ((bf16[4,2,3,128,128]{4,3,2,1,0:T(8,128)(2,1)}), bf16[4,2,3,128,128]{4,3,2,1,0:T(8,128)(2,1)}, u32[]{:S(2)}, u32[]{:S(2)}) async-start(bf16[4,2,3,128,128]{4,3,2,1,0:T(8,128)(2,1)} %bitcast.140), calls=%async_computation.1 | async-start | bytes 1572864 | tf_op jit(solution)/shard_map/all_to_all | solution.py:348
  58.1 34.2 %collective-permute-start.2 = (bf16[4,2,2,256,128]{4,3,2,1,0:T(8,128)(2,1)}, bf16[4,2,2,256,128]{4,3,2,1,0:T(8,128)(2,1)}, u32[]{:S(2)}, u32[]{:S(2)}) collective-permute-start(bf16[4,2,2,256,128]{4,3,2,1,0:T(8,128)(2,1)} %slice.80), channel_id=1, source_target_pairs={{0,4},{4,0},{8,12},{12,8},{1,5},{5,1},{9,13},{13,9},{2,6},{6,2},{1... | collective-permute-start | bytes 3145736 | tf_op jit(solution)/shard_map/ppermute | solution.py:355
  59.9 32.4 %collective-permute-start.3 = (bf16[4,2,2,256,128]{4,3,2,1,0:T(8,128)(2,1)}, bf16[4,2,2,256,128]{4,3,2,1,0:T(8,128)(2,1)}, u32[]{:S(2)}, u32[]{:S(2)}) collective-permute-start(bf16[4,2,2,256,128]{4,3,2,1,0:T(8,128)(2,1)} %slice.80), channel_id=1, source_target_pairs={{0,0},{4,8},{8,4},{12,12},{1,1},{5,9},{9,5},{13,13},{2,2},{6,10},{... | collective-permute-start | bytes 3145736 | tf_op jit(solution)/shard_map/ppermute | solution.py:356
  69.8 4.6 %copy-start.7 = (bf16[1,128,3072]{2,1,0:T(8,128)(2,1)S(1)}, bf16[1,128,3072]{2,1,0:T(8,128)(2,1)}, u32[]{:S(2)}) copy-start(bf16[1,128,3072]{2,1,0:T(8,128)(2,1)} %get-tuple-element.12) | copy-start | bytes 2359300
  71.0 15.1 %all-to-all-start.2 = ((bf16[4,2,3,128,128]{4,3,2,1,0:T(8,128)(2,1)}), bf16[4,2,3,128,128]{4,3,2,1,0:T(8,128)(2,1)S(1)}, u32[]{:S(2)}, u32[]{:S(2)}) async-start(bf16[4,2,3,128,128]{4,3,2,1,0:T(8,128)(2,1)} %bitcast.56), calls=%async_computation.2 | async-start | bytes 1572864 | tf_op jit(solution)/shard_map/all_to_all | solution.py:348
  74.5 36.1 %collective-permute-start.12 = (bf16[1,128,3072]{2,1,0:T(8,128)(2,1)S(1)}, bf16[1,128,3072]{2,1,0:T(8,128)(2,1)S(1)}, u32[]{:S(2)}, u32[]{:S(2)}) collective-permute-start(bf16[1,128,3072]{2,1,0:T(8,128)(2,1)S(1)} %copy-done.7), channel_id=1, source_target_pairs={{0,16},{16,0},{1,17},{17,1},{2,18},{18,2},{3,19},{19,3},{4,20},{20... | collective-permute-start | bytes 2359304 | tf_op jit(solution)/shard_map/ppermute | solution.py:325
  78.7 32.4 %collective-permute-start.4 = (bf16[4,2,2,128,128]{4,3,2,1,0:T(8,128)(2,1)}, bf16[4,2,2,128,128]{4,3,2,1,0:T(8,128)(2,1)}, u32[]{:S(2)}, u32[]{:S(2)}) collective-permute-start(bf16[4,2,2,128,128]{4,3,2,1,0:T(8,128)(2,1)} %slice.81), channel_id=1, source_target_pairs={{0,4},{4,0},{8,12},{12,8},{1,5},{5,1},{9,13},{13,9},{2,6},{6,2},{1... | collective-permute-start | bytes 1572872 | tf_op jit(solution)/shard_map/ppermute | solution.py:355
  86.1 11.6 %copy-start.2 = (bf16[4,2,3,128,128]{4,3,2,1,0:T(8,128)(2,1)}, bf16[4,2,3,128,128]{4,3,2,1,0:T(8,128)(2,1)S(1)}, u32[]{:S(2)}) copy-start(bf16[4,2,3,128,128]{4,3,2,1,0:T(8,128)(2,1)S(1)} %all-to-all-done.2.refs_2_.refs_5_) | copy-start | bytes 2359300
  86.9 25.8 %collective-permute-start.6 = (bf16[4,2,2,128,128]{4,3,2,1,0:T(8,128)(2,1)}, bf16[4,2,2,128,128]{4,3,2,1,0:T(8,128)(2,1)}, u32[]{:S(2)}, u32[]{:S(2)}) collective-permute-start(bf16[4,2,2,128,128]{4,3,2,1,0:T(8,128)(2,1)} %slice.81), channel_id=1, source_target_pairs={{0,0},{4,8},{8,4},{12,12},{1,1},{5,9},{9,5},{13,13},{2,2},{6,10},{... | collective-permute-start | bytes 1572872 | tf_op jit(solution)/shard_map/ppermute | solution.py:356
  92.3 20.4 %collective-permute-start.5 = (bf16[4,2,2,128,128]{4,3,2,1,0:T(8,128)(2,1)}, bf16[4,2,2,128,128]{4,3,2,1,0:T(8,128)(2,1)}, u32[]{:S(2)}, u32[]{:S(2)}) collective-permute-start(bf16[4,2,2,128,128]{4,3,2,1,0:T(8,128)(2,1)} %slice.82), channel_id=1, source_target_pairs={{0,4},{4,0},{8,12},{12,8},{1,5},{5,1},{9,13},{13,9},{2,6},{6,2},{1... | collective-permute-start | bytes 1572872 | tf_op jit(solution)/shard_map/ppermute | solution.py:355
  92.3 20.4 %collective-permute-start.7 = (bf16[4,2,2,128,128]{4,3,2,1,0:T(8,128)(2,1)}, bf16[4,2,2,128,128]{4,3,2,1,0:T(8,128)(2,1)}, u32[]{:S(2)}, u32[]{:S(2)}) collective-permute-start(bf16[4,2,2,128,128]{4,3,2,1,0:T(8,128)(2,1)} %slice.82), channel_id=1, source_target_pairs={{0,0},{4,8},{8,4},{12,12},{1,1},{5,9},{9,5},{13,13},{2,2},{6,10},{... | collective-permute-start | bytes 1572872 | tf_op jit(solution)/shard_map/ppermute | solution.py:356
  110.6 21.1 %copy-start.4 = (bf16[1,128,3072]{2,1,0:T(8,128)(2,1)}, bf16[1,128,3072]{2,1,0:T(8,128)(2,1)S(1)}, u32[]{:S(2)}) copy-start(bf16[1,128,3072]{2,1,0:T(8,128)(2,1)S(1)} %collective-permute-done.12.refs_5_) | copy-start | bytes 2359300
  110.6 21.3 %collective-permute-start.9 = (bf16[1,128,3072]{2,1,0:T(8,128)(2,1)}, bf16[1,128,3072]{2,1,0:T(8,128)(2,1)S(1)}, u32[]{:S(2)}, u32[]{:S(2)}) collective-permute-start(bf16[1,128,3072]{2,1,0:T(8,128)(2,1)} %collective-permute-done.8.refs_1_), channel_id=1, source_target_pairs={{0,2},{1,3},{2,0},{3,1},{4,6},{5,7},{6,4},{7,5},{8,10},{9,11},{10,... | collective-permute-start | bytes 2359304 | tf_op jit(solution)/shard_map/ppermute | solution.py:370
  111.0 37.1 %collective-permute-start.13 = (bf16[1,128,3072]{2,1,0:T(8,128)(2,1)S(1)}, bf16[1,128,3072]{2,1,0:T(8,128)(2,1)S(1)}, u32[]{:S(2)}, u32[]{:S(2)}) collective-permute-start(bf16[1,128,3072]{2,1,0:T(8,128)(2,1)S(1)} %collective-permute-done.12.refs_5_), channel_id=1, source_target_pairs={{0,2},{1,3},{2,0},{3,1},{4,6},{5,7},{6,4},{7,5},{8,10},{9,11},{10,... | collective-permute-start | bytes 2359304 | tf_op jit(solution)/shard_map/ppermute | solution.py:370
  127.7 31.3 %all-to-all-start.3 = ((bf16[8,2,256,128]{3,2,1,0:T(8,128)(2,1)}), bf16[8,2,256,128]{3,2,1,0:T(8,128)(2,1)S(1)}, u32[]{:S(2)}, u32[]{:S(2)}) async-start(bf16[8,2,256,128]{3,2,1,0:T(8,128)(2,1)} %bitcast.141), calls=%async_computation.3 | async-start | bytes 2097152 | tf_op jit(solution)/shard_map/all_to_all | solution.py:381
  131.3 17.6 %collective-permute-start.10 = (bf16[1,128,3072]{2,1,0:T(8,128)(2,1)}, bf16[1,128,3072]{2,1,0:T(8,128)(2,1)}, u32[]{:S(2)}, u32[]{:S(2)}) collective-permute-start(bf16[1,128,3072]{2,1,0:T(8,128)(2,1)} %collective-permute-done.8.refs_1_), channel_id=1, source_target_pairs={{0,1},{1,0},{2,3},{3,2},{4,5},{5,4},{6,7},{7,6},{8,9},{9,8},{10,11... | collective-permute-start | bytes 2359304 | tf_op jit(solution)/shard_map/ppermute | solution.py:370
  131.7 17.2 %collective-permute-start.14 = (bf16[1,128,3072]{2,1,0:T(8,128)(2,1)S(1)}, bf16[1,128,3072]{2,1,0:T(8,128)(2,1)}, u32[]{:S(2)}, u32[]{:S(2)}) collective-permute-start(bf16[1,128,3072]{2,1,0:T(8,128)(2,1)S(1)} %collective-permute-done.12.refs_5_), channel_id=1, source_target_pairs={{0,1},{1,0},{2,3},{3,2},{4,5},{5,4},{6,7},{7,6},{8,9},{9,8},{10,11... | collective-permute-start | bytes 2359304 | tf_op jit(solution)/shard_map/ppermute | solution.py:370
  131.9 27.1 %copy-start.5 = (bf16[1,128,3072]{2,1,0:T(8,128)(2,1)}, bf16[1,128,3072]{2,1,0:T(8,128)(2,1)S(1)}, u32[]{:S(2)}) copy-start(bf16[1,128,3072]{2,1,0:T(8,128)(2,1)S(1)} %collective-permute-done.9.refs_2_) | copy-start | bytes 2359300
  131.9 27.1 %collective-permute-start.11 = (bf16[1,128,3072]{2,1,0:T(8,128)(2,1)S(1)}, bf16[1,128,3072]{2,1,0:T(8,128)(2,1)}, u32[]{:S(2)}, u32[]{:S(2)}) collective-permute-start(bf16[1,128,3072]{2,1,0:T(8,128)(2,1)S(1)} %collective-permute-done.9.refs_2_), channel_id=1, source_target_pairs={{0,1},{1,0},{2,3},{3,2},{4,5},{5,4},{6,7},{7,6},{8,9},{9,8},{10,11... | collective-permute-start | bytes 2359304 | tf_op jit(solution)/shard_map/ppermute | solution.py:370
  148.1 10.9 %copy-start.6 = (bf16[1,128,3072]{2,1,0:T(8,128)(2,1)}, bf16[1,128,3072]{2,1,0:T(8,128)(2,1)S(1)}, u32[]{:S(2)}) copy-start(bf16[1,128,3072]{2,1,0:T(8,128)(2,1)S(1)} %collective-permute-done.13.refs_6_) | copy-start | bytes 2359300
  148.1 10.9 %collective-permute-start.15 = (bf16[1,128,3072]{2,1,0:T(8,128)(2,1)S(1)}, bf16[1,128,3072]{2,1,0:T(8,128)(2,1)}, u32[]{:S(2)}, u32[]{:S(2)}) collective-permute-start(bf16[1,128,3072]{2,1,0:T(8,128)(2,1)S(1)} %collective-permute-done.13.refs_6_), channel_id=1, source_target_pairs={{0,1},{1,0},{2,3},{3,2},{4,5},{5,4},{6,7},{7,6},{8,9},{9,8},{10,11... | collective-permute-start | bytes 2359304 | tf_op jit(solution)/shard_map/ppermute | solution.py:370
  159.0 1.0 copy-start.1

commit v4 on v3

--- a/solution.py
+++ b/solution.py
@@ -127,7 +127,8 @@
     return result.astype(jnp.bfloat16)
 
 
-REMOTE_CUTS = 2
+MIX_VMEM = 20 << 20
+ATTEND_VMEM = 32 << 20
 
 
 def shift_perm(count, by):
@@ -142,7 +143,7 @@
     queries = refs[:parts]
     rest = refs[parts:]
     if not first:
-        before_ref, rest = rest[0], rest[1:]
+        before_refs, rest = rest[:parts], rest[parts:]
     kv_refs, out_ref = rest[:-1], rest[-1]
     groups = len(kv_refs) // 3
     head_dim = queries[0].shape[-1]
@@ -153,13 +154,12 @@
     both = scalar_ref[0] > 0
 
     def block(start, width, rows):
-        query = jnp.concatenate([ref[0, 0, 0] for ref in queries], axis=0)
+        query = jnp.concatenate([ref[0, 0] for ref in queries], axis=0)
         keys, values = [], []
         for ref in kv_refs[: rows * groups]:
             tokens = ref.shape[3]
-            at = ref.shape[2] - 2
-            key = ref[pl.ds(start, width), 0, at].reshape(width * tokens, head_dim)
-            value = ref[pl.ds(start, width), 0, at + 1].reshape(width * tokens, head_dim)
+            key = ref[pl.ds(start, width), 0, 0].reshape(width * tokens, head_dim)
+            value = ref[pl.ds(start, width), 0, 1].reshape(width * tokens, head_dim)
             keys.append(key)
             values.append(jnp.concatenate([value, jnp.ones_like(value)], axis=1))
         halves = 2
@@ -183,7 +183,8 @@
                     peak = piece if peak is None else jnp.maximum(peak, piece)
             peak = peak.max(axis=1, keepdims=True)
             if not first:
-                old_peak = before_ref[0, 0, here, at_peak:]
+                before = jnp.concatenate([ref[0, 0] for ref in before_refs], axis=0)[here]
+                old_peak = before[:, at_peak:]
                 peak = jnp.maximum(peak, old_peak)
             offset = peak * to_exp2
             summed = None
@@ -196,7 +197,7 @@
                 summed = term if summed is None else summed + term
             if not first:
                 fade = jnp.exp2(old_peak * to_exp2 - offset)
-                summed = summed + before_ref[0, 0, here, :] * fade
+                summed = summed + before * fade
             if last:
                 out = summed[:, :head_dim] / summed[:, head_dim : head_dim + 1]
                 out = out.astype(out_ref.dtype)
@@ -217,48 +218,54 @@
             pl.when(case)(functools.partial(block, start, 2 if at_edge else 3, rows))
 
 
-def attend(valid, streams, before, rows, scale, last, places):
-    columns, heads, _, _, head_dim = streams[0].shape
-    tokens = sum(stream.shape[3] for stream in streams)
+def attend(scalars, queries, states, rows, scale, places=0):
+    columns, heads, _, head_dim = queries[0].shape
+    tokens = sum(query.shape[2] for query in queries)
     keys = sum(kv.shape[3] for kv in rows) * 10 // 4
-    first = before is None
 
     def at_query(h, c, v):
         return (c, h, 0, 0)
 
     def kv_spec(kv):
         return pl.BlockSpec(
-            (columns, 1, kv.shape[2], kv.shape[3], head_dim), lambda h, c, v: (0, h, 0, 0, 0)
-        )
-
-    if last:
+            (columns, 1, 2, kv.shape[3], head_dim), lambda h, c, v: (0, h, 0, 0, 0)
+        )
+
+    if places:
         each = tokens // places
-        out_spec = pl.BlockSpec((places, 1, 1, each, head_dim), lambda h, c, v: (0, c, h, 0, 0))
+        out_spec = pl.BlockSpec(
+            (places, 1, 1, each, head_dim), lambda h, c, v: (0, c, h, 0, 0)
+        )
         out_shape = jax.ShapeDtypeStruct((places, columns, heads, each, head_dim), jnp.bfloat16)
     else:
         out_spec = pl.BlockSpec((1, 1, tokens, 2 * head_dim), at_query)
         out_shape = jax.ShapeDtypeStruct((columns, heads, tokens, 2 * head_dim), jnp.float32)
     pairs = heads * columns * tokens * keys
-    state = [] if first else [before]
+    arrays = [*queries, *states, *rows]
+    in_specs = [
+        pl.BlockSpec((1, 1, query.shape[2], head_dim), at_query) for query in queries
+    ]
+    in_specs += [
+        pl.BlockSpec((1, 1, state.shape[2], 2 * head_dim), at_query) for state in states
+    ]
+    in_specs += [kv_spec(kv) for kv in rows]
     return pl.pallas_call(
-        functools.partial(attention_kernel, len(streams), columns, scale, first, last),
+        functools.partial(
+            attention_kernel, len(queries), columns, scale, not states, bool(places)
+        ),
         grid_spec=pltpu.PrefetchScalarGridSpec(
             num_scalar_prefetch=1,
             grid=(heads, columns),
-            in_specs=[
-                pl.BlockSpec((1, 1, 1, stream.shape[3], head_dim), lambda h, c, v: (c, h, 0, 0, 0))
-                for stream in streams
-            ]
-            + [pl.BlockSpec((1, 1, tokens, 2 * head_dim), at_query) for _ in state]
-            + [kv_spec(kv) for kv in rows],
+            in_specs=in_specs,
             out_specs=out_spec,
         ),
         out_shape=out_shape,
         cost_estimate=pl.CostEstimate(
             flops=pairs * head_dim * 8, bytes_accessed=pairs * 4, transcendentals=pairs
         ),
+        compiler_params=pltpu.CompilerParams(vmem_limit_bytes=ATTEND_VMEM),
         name="tile_attention",
-    )(valid, *streams, *state, *rows)
+    )(scalars, *arrays)
 
 
 def mix_kernel(at_ref, attended_ref, *refs):
@@ -279,7 +286,7 @@
 def mix(order, attended, weights):
     heads, tokens, head_dim = attended.shape
     width = weights[0].shape[-1]
-    step = math.gcd(width, 768)
+    step = math.gcd(width, 1024)
     return pl.pallas_call(
         mix_kernel,
         grid_spec=pltpu.PrefetchScalarGridSpec(
@@ -298,6 +305,7 @@
             bytes_accessed=2 * heads * head_dim * width,
             transcendentals=0,
         ),
+        compiler_params=pltpu.CompilerParams(vmem_limit_bytes=MIX_VMEM),
         name="mix_heads",
     )(order, attended, *weights)
 
@@ -306,87 +314,86 @@
     frame_parts = lax.axis_size("ta")
     row_parts = lax.axis_size("ha")
     col_parts = lax.axis_size("wa")
-    frames = latents.shape[1]
     heads_local, head_dim = input_weight.shape[2:]
     heads_each = heads_local // col_parts
     here, column_at = lax.axis_index("ta"), lax.axis_index("wa")
-    cuts = REMOTE_CUTS if frames % REMOTE_CUTS == 0 else 1
-    step = frames // cuts
-    own = [lax.slice_in_dim(latents, i * step, (i + 1) * step, axis=1) for i in range(cuts)]
     chunks = [latents]
     for by in range(1, frame_parts):
-        for chunk in own:
-            chunks.append(lax.ppermute(chunk, "ta", shift_perm(frame_parts, by)))
+        chunks.append(lax.ppermute(latents, "ta", shift_perm(frame_parts, by)))
 
     fetched = []
     for by in range(1, frame_parts):
-        for k in range(heads_each):
-            share = lax.dynamic_slice_in_dim(output_weight, column_at * heads_each + k, 1, axis=0)
-            share = lax.ppermute(after(share, chunks[-1]), "ta", shift_perm(frame_parts, by))
-            fetched.append((by, k, share))
+        for mask in range(0, col_parts, 2):
+            for k in range(heads_each):
+                head = (column_at ^ mask) * heads_each + k
+                share = lax.dynamic_slice_in_dim(output_weight, head, 1, axis=0)
+                share = lax.ppermute(share, "ta", shift_perm(frame_parts, by))
+                fetched.append((by, mask, k, share))
 
     def project(chunk):
-        projected = jnp.einsum(
+        return jnp.einsum(
             "cfhwd,dsne->cfhwsne", chunk, input_weight, preferred_element_type=jnp.float32
         )
-        normed = jnp.stack(
-            [
-                rms_norm(projected[:, :, :, :, 0], norm_gains[0]),
-                rms_norm(projected[:, :, :, :, 1], norm_gains[1]),
-                projected[:, :, :, :, 2],
-            ]
-        ).astype(jnp.bfloat16)
-        return normed.transpose(5, 0, 1, 2, 3, 4, 6)
-
-    streams = []
+
+    def as_query(projected):
+        query = rms_norm(projected, norm_gains[0]).astype(jnp.bfloat16)
+        query = query.transpose(4, 0, 1, 2, 3, 5)
+        return query.reshape(col_parts, heads_each, -1, head_dim)
+
+    def as_key_value(projected):
+        key = rms_norm(projected[:, :, :, :, 0], norm_gains[1]).astype(jnp.bfloat16)
+        value = projected[:, :, :, :, 1].astype(jnp.bfloat16)
+        key_value = jnp.stack([key, value]).transpose(5, 0, 1, 2, 3, 4, 6)
+        return key_value.reshape(col_parts, heads_each, 2, -1, head_dim)
+
+    queries, keys_values = [], []
     ready = None
     for chunk in chunks:
         if ready is not None:
             chunk = after(chunk, ready)
-        ready = project(chunk)
-        dealt = ready.reshape(col_parts, heads_each, 3, -1, head_dim)
-        streams.append(lax.all_to_all(dealt, "wa", 0, 0))
+        projected = project(chunk)
+        key_value = as_key_value(projected[:, :, :, :, 1:])
+        query = as_query(projected[:, :, :, :, 0])
+        ready = (query, key_value)
+        keys_values.append(lax.all_to_all(key_value, "wa", 0, 0))
+        queries.append(lax.all_to_all(query, "wa", 0, 0))
     pair = [(i, i ^ 1) for i in range(row_parts)]
-    side = [(i, ((i + 1) ^ 1) - 1) for i in range(1, row_parts - 1)]
-    side += [(i, i) for i in {0, row_parts - 1}]
-    paired, beside = [], []
-    for stream in streams:
-        keys_values = stream[:, :, 1:]
-        paired.append(lax.ppermute(keys_values, "ha", pair))
-        beside.append(lax.ppermute(keys_values, "ha", sorted(side)))
+    side = []
+    for i in range(row_parts):
+        for k in range(col_parts):
+            if 0 < i < row_parts - 1:
+                to = (((i + 1) ^ 1) - 1) * col_parts + k
+            else:
+                to = i * col_parts + (k ^ 1)
+            side.append((i * col_parts + k, to))
+    rows = []
+    for key_value in keys_values:
+        paired = lax.ppermute(key_value, "ha", pair)
+        beside = lax.ppermute(key_value, ("ha", "wa"), side)
+        rows.append((key_value, paired, beside))
     height_index = lax.axis_index("ha")
     inside = (height_index > 0) & (height_index < row_parts - 1)
     places = [lax.rem(here + (frame_parts - by), frame_parts) for by in range(frame_parts)]
     scalars = jnp.stack([inside.astype(jnp.int32)] + places)
     scale = 1.0 / math.sqrt(head_dim)
 
-    def spread(block):
-        held = [(0, block)]
-        distance = col_parts // 2
-        while distance:
-            perm = [(i, i ^ distance) for i in range(col_parts)]
-            got = []
-            for mask, part in held:
-                got.append((mask ^ distance, lax.ppermute(part, "wa", perm)))
-            held = held + got
-            distance //= 2
-        return held
-
-    state = attend(scalars, streams, None, [streams[0], paired[0], beside[0]], scale, False, 1)
-    attended = attend(
-        scalars, streams, state, streams[1:] + paired[1:] + beside[1:], scale, True,
-        frame_parts,
-    )
+    states = []
+    for query in queries:
+        states.append(attend(scalars, [query], [], rows[0], scale))
+    last_rows = [row[k] for k in range(3) for row in rows[1:]]
+    attended = attend(scalars, queries, states, last_rows, scale, frame_parts)
     sent = attended.reshape(frame_parts * col_parts, heads_each, -1, head_dim)
     got = lax.all_to_all(sent, ("ta", "wa"), 0, 0)
     got = got.reshape(frame_parts * heads_local, -1, head_dim)
     order = [here * heads_local + k for k in range(heads_local)]
     weights = [output_weight]
-    for by, k, block in fetched:
-        for mask, part in spread(block):
+    swap = [(i, i ^ 1) for i in range(col_parts)]
+    for by, mask, k, share in fetched:
+        other = lax.ppermute(share, "wa", swap)
+        for part, got_mask in ((share, mask), (other, mask ^ 1)):
             weights.append(part)
             order.append(
-                places[by] * heads_local + (column_at ^ mask) * heads_each + k
+                places[by] * heads_local + (column_at ^ got_mask) * heads_each + k
             )
     result = mix(jnp.stack(order).astype(jnp.int32), got, weights)
     return result.reshape(latents.shape)
@@ -405,7 +412,7 @@
         frames = latents.shape[1] * lax.axis_size("ta")
         width = lax.axis_size("wa")
         dealt_heads = input_weight.shape[2] % width == 0 and width & (width - 1) == 0
-        dealt_heads &= lax.axis_size("ha") % 2 == 0
+        dealt_heads &= lax.axis_size("ha") % 2 == 0 and lax.axis_size("ta") > 1 and width > 1
         if latents.shape[0] == 1 and dealt_heads and frames <= 2 * TILE_T:
             return row_plan(latents, input_weight, norm_gains, output_weight)
         return halo_plan(latents, input_weight, norm_gains, output_weight)

time: 172 us -> 160 us (0.930)
  the two profiles are of different devices: /device:TPU:0 before, /device:TPU:16 now
where the time goes in v4:
time: 160 us; the launch traced here: 158 us
  waiting for transfers between devices  44.9 us (28%)
  Pallas kernels  42.3 us (26%)
  starting transfers between devices  29.2 us (18%)
  matrix products  19 us (12%)
  local copies, waits for them, and re-layouts  13.9 us (9%)
  other arithmetic  8.06 us (5%)
    pallas_call x3, Pallas kernels, attend(): pl.pallas_call(functools.partial(attention_kernel, len(queries), columns,...  35.4 us
    dot_general x2, matrix products, project(): jnp.einsum('cfhwd,dsne->cfhwsne', chunk, input_weight, preferred_element_...  19 us
    ppermute x4, waiting for transfers between devices, row_plan(): share = lax.ppermute(share, 'ta', shift_perm(frame_parts, by))  15.1 us
    ppermute x1, waiting for transfers between devices, row_plan(): chunks.append(lax.ppermute(latents, 'ta', shift_perm(frame_parts, by)))  14.5 us
    all_to_all x2, starting transfers between devices, row_plan(): queries.append(lax.all_to_all(query, 'wa', 0, 0))  7.78 us
    all_to_all x2, starting transfers between devices, row_plan(): keys_values.append(lax.all_to_all(key_value, 'wa', 0, 0))  7.03 us
    pallas_call x1, Pallas kernels, mix(): pl.pallas_call(mix_kernel, grid_spec=pltpu.PrefetchScalarGridSpec(num_sca...  6.89 us
    all_to_all x2, waiting for transfers between devices, row_plan(): keys_values.append(lax.all_to_all(key_value, 'wa', 0, 0))  5.99 us
  transfers between devices with their start and end apart: 18, of which 6 were waited for; matrix products, arithmetic and copies ran while one was open for 22% of the time, Pallas kernels for 22%

profile of v4, /device:TPU:16, one launch (start us, length us, event | category | flops | bytes accessed | tf_op | source)
XLA Modules:
  0.0 157.7 jit_solution(3637209098167786641)
XLA Ops:
  0.0 1.5 collective-permute-start
  1.5 9.7 %fusion.7 = f32[1,4,8,8,3,8,128]{6,3,5,4,2,1,0:T(8,128)S(1)} fusion(bf16[3072,3,8,128,1,1]{3,2,1,0,5,4:T(8,128)(2,1)} %bitcast.101, bf16[1,4,8,8,3072]{4,3,2,1,0:T(8,128)(2,1)} %param.4), kind=kOutput, calls=%fused_computation.5 | convolution fusion | flops 4831838208 | bytes 23592960 | tf_op jit(solution)/shard_map/cfhwd,dsne->cfhwsne/dot_general | solution.py:334
  11.3 0.3 fusion.14
  11.7 0.1 fusion.19
  11.8 0.4 fusion.13
  12.1 0.1 maximum_bitcast_fusion
  12.2 0.7 copy-done.4
  12.9 1.3 copy.9
  14.2 3.5 %all-to-all-start.2 = ((bf16[4,2,2,256,128]{4,3,2,1,0:T(8,128)(2,1)}), bf16[4,2,2,256,128]{4,3,2,1,0:T(8,128)(2,1)S(1)}, u32[]{:S(2)}, u32[]{:S(2)}) async-start(bf16[4,2,2,256,128]{4,3,2,1,0:T(8,128)(2,1)} %bitcast.32), calls=%async_computation.2 | async-start | bytes 2097152 | tf_op jit(solution)/shard_map/all_to_all | solution.py:358
  17.7 1.6 %multiply_reduce_fusion.2 = f32[4,8,8,8]{2,3,1,0:T(8,128)S(1)} fusion(f32[1,4,8,8,3,8,128]{6,3,5,4,2,1,0:T(8,128)} %copy-done.4), kind=kLoop, calls=%fused_computation.26 | loop fusion | flops 522240 | bytes 1056768 | tf_op jit(solution)/shard_map/reduce_sum | solution.py:36
  19.3 1.6 fusion.17
  20.9 0.9 copy.7
  21.9 14.5 %collective-permute-done = bf16[1,4,8,8,3072]{4,3,2,1,0:T(8,128)(2,1)S(1)} collective-permute-done((bf16[1,4,8,8,3072]{4,3,2,1,0:T(8,128)(2,1)}, bf16[1,4,8,8,3072]{4,3,2,1,0:T(8,128)(2,1)S(1)}, u32[]{:S(2)}, u32[]{:S(2)}) %collective-permute-start) | collective-permute-done | bytes 1572896 | tf_op jit(solution)/shard_map/ppermute | solution.py:322
  36.3 9.3 %fusion.4 = f32[1,4,8,8,3,8,128]{6,3,5,2,1,4,0:T(8,128)S(1)} fusion(bf16[3072,3,8,128,1,1]{3,2,1,0,5,4:T(8,128)(2,1)} %bitcast.102, bf16[1,4,8,8,3072]{4,3,2,1,0:T(8,128)(2,1)S(1)} %collective-permute-done), kind=kOutput, calls=%fused_computation.4 | convolution fusion | flops 4831838208 | bytes 23592960 | tf_op jit(solution)/shard_map/cfhwd,dsne->cfhwsne/dot_general | solution.py:334
  45.6 0.3 multiply_reduce_fusion
  46.1 0.4 fusion.16
  46.5 0.1 maximum_bitcast_fusion.1
  46.6 0.7 copy-done.3
  47.3 1.3 copy.13
  48.6 3.5 %all-to-all-start.3 = ((bf16[4,2,2,256,128]{4,3,2,1,0:T(8,128)(2,1)}), bf16[4,2,2,256,128]{4,3,2,1,0:T(8,128)(2,1)S(1)}, u32[]{:S(2)}, u32[]{:S(2)}) async-start(bf16[4,2,2,256,128]{4,3,2,1,0:T(8,128)(2,1)} %bitcast.98), calls=%async_computation.3 | async-start | bytes 2097152 | tf_op jit(solution)/shard_map/all_to_all | solution.py:358
  52.1 1.6 %collective-permute-start.1 = (bf16[4,2,2,256,128]{4,3,2,1,0:T(8,128)(2,1)S(1)}, bf16[4,2,2,256,128]{4,3,2,1,0:T(8,128)(2,1)}, u32[]{:S(2)}, u32[]{:S(2)}) collective-permute-start(bf16[4,2,2,256,128]{4,3,2,1,0:T(8,128)(2,1)S(1)} %all-to-all-done.2.refs_1_), channel_id=1, source_target_pairs={{0,4},{4,0},{8,12},{12,8},{1,5},{5,1},{9,13},{13,9},{2,6},{6,2},{1... | collective-permute-start | bytes 3145736 | tf_op jit(solution)/shard_map/ppermute | solution.py:371
  53.7 3.6 %constant_dynamic-slice_fusion = (bf16[1,128,3072]{2,1,0:T(8,128)(2,1)}, bf16[1,128,3072]{2,1,0:T(8,128)(2,1)}, bf16[1,128,3072]{2,1,0:T(8,128)(2,1)}, bf16[1,128,3072]{2,1,0:T(8,128)(2,1)}) fusion(bf16[8,128,3072]{2,1,0:T(8,128)(2,1)} %refs_0_.1, s32[]{:T(128)S(6)} %select_n.15, s32[]{:T(128)S(6)} %select_n.14, s32[]{:T(128)S(6)} %select_n.13, s32[]{:T(128)S(6)} %select_n.12), kind=kLoop, calls=%fused_computation.35 | loop fusion | bytes 6291472 | tf_op jit(solution)/shard_map/dynamic_slice | solution.py:329
  57.4 1.5 collective-permute-start.9
  58.9 1.6 multiply_reduce_fusion.1
  60.5 6.0 %all-to-all-done.3.refs_4_ = bf16[4,2,2,256,128]{4,3,2,1,0:T(8,128)(2,1)S(1)} async-done(((bf16[4,2,2,256,128]{4,3,2,1,0:T(8,128)(2,1)}), bf16[4,2,2,256,128]{4,3,2,1,0:T(8,128)(2,1)S(1)}, u32[]{:S(2)}, u32[]{:S(2)}) %all-to-all-start.3) | async-done | bytes 1048608 | tf_op jit(solution)/shard_map/all_to_all | solution.py:358
  66.5 3.5 %all-to-all-start = ((bf16[4,2,256,128]{3,2,1,0:T(8,128)(2,1)}), bf16[4,2,256,128]{3,2,1,0:T(8,128)(2,1)S(1)}, u32[]{:S(2)}, u32[]{:S(2)}) async-start(bf16[4,2,256,128]{3,2,1,0:T(8,128)(2,1)} %bitcast.99), calls=%async_computation | async-start | bytes 1048576 | tf_op jit(solution)/shard_map/all_to_all | solution.py:359
  70.0 1.6 %collective-permute-start.3 = (bf16[4,2,2,256,128]{4,3,2,1,0:T(8,128)(2,1)S(1)}, bf16[4,2,2,256,128]{4,3,2,1,0:T(8,128)(2,1)}, u32[]{:S(2)}, u32[]{:S(2)}) collective-permute-start(bf16[4,2,2,256,128]{4,3,2,1,0:T(8,128)(2,1)S(1)} %all-to-all-done.3.refs_4_), channel_id=1, source_target_pairs={{0,4},{4,0},{8,12},{12,8},{1,5},{5,1},{9,13},{13,9},{2,6},{6,2},{1... | collective-permute-start | bytes 3145736 | tf_op jit(solution)/shard_map/ppermute | solution.py:371
  71.6 1.6 fusion.18
  73.2 0.9 copy.12
  74.1 4.6 %all-to-all-done.refs_0_ = bf16[4,2,256,128]{3,2,1,0:T(8,128)(2,1)S(1)} async-done(((bf16[4,2,256,128]{3,2,1,0:T(8,128)(2,1)}), bf16[4,2,256,128]{3,2,1,0:T(8,128)(2,1)S(1)}, u32[]{:S(2)}, u32[]{:S(2)}) %all-to-all-start) | async-done | bytes 524320 | tf_op jit(solution)/shard_map/all_to_all | solution.py:359
  78.7 4.3 %all-to-all-start.1 = ((bf16[4,2,256,128]{3,2,1,0:T(8,128)(2,1)}), bf16[4,2,256,128]{3,2,1,0:T(8,128)(2,1)}, u32[]{:S(2)}, u32[]{:S(2)}) async-start(bf16[4,2,256,128]{3,2,1,0:T(8,128)(2,1)} %bitcast.100), calls=%async_computation.1 | async-start | bytes 1048576 | tf_op jit(solution)/shard_map/all_to_all | solution.py:359
  83.1 1.5 collective-permute-start.11
  84.7 0.5 collective-permute-start.5
  85.2 9.8 %tile_attention.3.refs_2_ = f32[4,2,256,256]{3,2,1,0:T(8,128)S(1)} custom-call(s32[3]{0:T(128)S(1)} %pad_add_fusion.scalar_ref, bf16[4,2,256,128]{3,2,1,0:T(8,128)(2,1)S(1)} %all-to-all-done.refs_0_, bf16[4,2,2,256,128]{4,3,2,1,0:T(8,128)(2,1)S(1)} %all-to-all-done.2.refs_1_, bf16[4,2,2,256,128]{4,3,2,1,0:T(8,128)(2,1)} %collective-permute-done.1.refs_2_, ...), custom_call_target="tpu_custom_call" | custom-call | flops 4026531840 | bytes 15728640 | tf_op jit(solution)/shard_map/tile_attention/pallas_call | solution.py:252
  95.0 1.3 copy-done.1
  96.3 9.9 %tile_attention.4.refs_3_ = f32[4,2,256,256]{3,2,1,0:T(8,128)S(1)} custom-call(s32[3]{0:T(128)S(1)} %pad_add_fusion.scalar_ref, bf16[4,2,256,128]{3,2,1,0:T(8,128)(2,1)} %all-to-all-done.1.refs_0_.refs_1_, bf16[4,2,2,256,128]{4,3,2,1,0:T(8,128)(2,1)S(1)} %all-to-all-done.2.refs_1_, bf16[4,2,2,256,128]{4,3,2,1,0:T(8,128)(2,1)} %collective-permute-done.1.refs_2_, ...), custom_call_target="tpu_custom_call" | custom-call | flops 4026531840 | bytes 15728640 | tf_op jit(solution)/shard_map/tile_attention/pallas_call | solution.py:252
  106.2 1.6 %collective-permute-start.7 = (bf16[1,128,3072]{2,1,0:T(8,128)(2,1)}, bf16[1,128,3072]{2,1,0:T(8,128)(2,1)}, u32[]{:S(2)}, u32[]{:S(2)}) collective-permute-start(bf16[1,128,3072]{2,1,0:T(8,128)(2,1)} %get-tuple-element.9), channel_id=1, source_target_pairs={{0,16},{16,0},{1,17},{17,1},{2,18},{18,2},{3,19},{19,3},{4,20},{20... | collective-permute-start | bytes 2359304 | tf_op jit(solution)/shard_map/ppermute | solution.py:330
  107.8 15.8 %tile_attention.5 = bf16[2,4,2,256,128]{4,3,2,1,0:T(8,128)(2,1)} custom-call(s32[3]{0:T(128)S(1)} %pad_add_fusion.scalar_ref, bf16[4,2,256,128]{3,2,1,0:T(8,128)(2,1)S(1)} %all-to-all-done.refs_0_, bf16[4,2,256,128]{3,2,1,0:T(8,128)(2,1)} %all-to-all-done.1.refs_0_.refs_1_, f32[4,2,256,256]{3,2,1,0:T(8,128)S(1)} %copy-done.2, ...), custom_call_target="tpu_custom_call" | custom-call | flops 8053063680 | bytes 31457280 | tf_op jit(solution)/shard_map/tile_attention/pallas_call | solution.py:252
  123.6 3.6 %all-to-all-start.4 = ((bf16[8,2,256,128]{3,2,1,0:T(8,128)(2,1)}), bf16[8,2,256,128]{3,2,1,0:T(8,128)(2,1)S(1)}, u32[]{:S(2)}, u32[]{:S(2)}) async-start(bf16[8,2,256,128]{3,2,1,0:T(8,128)(2,1)} %bitcast.45), calls=%async_computation.4 | async-start | bytes 2097152 | tf_op jit(solution)/shard_map/all_to_all | solution.py:386
  127.2 0.4 collective-permute-start.10
  127.6 0.2 collective-permute-start.12
  127.8 0.3 collective-permute-start.6
  128.1 15.1 %collective-permute-done.7.refs_3_ = bf16[1,128,3072]{2,1,0:T(8,128)(2,1)} collective-permute-done((bf16[1,128,3072]{2,1,0:T(8,128)(2,1)}, bf16[1,128,3072]{2,1,0:T(8,128)(2,1)}, u32[]{:S(2)}, u32[]{:S(2)}) %collective-permute-start.7) | collective-permute-done | bytes 786464 | tf_op jit(solution)/shard_map/ppermute | solution.py:330
  143.2 0.1 stack.92.at_ref
  143.3 2.5 %collective-permute-done.8.refs_4_ = bf16[1,128,3072]{2,1,0:T(8,128)(2,1)} collective-permute-done((bf16[1,128,3072]{2,1,0:T(8,128)(2,1)}, bf16[1,128,3072]{2,1,0:T(8,128)(2,1)}, u32[]{:S(2)}, u32[]{:S(2)}) %collective-permute-start.8) | collective-permute-done | bytes 786464 | tf_op jit(solution)/shard_map/ppermute | solution.py:392
  145.8 2.2 %all-to-all-done.4 = bf16[8,2,256,128]{3,2,1,0:T(8,128)(2,1)S(1)} async-done(((bf16[8,2,256,128]{3,2,1,0:T(8,128)(2,1)}), bf16[8,2,256,128]{3,2,1,0:T(8,128)(2,1)S(1)}, u32[]{:S(2)}, u32[]{:S(2)}) %all-to-all-start.4) | async-done | bytes 1048608 | tf_op jit(solution)/shard_map/all_to_all | solution.py:386
  148.0 2.8 %copy-done = bf16[8,128,3072]{2,1,0:T(8,128)(2,1)S(1)} copy-done((bf16[8,128,3072]{2,1,0:T(8,128)(2,1)S(1)}, bf16[8,128,3072]{2,1,0:T(8,128)(2,1)}, u32[]{:S(2)}) %copy-start) | copy-done | bytes 6291480
  150.8 6.9 %mix_heads.1 = bf16[256,3072]{1,0:T(8,128)(2,1)} custom-call(s32[16]{0:T(128)S(1)} %stack.92.at_ref, bf16[16,256,128]{2,1,0:T(8,128)(2,1)S(1)} %bitcast.97, bf16[8,128,3072]{2,1,0:T(8,128)(2,1)S(1)} %copy-done, bf16[1,128,3072]{2,1,0:T(8,128)(2,1)} %collective-permute-done.5.refs_1_, bf16[1,128,3072]{2,1,0:T(8,128)(2,1)} %collective-permute-done.6.refs_2_, ...), custom_call_target="tpu_custom_call" | custom-call | flops 3221225472 | bytes 12582912 | tf_op jit(solution)/shard_map/mix_heads/pallas_call | solution.py:290
  (30 shorter events, 0.3 us)
Async XLA Ops:
  0.0 36.3 %collective-permute-start = (bf16[1,4,8,8,3072]{4,3,2,1,0:T(8,128)(2,1)}, bf16[1,4,8,8,3072]{4,3,2,1,0:T(8,128)(2,1)S(1)}, u32[]{:S(2)}, u32[]{:S(2)}) collective-permute-start(bf16[1,4,8,8,3072]{4,3,2,1,0:T(8,128)(2,1)} %param.4), channel_id=1, source_target_pairs={{0,16},{16,0},{1,17},{17,1},{2,18},{18,2},{3,19},{19,3},{4,20},{20... | collective-permute-start | bytes 4718600 | tf_op jit(solution)/shard_map/ppermute | solution.py:322
  1.5 9.7 %copy-start.5 = (f32[2,128]{1,0:T(2,128)S(1)}, f32[2,128]{1,0:T(2,128)}, u32[]{:S(2)}) copy-start(f32[2,128]{1,0:T(2,128)} %param.6) | copy-start | bytes 3076
  11.3 1.6 %copy-start.4 = (f32[1,4,8,8,3,8,128]{6,3,5,4,2,1,0:T(8,128)}, f32[1,4,8,8,3,8,128]{6,3,5,4,2,1,0:T(8,128)S(1)}, u32[]{:S(2)}) copy-start(f32[1,4,8,8,3,8,128]{6,3,5,4,2,1,0:T(8,128)S(1)} %fusion.7) | copy-start | bytes 9437188
  14.2 34.4 %all-to-all-start.2 = ((bf16[4,2,2,256,128]{4,3,2,1,0:T(8,128)(2,1)}), bf16[4,2,2,256,128]{4,3,2,1,0:T(8,128)(2,1)S(1)}, u32[]{:S(2)}, u32[]{:S(2)}) async-start(bf16[4,2,2,256,128]{4,3,2,1,0:T(8,128)(2,1)} %bitcast.32), calls=%async_computation.2 | async-start | bytes 2097152 | tf_op jit(solution)/shard_map/all_to_all | solution.py:358
  45.6 1.6 %copy-start.3 = (f32[1,4,8,8,3,8,128]{6,3,5,2,1,4,0:T(8,128)}, f32[1,4,8,8,3,8,128]{6,3,5,2,1,4,0:T(8,128)S(1)}, u32[]{:S(2)}) copy-start(f32[1,4,8,8,3,8,128]{6,3,5,2,1,4,0:T(8,128)S(1)} %fusion.4) | copy-start | bytes 9437188
  48.6 17.9 %all-to-all-start.3 = ((bf16[4,2,2,256,128]{4,3,2,1,0:T(8,128)(2,1)}), bf16[4,2,2,256,128]{4,3,2,1,0:T(8,128)(2,1)S(1)}, u32[]{:S(2)}, u32[]{:S(2)}) async-start(bf16[4,2,2,256,128]{4,3,2,1,0:T(8,128)(2,1)} %bitcast.98), calls=%async_computation.3 | async-start | bytes 2097152 | tf_op jit(solution)/shard_map/all_to_all | solution.py:358
  52.1 31.0 %collective-permute-start.1 = (bf16[4,2,2,256,128]{4,3,2,1,0:T(8,128)(2,1)S(1)}, bf16[4,2,2,256,128]{4,3,2,1,0:T(8,128)(2,1)}, u32[]{:S(2)}, u32[]{:S(2)}) collective-permute-start(bf16[4,2,2,256,128]{4,3,2,1,0:T(8,128)(2,1)S(1)} %all-to-all-done.2.refs_1_), channel_id=1, source_target_pairs={{0,4},{4,0},{8,12},{12,8},{1,5},{5,1},{9,13},{13,9},{2,6},{6,2},{1... | collective-permute-start | bytes 3145736 | tf_op jit(solution)/shard_map/ppermute | solution.py:371
  53.7 30.9 %collective-permute-start.2 = (bf16[4,2,2,256,128]{4,3,2,1,0:T(8,128)(2,1)S(1)}, bf16[4,2,2,256,128]{4,3,2,1,0:T(8,128)(2,1)}, u32[]{:S(2)}, u32[]{:S(2)}) collective-permute-start(bf16[4,2,2,256,128]{4,3,2,1,0:T(8,128)(2,1)S(1)} %all-to-all-done.2.refs_1_), channel_id=1, source_target_pairs={{0,1},{1,0},{2,3},{3,2},{4,8},{5,9},{6,10},{7,11},{8,4},{9,5},{10,... | collective-permute-start | bytes 3145736 | tf_op jit(solution)/shard_map/ppermute | solution.py:372
  57.4 69.8 %collective-permute-start.9 = (bf16[1,128,3072]{2,1,0:T(8,128)(2,1)}, bf16[1,128,3072]{2,1,0:T(8,128)(2,1)S(1)}, u32[]{:S(2)}, u32[]{:S(2)}) collective-permute-start(bf16[1,128,3072]{2,1,0:T(8,128)(2,1)} %get-tuple-element.8), channel_id=1, source_target_pairs={{0,16},{16,0},{1,17},{17,1},{2,18},{18,2},{3,19},{19,3},{4,20},{20... | collective-permute-start | bytes 2359304 | tf_op jit(solution)/shard_map/ppermute | solution.py:330
  66.5 12.3 %all-to-all-start = ((bf16[4,2,256,128]{3,2,1,0:T(8,128)(2,1)}), bf16[4,2,256,128]{3,2,1,0:T(8,128)(2,1)S(1)}, u32[]{:S(2)}, u32[]{:S(2)}) async-start(bf16[4,2,256,128]{3,2,1,0:T(8,128)(2,1)} %bitcast.99), calls=%async_computation | async-start | bytes 1048576 | tf_op jit(solution)/shard_map/all_to_all | solution.py:359
  70.0 36.2 %collective-permute-start.3 = (bf16[4,2,2,256,128]{4,3,2,1,0:T(8,128)(2,1)S(1)}, bf16[4,2,2,256,128]{4,3,2,1,0:T(8,128)(2,1)}, u32[]{:S(2)}, u32[]{:S(2)}) collective-permute-start(bf16[4,2,2,256,128]{4,3,2,1,0:T(8,128)(2,1)S(1)} %all-to-all-done.3.refs_4_), channel_id=1, source_target_pairs={{0,4},{4,0},{8,12},{12,8},{1,5},{5,1},{9,13},{13,9},{2,6},{6,2},{1... | collective-permute-start | bytes 3145736 | tf_op jit(solution)/shard_map/ppermute | solution.py:371
  71.6 36.2 %collective-permute-start.4 = (bf16[4,2,2,256,128]{4,3,2,1,0:T(8,128)(2,1)S(1)}, bf16[4,2,2,256,128]{4,3,2,1,0:T(8,128)(2,1)}, u32[]{:S(2)}, u32[]{:S(2)}) collective-permute-start(bf16[4,2,2,256,128]{4,3,2,1,0:T(8,128)(2,1)S(1)} %all-to-all-done.3.refs_4_), channel_id=1, source_target_pairs={{0,1},{1,0},{2,3},{3,2},{4,8},{5,9},{6,10},{7,11},{8,4},{9,5},{10,... | collective-permute-start | bytes 3145736 | tf_op jit(solution)/shard_map/ppermute | solution.py:372
  78.7 17.6 %all-to-all-start.1 = ((bf16[4,2,256,128]{3,2,1,0:T(8,128)(2,1)}), bf16[4,2,256,128]{3,2,1,0:T(8,128)(2,1)}, u32[]{:S(2)}, u32[]{:S(2)}) async-start(bf16[4,2,256,128]{3,2,1,0:T(8,128)(2,1)} %bitcast.100), calls=%async_computation.1 | async-start | bytes 1048576 | tf_op jit(solution)/shard_map/all_to_all | solution.py:359
  83.1 44.4 %collective-permute-start.11 = (bf16[1,128,3072]{2,1,0:T(8,128)(2,1)}, bf16[1,128,3072]{2,1,0:T(8,128)(2,1)}, u32[]{:S(2)}, u32[]{:S(2)}) collective-permute-start(bf16[1,128,3072]{2,1,0:T(8,128)(2,1)} %get-tuple-element.7), channel_id=1, source_target_pairs={{0,16},{16,0},{1,17},{17,1},{2,18},{18,2},{3,19},{19,3},{4,20},{20... | collective-permute-start | bytes 2359304 | tf_op jit(solution)/shard_map/ppermute | solution.py:330
  84.7 43.1 %collective-permute-start.5 = (bf16[1,128,3072]{2,1,0:T(8,128)(2,1)}, bf16[1,128,3072]{2,1,0:T(8,128)(2,1)}, u32[]{:S(2)}, u32[]{:S(2)}) collective-permute-start(bf16[1,128,3072]{2,1,0:T(8,128)(2,1)} %get-tuple-element.10), channel_id=1, source_target_pairs={{0,16},{16,0},{1,17},{17,1},{2,18},{18,2},{3,19},{19,3},{4,20},{20... | collective-permute-start | bytes 2359304 | tf_op jit(solution)/shard_map/ppermute | solution.py:330
  95.0 1.3 copy-start.1
  96.3 11.5 %copy-start.2 = (f32[4,2,256,256]{3,2,1,0:T(8,128)S(1)}, f32[4,2,256,256]{3,2,1,0:T(8,128)}, u32[]{:S(2)}) copy-start(f32[4,2,256,256]{3,2,1,0:T(8,128)} %copy-done.1) | copy-start | bytes 6291460
  106.2 37.0 %collective-permute-start.7 = (bf16[1,128,3072]{2,1,0:T(8,128)(2,1)}, bf16[1,128,3072]{2,1,0:T(8,128)(2,1)}, u32[]{:S(2)}, u32[]{:S(2)}) collective-permute-start(bf16[1,128,3072]{2,1,0:T(8,128)(2,1)} %get-tuple-element.9), channel_id=1, source_target_pairs={{0,16},{16,0},{1,17},{17,1},{2,18},{18,2},{3,19},{19,3},{4,20},{20... | collective-permute-start | bytes 2359304 | tf_op jit(solution)/shard_map/ppermute | solution.py:330
  123.6 24.4 %all-to-all-start.4 = ((bf16[8,2,256,128]{3,2,1,0:T(8,128)(2,1)}), bf16[8,2,256,128]{3,2,1,0:T(8,128)(2,1)S(1)}, u32[]{:S(2)}, u32[]{:S(2)}) async-start(bf16[8,2,256,128]{3,2,1,0:T(8,128)(2,1)} %bitcast.45), calls=%async_computation.4 | async-start | bytes 2097152 | tf_op jit(solution)/shard_map/all_to_all | solution.py:386
  127.2 16.1 %collective-permute-start.10 = (bf16[1,128,3072]{2,1,0:T(8,128)(2,1)S(1)}, bf16[1,128,3072]{2,1,0:T(8,128)(2,1)S(1)}, u32[]{:S(2)}, u32[]{:S(2)}) collective-permute-start(bf16[1,128,3072]{2,1,0:T(8,128)(2,1)S(1)} %collective-permute-done.9.refs_5_), channel_id=1, source_target_pairs={{0,1},{1,0},{2,3},{3,2},{4,5},{5,4},{6,7},{7,6},{8,9},{9,8},{10,11... | collective-permute-start | bytes 2359304 | tf_op jit(solution)/shard_map/ppermute | solution.py:392
  127.6 15.8 %collective-permute-start.12 = (bf16[1,128,3072]{2,1,0:T(8,128)(2,1)}, bf16[1,128,3072]{2,1,0:T(8,128)(2,1)}, u32[]{:S(2)}, u32[]{:S(2)}) collective-permute-start(bf16[1,128,3072]{2,1,0:T(8,128)(2,1)} %collective-permute-done.11.refs_7_), channel_id=1, source_target_pairs={{0,1},{1,0},{2,3},{3,2},{4,5},{5,4},{6,7},{7,6},{8,9},{9,8},{10,11... | collective-permute-start | bytes 2359304 | tf_op jit(solution)/shard_map/ppermute | solution.py:392
  127.8 15.6 %collective-permute-start.6 = (bf16[1,128,3072]{2,1,0:T(8,128)(2,1)}, bf16[1,128,3072]{2,1,0:T(8,128)(2,1)}, u32[]{:S(2)}, u32[]{:S(2)}) collective-permute-start(bf16[1,128,3072]{2,1,0:T(8,128)(2,1)} %collective-permute-done.5.refs_1_), channel_id=1, source_target_pairs={{0,1},{1,0},{2,3},{3,2},{4,5},{5,4},{6,7},{7,6},{8,9},{9,8},{10,11... | collective-permute-start | bytes 2359304 | tf_op jit(solution)/shard_map/ppermute | solution.py:392
  143.2 2.6 %collective-permute-start.8 = (bf16[1,128,3072]{2,1,0:T(8,128)(2,1)}, bf16[1,128,3072]{2,1,0:T(8,128)(2,1)}, u32[]{:S(2)}, u32[]{:S(2)}) collective-permute-start(bf16[1,128,3072]{2,1,0:T(8,128)(2,1)} %collective-permute-done.7.refs_3_), channel_id=1, source_target_pairs={{0,1},{1,0},{2,3},{3,2},{4,5},{5,4},{6,7},{7,6},{8,9},{9,8},{10,11... | collective-permute-start | bytes 2359304 | tf_op jit(solution)/shard_map/ppermute | solution.py:392
  148.0 2.8 %copy-start = (bf16[8,128,3072]{2,1,0:T(8,128)(2,1)S(1)}, bf16[8,128,3072]{2,1,0:T(8,128)(2,1)}, u32[]{:S(2)}) copy-start(bf16[8,128,3072]{2,1,0:T(8,128)(2,1)} %refs_0_.1) | copy-start | bytes 18874372

commit v5 on v4

--- a/solution.py
+++ b/solution.py
@@ -343,8 +343,11 @@
     def as_key_value(projected):
         key = rms_norm(projected[:, :, :, :, 0], norm_gains[1]).astype(jnp.bfloat16)
         value = projected[:, :, :, :, 1].astype(jnp.bfloat16)
-        key_value = jnp.stack([key, value]).transpose(5, 0, 1, 2, 3, 4, 6)
-        return key_value.reshape(col_parts, heads_each, 2, -1, head_dim)
+        halves = [
+            half.transpose(4, 0, 1, 2, 3, 5).reshape(col_parts, heads_each, 1, -1, head_dim)
+            for half in (key, value)
+        ]
+        return jnp.concatenate(halves, axis=2)
 
     queries, keys_values = [], []
     ready = None
@@ -355,7 +358,8 @@
         key_value = as_key_value(projected[:, :, :, :, 1:])
         query = as_query(projected[:, :, :, :, 0])
         ready = (query, key_value)
-        keys_values.append(lax.all_to_all(key_value, "wa", 0, 0))
+        dealt = lax.all_to_all(key_value, "wa", 0, 0)
+        keys_values.append(after(dealt, query))
         queries.append(lax.all_to_all(query, "wa", 0, 0))
     pair = [(i, i ^ 1) for i in range(row_parts)]
     side = []

time: 160 us -> 169 us (1.056)
  waiting for transfers between devices: 44.9 us -> 60.5 us
  local copies, waits for them, and re-layouts: 13.9 us -> 10.4 us
  other arithmetic: 8.06 us -> 5.03 us
    ppermute x4, waiting for transfers between devices: 15.1 us -> 24.4 us  [row_plan(): share = lax.ppermute(share, 'ta', shift_perm(frame_parts, by))]
    all_to_all x2, waiting for transfers between devices: 5.99 us -> 11.8 us  [row_plan(): dealt = lax.all_to_all(key_value, 'wa', 0, 0)]
    ppermute x1, waiting for transfers between devices: 14.5 us -> 17.7 us  [row_plan(): chunks.append(lax.ppermute(latents, 'ta', shift_perm(frame_parts, by)))]
    all_to_all x2, waiting for transfers between devices: 4.6 us -> 1.97 us  [row_plan(): queries.append(lax.all_to_all(query, 'wa', 0, 0))]
    reduce_sum x4 -> x2, other arithmetic: 3.84 us -> 1.23 us  [rms_norm(): mean_square = jnp.mean(values * values, axis=-1, keepdims=True)]
    concatenate x0 -> x2, other arithmetic: none -> 2.16 us  [as_key_value(): return jnp.concatenate(halves, axis=2)]
    transpose x2 -> x6, local copies, waits for them, and re-layouts: 2.57 us -> 0.71 us  [as_key_value(): half.transpose(4, 0, 1, 2, 3, 5)]
    transpose x4 -> x2, other arithmetic: 3.33 us -> 1.47 us  [as_key_value(): half.transpose(4, 0, 1, 2, 3, 5)]
  transfers between devices with their start and end apart: 18 -> 18, of which waited for: 6 -> 7; matrix products, arithmetic and copies ran while one was open for 22% -> 18% of each run, Pallas kernels for 22% -> 21%
where the time goes in v5:
time: 169 us; the launch traced here: 166 us
  waiting for transfers between devices  60.5 us (36%)
  Pallas kernels  42.3 us (25%)
  starting transfers between devices  28.9 us (17%)
  matrix products  19 us (11%)
  local copies, waits for them, and re-layouts  10.4 us (6%)
  other arithmetic  5.03 us (3%)
    pallas_call x3, Pallas kernels, attend(): pl.pallas_call(functools.partial(attention_kernel, len(queries), columns,...  35.4 us
    ppermute x4, waiting for transfers between devices, row_plan(): share = lax.ppermute(share, 'ta', shift_perm(frame_parts, by))  24.4 us
    dot_general x2, matrix products, project(): jnp.einsum('cfhwd,dsne->cfhwsne', chunk, input_weight, preferred_element_...  19 us
    ppermute x1, waiting for transfers between devices, row_plan(): chunks.append(lax.ppermute(latents, 'ta', shift_perm(frame_parts, by)))  17.7 us
    all_to_all x2, waiting for transfers between devices, row_plan(): dealt = lax.all_to_all(key_value, 'wa', 0, 0)  11.8 us
    all_to_all x2, starting transfers between devices, row_plan(): queries.append(lax.all_to_all(query, 'wa', 0, 0))  7.79 us
    all_to_all x2, starting transfers between devices, row_plan(): dealt = lax.all_to_all(key_value, 'wa', 0, 0)  7.03 us
    pallas_call x1, Pallas kernels, mix(): pl.pallas_call(mix_kernel, grid_spec=pltpu.PrefetchScalarGridSpec(num_sca...  6.89 us
  transfers between devices with their start and end apart: 18, of which 7 were waited for; matrix products, arithmetic and copies ran while one was open for 18% of the time, Pallas kernels for 21%

profile of v5, /device:TPU:16, one launch (start us, length us, event | category | flops | bytes accessed | tf_op | source)
XLA Modules:
  0.0 166.5 jit_solution(4443476522937664018)
XLA Ops:
  0.0 1.5 collective-permute-start
  1.5 9.7 %fusion.7 = f32[1,4,8,8,3,8,128]{6,3,5,4,2,1,0:T(8,128)S(1)} fusion(bf16[3072,3,8,128,1,1]{3,2,1,0,5,4:T(8,128)(2,1)} %bitcast.109, bf16[1,4,8,8,3072]{4,3,2,1,0:T(8,128)(2,1)} %param.4), kind=kOutput, calls=%fused_computation.5 | convolution fusion | flops 4831838208 | bytes 23592960 | tf_op jit(solution)/shard_map/cfhwd,dsne->cfhwsne/dot_general | solution.py:334
  11.3 0.6 multiply_reduce_fusion.2
  12.0 0.7 fusion.13
  12.7 0.1 copy.8
  12.8 0.1 fusion.16
  12.9 0.1 copy.9
  13.1 1.1 pad_maximum_fusion
  14.1 3.5 %all-to-all-start.2 = ((bf16[4,2,2,256,128]{4,3,2,1,0:T(8,128)(2,1)}), bf16[4,2,2,256,128]{4,3,2,1,0:T(8,128)(2,1)S(1)}, u32[]{:S(2)}, u32[]{:S(2)}) async-start(bf16[4,2,2,256,128]{4,3,2,1,0:T(8,128)(2,1)} %pad_maximum_fusion), calls=%async_computation.2 | async-start | bytes 2097152 | tf_op jit(solution)/shard_map/all_to_all | solution.py:361
  17.7 0.9 copy.7
  18.6 17.7 %collective-permute-done = bf16[1,4,8,8,3072]{4,3,2,1,0:T(8,128)(2,1)S(1)} collective-permute-done((bf16[1,4,8,8,3072]{4,3,2,1,0:T(8,128)(2,1)}, bf16[1,4,8,8,3072]{4,3,2,1,0:T(8,128)(2,1)S(1)}, u32[]{:S(2)}, u32[]{:S(2)}) %collective-permute-start) | collective-permute-done | bytes 1572896 | tf_op jit(solution)/shard_map/ppermute | solution.py:322
  36.3 9.3 %fusion.4 = f32[1,4,8,8,3,8,128]{6,3,5,2,1,4,0:T(8,128)S(1)} fusion(bf16[3072,3,8,128,1,1]{3,2,1,0,5,4:T(8,128)(2,1)} %bitcast.110, bf16[1,4,8,8,3072]{4,3,2,1,0:T(8,128)(2,1)S(1)} %collective-permute-done), kind=kOutput, calls=%fused_computation.4 | convolution fusion | flops 4831838208 | bytes 23592960 | tf_op jit(solution)/shard_map/cfhwd,dsne->cfhwsne/dot_general | solution.py:334
  45.6 0.6 multiply_reduce_fusion
  46.3 0.7 fusion.15
  47.0 0.1 copy.13
  47.2 0.1 fusion.17
  47.3 0.1 copy.14
  47.4 1.1 pad_maximum_fusion.1
  48.5 3.5 %all-to-all-start.3 = ((bf16[4,2,2,256,128]{4,3,2,1,0:T(8,128)(2,1)}), bf16[4,2,2,256,128]{4,3,2,1,0:T(8,128)(2,1)S(1)}, u32[]{:S(2)}, u32[]{:S(2)}) async-start(bf16[4,2,2,256,128]{4,3,2,1,0:T(8,128)(2,1)} %pad_maximum_fusion.1), calls=%async_computation.3 | async-start | bytes 2097152 | tf_op jit(solution)/shard_map/all_to_all | solution.py:361
  52.0 1.6 collective-permute-start.1
  53.7 0.9 copy.12
  54.6 11.8 %all-to-all-done.3.refs_4_ = bf16[4,2,2,256,128]{4,3,2,1,0:T(8,128)(2,1)S(1)} async-done(((bf16[4,2,2,256,128]{4,3,2,1,0:T(8,128)(2,1)}), bf16[4,2,2,256,128]{4,3,2,1,0:T(8,128)(2,1)S(1)}, u32[]{:S(2)}, u32[]{:S(2)}) %all-to-all-start.3) | async-done | bytes 1048608 | tf_op jit(solution)/shard_map/all_to_all | solution.py:361
  66.4 3.5 %all-to-all-start = ((bf16[4,2,256,128]{3,2,1,0:T(8,128)(2,1)}), bf16[4,2,256,128]{3,2,1,0:T(8,128)(2,1)S(1)}, u32[]{:S(2)}, u32[]{:S(2)}) async-start(bf16[4,2,256,128]{3,2,1,0:T(8,128)(2,1)} %bitcast.103), calls=%async_computation | async-start | bytes 1048576 | tf_op jit(solution)/shard_map/all_to_all | solution.py:363
  69.9 1.6 collective-permute-start.3
  71.6 0.0 collective-permute-start.4
  71.6 3.6 %constant_dynamic-slice_fusion = (bf16[1,128,3072]{2,1,0:T(8,128)(2,1)}, bf16[1,128,3072]{2,1,0:T(8,128)(2,1)}, bf16[1,128,3072]{2,1,0:T(8,128)(2,1)}, bf16[1,128,3072]{2,1,0:T(8,128)(2,1)}) fusion(bf16[8,128,3072]{2,1,0:T(8,128)(2,1)} %refs_0_.1, s32[]{:T(128)S(6)} %select_n.15, s32[]{:T(128)S(6)} %select_n.14, s32[]{:T(128)S(6)} %select_n.13, s32[]{:T(128)S(6)} %select_n.12), kind=kLoop, calls=%fused_computation.34 | loop fusion | bytes 6291472 | tf_op jit(solution)/shard_map/dynamic_slice | solution.py:329
  75.2 1.5 collective-permute-start.9
  76.7 2.0 %all-to-all-done.refs_0_ = bf16[4,2,256,128]{3,2,1,0:T(8,128)(2,1)S(1)} async-done(((bf16[4,2,256,128]{3,2,1,0:T(8,128)(2,1)}), bf16[4,2,256,128]{3,2,1,0:T(8,128)(2,1)S(1)}, u32[]{:S(2)}, u32[]{:S(2)}) %all-to-all-start) | async-done | bytes 524320 | tf_op jit(solution)/shard_map/all_to_all | solution.py:363
  78.7 4.3 %all-to-all-start.1 = ((bf16[4,2,256,128]{3,2,1,0:T(8,128)(2,1)}), bf16[4,2,256,128]{3,2,1,0:T(8,128)(2,1)}, u32[]{:S(2)}, u32[]{:S(2)}) async-start(bf16[4,2,256,128]{3,2,1,0:T(8,128)(2,1)} %bitcast.104), calls=%async_computation.1 | async-start | bytes 1048576 | tf_op jit(solution)/shard_map/all_to_all | solution.py:363
  83.0 0.1 pad_add_fusion.scalar_ref
  83.1 1.5 collective-permute-start.11
  84.6 0.5 collective-permute-start.5
  85.2 9.8 %tile_attention.3.refs_2_ = f32[4,2,256,256]{3,2,1,0:T(8,128)S(1)} custom-call(s32[3]{0:T(128)S(1)} %pad_add_fusion.scalar_ref, bf16[4,2,256,128]{3,2,1,0:T(8,128)(2,1)S(1)} %all-to-all-done.refs_0_, bf16[4,2,2,256,128]{4,3,2,1,0:T(8,128)(2,1)S(1)} %all-to-all-done.2.refs_1_, bf16[4,2,2,256,128]{4,3,2,1,0:T(8,128)(2,1)} %collective-permute-done.1.refs_2_, ...), custom_call_target="tpu_custom_call" | custom-call | flops 4026531840 | bytes 15728640 | tf_op jit(solution)/shard_map/tile_attention/pallas_call | solution.py:252
  94.9 1.3 copy-done.1
  96.2 0.0 all-to-all-done.1.refs_0_.refs_1_
  96.3 9.9 %tile_attention.4.refs_3_ = f32[4,2,256,256]{3,2,1,0:T(8,128)S(1)} custom-call(s32[3]{0:T(128)S(1)} %pad_add_fusion.scalar_ref, bf16[4,2,256,128]{3,2,1,0:T(8,128)(2,1)} %all-to-all-done.1.refs_0_.refs_1_, bf16[4,2,2,256,128]{4,3,2,1,0:T(8,128)(2,1)S(1)} %all-to-all-done.2.refs_1_, bf16[4,2,2,256,128]{4,3,2,1,0:T(8,128)(2,1)} %collective-permute-done.1.refs_2_, ...), custom_call_target="tpu_custom_call" | custom-call | flops 4026531840 | bytes 15728640 | tf_op jit(solution)/shard_map/tile_attention/pallas_call | solution.py:252
  106.2 1.6 collective-permute-start.7
  107.8 15.8 %tile_attention.5 = bf16[2,4,2,256,128]{4,3,2,1,0:T(8,128)(2,1)} custom-call(s32[3]{0:T(128)S(1)} %pad_add_fusion.scalar_ref, bf16[4,2,256,128]{3,2,1,0:T(8,128)(2,1)S(1)} %all-to-all-done.refs_0_, bf16[4,2,256,128]{3,2,1,0:T(8,128)(2,1)} %all-to-all-done.1.refs_0_.refs_1_, f32[4,2,256,256]{3,2,1,0:T(8,128)S(1)} %copy-done.2, ...), custom_call_target="tpu_custom_call" | custom-call | flops 8053063680 | bytes 31457280 | tf_op jit(solution)/shard_map/tile_attention/pallas_call | solution.py:252
  123.5 3.6 %all-to-all-start.4 = ((bf16[8,2,256,128]{3,2,1,0:T(8,128)(2,1)}), bf16[8,2,256,128]{3,2,1,0:T(8,128)(2,1)S(1)}, u32[]{:S(2)}, u32[]{:S(2)}) async-start(bf16[8,2,256,128]{3,2,1,0:T(8,128)(2,1)} %bitcast.49), calls=%async_computation.4 | async-start | bytes 2097152 | tf_op jit(solution)/shard_map/all_to_all | solution.py:390
  127.1 0.4 collective-permute-start.10
  127.5 0.2 collective-permute-start.12
  127.7 2.0 %collective-permute-done.5.refs_1_ = bf16[1,128,3072]{2,1,0:T(8,128)(2,1)} collective-permute-done((bf16[1,128,3072]{2,1,0:T(8,128)(2,1)}, bf16[1,128,3072]{2,1,0:T(8,128)(2,1)}, u32[]{:S(2)}, u32[]{:S(2)}) %collective-permute-start.5) | collective-permute-done | bytes 786464 | tf_op jit(solution)/shard_map/ppermute | solution.py:330
  129.6 22.5 %collective-permute-done.7.refs_3_ = bf16[1,128,3072]{2,1,0:T(8,128)(2,1)} collective-permute-done((bf16[1,128,3072]{2,1,0:T(8,128)(2,1)}, bf16[1,128,3072]{2,1,0:T(8,128)(2,1)}, u32[]{:S(2)}, u32[]{:S(2)}) %collective-permute-start.7) | collective-permute-done | bytes 786464 | tf_op jit(solution)/shard_map/ppermute | solution.py:330
  152.1 0.1 stack.82.at_ref
  152.2 2.5 %collective-permute-done.8.refs_4_ = bf16[1,128,3072]{2,1,0:T(8,128)(2,1)} collective-permute-done((bf16[1,128,3072]{2,1,0:T(8,128)(2,1)}, bf16[1,128,3072]{2,1,0:T(8,128)(2,1)}, u32[]{:S(2)}, u32[]{:S(2)}) %collective-permute-start.8) | collective-permute-done | bytes 786464 | tf_op jit(solution)/shard_map/ppermute | solution.py:396
  154.7 2.0 %all-to-all-done.4 = bf16[8,2,256,128]{3,2,1,0:T(8,128)(2,1)S(1)} async-done(((bf16[8,2,256,128]{3,2,1,0:T(8,128)(2,1)}), bf16[8,2,256,128]{3,2,1,0:T(8,128)(2,1)S(1)}, u32[]{:S(2)}, u32[]{:S(2)}) %all-to-all-start.4) | async-done | bytes 1048608 | tf_op jit(solution)/shard_map/all_to_all | solution.py:390
  156.8 2.8 %copy-done = bf16[8,128,3072]{2,1,0:T(8,128)(2,1)S(1)} copy-done((bf16[8,128,3072]{2,1,0:T(8,128)(2,1)S(1)}, bf16[8,128,3072]{2,1,0:T(8,128)(2,1)}, u32[]{:S(2)}) %copy-start) | copy-done | bytes 6291480
  159.6 6.9 %mix_heads.1 = bf16[256,3072]{1,0:T(8,128)(2,1)} custom-call(s32[16]{0:T(128)S(1)} %stack.82.at_ref, bf16[16,256,128]{2,1,0:T(8,128)(2,1)S(1)} %bitcast.102, bf16[8,128,3072]{2,1,0:T(8,128)(2,1)S(1)} %copy-done, bf16[1,128,3072]{2,1,0:T(8,128)(2,1)} %collective-permute-done.5.refs_1_, bf16[1,128,3072]{2,1,0:T(8,128)(2,1)} %collective-permute-done.6.refs_2_, ...), custom_call_target="tpu_custom_call" | custom-call | flops 3221225472 | bytes 12582912 | tf_op jit(solution)/shard_map/mix_heads/pallas_call | solution.py:290
  (23 shorter events, 0.1 us)
Async XLA Ops:
  0.0 36.3 %collective-permute-start = (bf16[1,4,8,8,3072]{4,3,2,1,0:T(8,128)(2,1)}, bf16[1,4,8,8,3072]{4,3,2,1,0:T(8,128)(2,1)S(1)}, u32[]{:S(2)}, u32[]{:S(2)}) collective-permute-start(bf16[1,4,8,8,3072]{4,3,2,1,0:T(8,128)(2,1)} %param.4), channel_id=1, source_target_pairs={{0,16},{16,0},{1,17},{17,1},{2,18},{18,2},{3,19},{19,3},{4,20},{20... | collective-permute-start | bytes 4718600 | tf_op jit(solution)/shard_map/ppermute | solution.py:322
  1.5 10.4 %copy-start.3 = (f32[2,128]{1,0:T(2,128)S(1)}, f32[2,128]{1,0:T(2,128)}, u32[]{:S(2)}) copy-start(f32[2,128]{1,0:T(2,128)} %param.6) | copy-start | bytes 3076
  14.1 34.4 %all-to-all-start.2 = ((bf16[4,2,2,256,128]{4,3,2,1,0:T(8,128)(2,1)}), bf16[4,2,2,256,128]{4,3,2,1,0:T(8,128)(2,1)S(1)}, u32[]{:S(2)}, u32[]{:S(2)}) async-start(bf16[4,2,2,256,128]{4,3,2,1,0:T(8,128)(2,1)} %pad_maximum_fusion), calls=%async_computation.2 | async-start | bytes 2097152 | tf_op jit(solution)/shard_map/all_to_all | solution.py:361
  48.5 17.9 %all-to-all-start.3 = ((bf16[4,2,2,256,128]{4,3,2,1,0:T(8,128)(2,1)}), bf16[4,2,2,256,128]{4,3,2,1,0:T(8,128)(2,1)S(1)}, u32[]{:S(2)}, u32[]{:S(2)}) async-start(bf16[4,2,2,256,128]{4,3,2,1,0:T(8,128)(2,1)} %pad_maximum_fusion.1), calls=%async_computation.3 | async-start | bytes 2097152 | tf_op jit(solution)/shard_map/all_to_all | solution.py:361
  52.0 31.1 %collective-permute-start.1 = (bf16[4,2,2,256,128]{4,3,2,1,0:T(8,128)(2,1)S(1)}, bf16[4,2,2,256,128]{4,3,2,1,0:T(8,128)(2,1)}, u32[]{:S(2)}, u32[]{:S(2)}) collective-permute-start(bf16[4,2,2,256,128]{4,3,2,1,0:T(8,128)(2,1)S(1)} %all-to-all-done.2.refs_1_), channel_id=1, source_target_pairs={{0,4},{4,0},{8,12},{12,8},{1,5},{5,1},{9,13},{13,9},{2,6},{6,2},{1... | collective-permute-start | bytes 3145736 | tf_op jit(solution)/shard_map/ppermute | solution.py:375
  53.7 31.0 %collective-permute-start.2 = (bf16[4,2,2,256,128]{4,3,2,1,0:T(8,128)(2,1)S(1)}, bf16[4,2,2,256,128]{4,3,2,1,0:T(8,128)(2,1)}, u32[]{:S(2)}, u32[]{:S(2)}) collective-permute-start(bf16[4,2,2,256,128]{4,3,2,1,0:T(8,128)(2,1)S(1)} %all-to-all-done.2.refs_1_), channel_id=1, source_target_pairs={{0,1},{1,0},{2,3},{3,2},{4,8},{5,9},{6,10},{7,11},{8,4},{9,5},{10,... | collective-permute-start | bytes 3145736 | tf_op jit(solution)/shard_map/ppermute | solution.py:376
  66.4 12.3 %all-to-all-start = ((bf16[4,2,256,128]{3,2,1,0:T(8,128)(2,1)}), bf16[4,2,256,128]{3,2,1,0:T(8,128)(2,1)S(1)}, u32[]{:S(2)}, u32[]{:S(2)}) async-start(bf16[4,2,256,128]{3,2,1,0:T(8,128)(2,1)} %bitcast.103), calls=%async_computation | async-start | bytes 1048576 | tf_op jit(solution)/shard_map/all_to_all | solution.py:363
  69.9 36.2 %collective-permute-start.3 = (bf16[4,2,2,256,128]{4,3,2,1,0:T(8,128)(2,1)S(1)}, bf16[4,2,2,256,128]{4,3,2,1,0:T(8,128)(2,1)}, u32[]{:S(2)}, u32[]{:S(2)}) collective-permute-start(bf16[4,2,2,256,128]{4,3,2,1,0:T(8,128)(2,1)S(1)} %all-to-all-done.3.refs_4_), channel_id=1, source_target_pairs={{0,4},{4,0},{8,12},{12,8},{1,5},{5,1},{9,13},{13,9},{2,6},{6,2},{1... | collective-permute-start | bytes 3145736 | tf_op jit(solution)/shard_map/ppermute | solution.py:375
  71.6 36.2 %collective-permute-start.4 = (bf16[4,2,2,256,128]{4,3,2,1,0:T(8,128)(2,1)S(1)}, bf16[4,2,2,256,128]{4,3,2,1,0:T(8,128)(2,1)}, u32[]{:S(2)}, u32[]{:S(2)}) collective-permute-start(bf16[4,2,2,256,128]{4,3,2,1,0:T(8,128)(2,1)S(1)} %all-to-all-done.3.refs_4_), channel_id=1, source_target_pairs={{0,1},{1,0},{2,3},{3,2},{4,8},{5,9},{6,10},{7,11},{8,4},{9,5},{10,... | collective-permute-start | bytes 3145736 | tf_op jit(solution)/shard_map/ppermute | solution.py:376
  75.2 51.9 %collective-permute-start.9 = (bf16[1,128,3072]{2,1,0:T(8,128)(2,1)}, bf16[1,128,3072]{2,1,0:T(8,128)(2,1)S(1)}, u32[]{:S(2)}, u32[]{:S(2)}) collective-permute-start(bf16[1,128,3072]{2,1,0:T(8,128)(2,1)} %get-tuple-element.16), channel_id=1, source_target_pairs={{0,16},{16,0},{1,17},{17,1},{2,18},{18,2},{3,19},{19,3},{4,20},{20... | collective-permute-start | bytes 2359304 | tf_op jit(solution)/shard_map/ppermute | solution.py:330
  78.7 17.6 %all-to-all-start.1 = ((bf16[4,2,256,128]{3,2,1,0:T(8,128)(2,1)}), bf16[4,2,256,128]{3,2,1,0:T(8,128)(2,1)}, u32[]{:S(2)}, u32[]{:S(2)}) async-start(bf16[4,2,256,128]{3,2,1,0:T(8,128)(2,1)} %bitcast.104), calls=%async_computation.1 | async-start | bytes 1048576 | tf_op jit(solution)/shard_map/all_to_all | solution.py:363
  83.1 44.4 %collective-permute-start.11 = (bf16[1,128,3072]{2,1,0:T(8,128)(2,1)}, bf16[1,128,3072]{2,1,0:T(8,128)(2,1)}, u32[]{:S(2)}, u32[]{:S(2)}) collective-permute-start(bf16[1,128,3072]{2,1,0:T(8,128)(2,1)} %get-tuple-element.15), channel_id=1, source_target_pairs={{0,16},{16,0},{1,17},{17,1},{2,18},{18,2},{3,19},{19,3},{4,20},{20... | collective-permute-start | bytes 2359304 | tf_op jit(solution)/shard_map/ppermute | solution.py:330
  84.6 45.0 %collective-permute-start.5 = (bf16[1,128,3072]{2,1,0:T(8,128)(2,1)}, bf16[1,128,3072]{2,1,0:T(8,128)(2,1)}, u32[]{:S(2)}, u32[]{:S(2)}) collective-permute-start(bf16[1,128,3072]{2,1,0:T(8,128)(2,1)} %get-tuple-element.18), channel_id=1, source_target_pairs={{0,16},{16,0},{1,17},{17,1},{2,18},{18,2},{3,19},{19,3},{4,20},{20... | collective-permute-start | bytes 2359304 | tf_op jit(solution)/shard_map/ppermute | solution.py:330
  94.9 1.3 copy-start.1
  96.3 11.5 %copy-start.2 = (f32[4,2,256,256]{3,2,1,0:T(8,128)S(1)}, f32[4,2,256,256]{3,2,1,0:T(8,128)}, u32[]{:S(2)}) copy-start(f32[4,2,256,256]{3,2,1,0:T(8,128)} %copy-done.1) | copy-start | bytes 6291460
  106.2 45.9 %collective-permute-start.7 = (bf16[1,128,3072]{2,1,0:T(8,128)(2,1)}, bf16[1,128,3072]{2,1,0:T(8,128)(2,1)}, u32[]{:S(2)}, u32[]{:S(2)}) collective-permute-start(bf16[1,128,3072]{2,1,0:T(8,128)(2,1)} %get-tuple-element.17), channel_id=1, source_target_pairs={{0,16},{16,0},{1,17},{17,1},{2,18},{18,2},{3,19},{19,3},{4,20},{20... | collective-permute-start | bytes 2359304 | tf_op jit(solution)/shard_map/ppermute | solution.py:330
  123.5 33.3 %all-to-all-start.4 = ((bf16[8,2,256,128]{3,2,1,0:T(8,128)(2,1)}), bf16[8,2,256,128]{3,2,1,0:T(8,128)(2,1)S(1)}, u32[]{:S(2)}, u32[]{:S(2)}) async-start(bf16[8,2,256,128]{3,2,1,0:T(8,128)(2,1)} %bitcast.49), calls=%async_computation.4 | async-start | bytes 2097152 | tf_op jit(solution)/shard_map/all_to_all | solution.py:390
  127.1 25.1 %collective-permute-start.10 = (bf16[1,128,3072]{2,1,0:T(8,128)(2,1)S(1)}, bf16[1,128,3072]{2,1,0:T(8,128)(2,1)S(1)}, u32[]{:S(2)}, u32[]{:S(2)}) collective-permute-start(bf16[1,128,3072]{2,1,0:T(8,128)(2,1)S(1)} %collective-permute-done.9.refs_5_), channel_id=1, source_target_pairs={{0,1},{1,0},{2,3},{3,2},{4,5},{5,4},{6,7},{7,6},{8,9},{9,8},{10,11... | collective-permute-start | bytes 2359304 | tf_op jit(solution)/shard_map/ppermute | solution.py:396
  127.5 24.7 %collective-permute-start.12 = (bf16[1,128,3072]{2,1,0:T(8,128)(2,1)}, bf16[1,128,3072]{2,1,0:T(8,128)(2,1)}, u32[]{:S(2)}, u32[]{:S(2)}) collective-permute-start(bf16[1,128,3072]{2,1,0:T(8,128)(2,1)} %collective-permute-done.11.refs_7_), channel_id=1, source_target_pairs={{0,1},{1,0},{2,3},{3,2},{4,5},{5,4},{6,7},{7,6},{8,9},{9,8},{10,11... | collective-permute-start | bytes 2359304 | tf_op jit(solution)/shard_map/ppermute | solution.py:396
  129.6 22.6 %collective-permute-start.6 = (bf16[1,128,3072]{2,1,0:T(8,128)(2,1)}, bf16[1,128,3072]{2,1,0:T(8,128)(2,1)}, u32[]{:S(2)}, u32[]{:S(2)}) collective-permute-start(bf16[1,128,3072]{2,1,0:T(8,128)(2,1)} %collective-permute-done.5.refs_1_), channel_id=1, source_target_pairs={{0,1},{1,0},{2,3},{3,2},{4,5},{5,4},{6,7},{7,6},{8,9},{9,8},{10,11... | collective-permute-start | bytes 2359304 | tf_op jit(solution)/shard_map/ppermute | solution.py:396
  152.1 2.6 %collective-permute-start.8 = (bf16[1,128,3072]{2,1,0:T(8,128)(2,1)}, bf16[1,128,3072]{2,1,0:T(8,128)(2,1)}, u32[]{:S(2)}, u32[]{:S(2)}) collective-permute-start(bf16[1,128,3072]{2,1,0:T(8,128)(2,1)} %collective-permute-done.7.refs_3_), channel_id=1, source_target_pairs={{0,1},{1,0},{2,3},{3,2},{4,5},{5,4},{6,7},{7,6},{8,9},{9,8},{10,11... | collective-permute-start | bytes 2359304 | tf_op jit(solution)/shard_map/ppermute | solution.py:396
  156.8 2.8 %copy-start = (bf16[8,128,3072]{2,1,0:T(8,128)(2,1)S(1)}, bf16[8,128,3072]{2,1,0:T(8,128)(2,1)}, u32[]{:S(2)}) copy-start(bf16[8,128,3072]{2,1,0:T(8,128)(2,1)} %refs_0_.1) | copy-start | bytes 18874372

commit v6 on v5

--- a/solution.py
+++ b/solution.py
@@ -127,8 +127,8 @@
     return result.astype(jnp.bfloat16)
 
 
-MIX_VMEM = 20 << 20
-ATTEND_VMEM = 32 << 20
+SMALL_VMEM = 32 << 20
+LARGE_VMEM = 60 << 20
 
 
 def shift_perm(count, by):
@@ -218,17 +218,26 @@
             pl.when(case)(functools.partial(block, start, 2 if at_edge else 3, rows))
 
 
-def attend(scalars, queries, states, rows, scale, places=0):
+def attend(scalars, queries, states, rows, scale, places=0, head=None):
     columns, heads, _, head_dim = queries[0].shape
     tokens = sum(query.shape[2] for query in queries)
     keys = sum(kv.shape[3] for kv in rows) * 10 // 4
+    low, count = (0, heads) if head is None else (head, 1)
+
+    def at_head(h, low):
+        return h + low if low else h
+
+    def at_slot(h, c, v):
+        return (c ^ v[v.shape[0] - 1], at_head(h, low), 0, 0)
 
     def at_query(h, c, v):
-        return (c, h, 0, 0)
+        return (c, at_head(h, low), 0, 0)
 
     def kv_spec(kv):
+        start = low if kv.shape[1] == heads else 0
         return pl.BlockSpec(
-            (columns, 1, 2, kv.shape[3], head_dim), lambda h, c, v: (0, h, 0, 0, 0)
+            (columns, 1, 2, kv.shape[3], head_dim),
+            lambda h, c, v: (0, at_head(h, start), 0, 0, 0),
         )
 
     if places:
@@ -236,14 +245,14 @@
         out_spec = pl.BlockSpec(
             (places, 1, 1, each, head_dim), lambda h, c, v: (0, c, h, 0, 0)
         )
-        out_shape = jax.ShapeDtypeStruct((places, columns, heads, each, head_dim), jnp.bfloat16)
+        out_shape = jax.ShapeDtypeStruct((places, columns, count, each, head_dim), jnp.bfloat16)
     else:
         out_spec = pl.BlockSpec((1, 1, tokens, 2 * head_dim), at_query)
         out_shape = jax.ShapeDtypeStruct((columns, heads, tokens, 2 * head_dim), jnp.float32)
-    pairs = heads * columns * tokens * keys
+    pairs = count * columns * tokens * keys
     arrays = [*queries, *states, *rows]
     in_specs = [
-        pl.BlockSpec((1, 1, query.shape[2], head_dim), at_query) for query in queries
+        pl.BlockSpec((1, 1, query.shape[2], head_dim), at_slot) for query in queries
     ]
     in_specs += [
         pl.BlockSpec((1, 1, state.shape[2], 2 * head_dim), at_query) for state in states
@@ -255,7 +264,7 @@
         ),
         grid_spec=pltpu.PrefetchScalarGridSpec(
             num_scalar_prefetch=1,
-            grid=(heads, columns),
+            grid=(count, columns),
             in_specs=in_specs,
             out_specs=out_spec,
         ),
@@ -263,51 +272,55 @@
         cost_estimate=pl.CostEstimate(
             flops=pairs * head_dim * 8, bytes_accessed=pairs * 4, transcendentals=pairs
         ),
-        compiler_params=pltpu.CompilerParams(vmem_limit_bytes=ATTEND_VMEM),
+        compiler_params=pltpu.CompilerParams(vmem_limit_bytes=LARGE_VMEM if head else SMALL_VMEM),
         name="tile_attention",
     )(scalars, *arrays)
 
 
-def mix_kernel(at_ref, attended_ref, *refs):
-    weight_refs, out_ref = refs[:-1], refs[-1]
-    places = []
-    for ref in weight_refs:
-        for k in range(ref.shape[0]):
-            places.append((ref, k))
-    total = 0.0
+def mix_kernel(final, at_ref, attended_ref, *refs):
+    out_ref = refs[-1]
+    weight_refs = refs[: -2 if final else -1]
+    total = refs[-2][...] if final else 0.0
+    places = [(ref, k) for ref in weight_refs for k in range(ref.shape[0])]
     for at in range(0, len(places), 2):
         pair = places[at : at + 2]
         left = jnp.concatenate([attended_ref[at_ref[at + i]] for i in range(len(pair))], axis=1)
-        right = jnp.concatenate([ref[k] for ref, k in pair], axis=0)
+        right = jnp.concatenate(
+            [ref[k].reshape(ref.shape[-2:]) for ref, k in pair], axis=0
+        )
         total = total + jnp.dot(left, right, preferred_element_type=jnp.float32)
     out_ref[...] = total.astype(out_ref.dtype)
 
 
-def mix(order, attended, weights):
-    heads, tokens, head_dim = attended.shape
-    width = weights[0].shape[-1]
+def mix(order, attended, local, head, weights, total, final):
+    _, tokens, head_dim = attended.shape
+    width = local.shape[-1]
     step = math.gcd(width, 1024)
+    heads = local.shape[0] + len(weights)
+    out_spec = pl.BlockSpec((tokens, step), lambda i, o: (0, i))
+    final_args = [total] if final else []
     return pl.pallas_call(
-        mix_kernel,
+        functools.partial(mix_kernel, final),
         grid_spec=pltpu.PrefetchScalarGridSpec(
             num_scalar_prefetch=1,
             grid=(width // step,),
-            in_specs=[pl.BlockSpec(attended.shape, lambda i, o: (0, 0, 0))]
-            + [
-                pl.BlockSpec((weight.shape[0], head_dim, step), lambda i, o: (0, 0, i))
-                for weight in weights
-            ],
-            out_specs=pl.BlockSpec((tokens, step), lambda i, o: (0, i)),
+            in_specs=[
+                pl.BlockSpec(attended.shape, lambda i, o: (0, 0, 0)),
+                pl.BlockSpec((local.shape[0], 1, head_dim, step), lambda i, o: (0, head, 0, i)),
+            ]
+            + [pl.BlockSpec((1, head_dim, step), lambda i, o: (0, 0, i)) for _ in weights]
+            + [out_spec for _ in final_args],
+            out_specs=out_spec,
         ),
-        out_shape=jax.ShapeDtypeStruct((tokens, width), jnp.bfloat16),
+        out_shape=jax.ShapeDtypeStruct((tokens, width), jnp.bfloat16 if final else jnp.float32),
         cost_estimate=pl.CostEstimate(
             flops=2 * heads * tokens * head_dim * width,
             bytes_accessed=2 * heads * head_dim * width,
             transcendentals=0,
         ),
-        compiler_params=pltpu.CompilerParams(vmem_limit_bytes=MIX_VMEM),
+        compiler_params=pltpu.CompilerParams(vmem_limit_bytes=LARGE_VMEM),
         name="mix_heads",
-    )(order, attended, *weights)
+    )(order, attended, local, *weights, *final_args)
 
 
 def row_plan(latents, input_weight, norm_gains, output_weight):
@@ -325,10 +338,18 @@
     for by in range(1, frame_parts):
         for mask in range(0, col_parts, 2):
             for k in range(heads_each):
+                if mask and (mask, k) == (col_parts - 2, heads_each - 1):
+                    continue
                 head = (column_at ^ mask) * heads_each + k
                 share = lax.dynamic_slice_in_dim(output_weight, head, 1, axis=0)
                 share = lax.ppermute(share, "ta", shift_perm(frame_parts, by))
                 fetched.append((by, mask, k, share))
+
+    for by, mask, k, share in list(fetched):
+        if col_parts > 2 and (mask, k) == (0, heads_each - 1):
+            mask = col_parts - 2
+            share = lax.ppermute(share, "wa", [(i, i ^ mask) for i in range(col_parts)])
+            fetched.append((by, mask, k, share))
 
     def project(chunk):
         return jnp.einsum(
@@ -360,7 +381,11 @@
         ready = (query, key_value)
         dealt = lax.all_to_all(key_value, "wa", 0, 0)
         keys_values.append(after(dealt, query))
-        queries.append(lax.all_to_all(query, "wa", 0, 0))
+        slots = [lax.dynamic_index_in_dim(query, column_at, 0, keepdims=False)]
+        for by in range(1, col_parts):
+            block = lax.dynamic_index_in_dim(query, column_at ^ by, 0, keepdims=False)
+            slots.append(lax.ppermute(block, "wa", [(i, i ^ by) for i in range(col_parts)]))
+        queries.append(jnp.stack(slots))
     pair = [(i, i ^ 1) for i in range(row_parts)]
     side = []
     for i in range(row_parts):
@@ -371,36 +396,50 @@
                 to = i * col_parts + (k ^ 1)
             side.append((i * col_parts + k, to))
     rows = []
-    for key_value in keys_values:
-        paired = lax.ppermute(key_value, "ha", pair)
-        beside = lax.ppermute(key_value, ("ha", "wa"), side)
+    for at, key_value in enumerate(keys_values):
+        shares = [key_value]
+        if at:
+            shares = [key_value[:, head : head + 1] for head in range(heads_each)]
+        paired, beside = [], []
+        for head, share in enumerate(shares):
+            paired.append(lax.ppermute(share, "ha", pair))
+            beside.append(lax.ppermute(share, ("ha", "wa"), side))
         rows.append((key_value, paired, beside))
     height_index = lax.axis_index("ha")
     inside = (height_index > 0) & (height_index < row_parts - 1)
     places = [lax.rem(here + (frame_parts - by), frame_parts) for by in range(frame_parts)]
-    scalars = jnp.stack([inside.astype(jnp.int32)] + places)
+    scalars = jnp.stack([inside.astype(jnp.int32)] + places + [column_at])
     scale = 1.0 / math.sqrt(head_dim)
 
+    first_rows = [rows[0][0], *rows[0][1], *rows[0][2]]
     states = []
     for query in queries:
-        states.append(attend(scalars, [query], [], rows[0], scale))
-    last_rows = [row[k] for k in range(3) for row in rows[1:]]
-    attended = attend(scalars, queries, states, last_rows, scale, frame_parts)
-    sent = attended.reshape(frame_parts * col_parts, heads_each, -1, head_dim)
-    got = lax.all_to_all(sent, ("ta", "wa"), 0, 0)
-    got = got.reshape(frame_parts * heads_local, -1, head_dim)
-    order = [here * heads_local + k for k in range(heads_local)]
-    weights = [output_weight]
+        states.append(attend(scalars, [query], [], first_rows, scale))
+
     swap = [(i, i ^ 1) for i in range(col_parts)]
+    spread = []
     for by, mask, k, share in fetched:
         other = lax.ppermute(share, "wa", swap)
-        for part, got_mask in ((share, mask), (other, mask ^ 1)):
-            weights.append(part)
-            order.append(
-                places[by] * heads_local + (column_at ^ got_mask) * heads_each + k
-            )
-    result = mix(jnp.stack(order).astype(jnp.int32), got, weights)
-    return result.reshape(latents.shape)
+        spread.append((by, mask, k, share))
+        spread.append((by, mask ^ 1, k, other))
+    local = output_weight.reshape(col_parts, heads_each, head_dim, -1)
+    total = None
+    for head in range(heads_each):
+        last_rows = [row[0] for row in rows[1:]]
+        last_rows += [row[1][head] for row in rows[1:]] + [row[2][head] for row in rows[1:]]
+        attended = attend(scalars, queries, states, last_rows, scale, frame_parts, head)
+        sent = attended.reshape(frame_parts * col_parts, -1, head_dim)
+        got = lax.all_to_all(sent, ("ta", "wa"), 0, 0, tiled=True)
+        got = got.reshape(frame_parts * col_parts, -1, head_dim)
+        order = [here * col_parts + k for k in range(col_parts)]
+        weights = []
+        for by, mask, k, part in spread:
+            if k == head:
+                weights.append(part)
+                order.append(places[by] * col_parts + (column_at ^ mask))
+        order = jnp.stack(order).astype(jnp.int32)
+        total = mix(order, got, local, head, weights, total, head == heads_each - 1)
+    return total.reshape(latents.shape)
 
 
 def solution(mesh):

time: 169 us -> 172 us (1.018)
  Pallas kernels: 42.3 us -> 51.4 us
  waiting for transfers between devices: 60.5 us -> 52.4 us
  starting transfers between devices: 28.9 us -> 32.4 us
  local copies, waits for them, and re-layouts: 10.4 us -> 7.36 us
  other arithmetic: 5.03 us -> 7.06 us
    ppermute x4 -> x13, waiting for transfers between devices: 0.01 us -> 18.9 us  [the longest x6 18.9 us: row_plan(): lax.ppermute(block, 'wa', [(i, i ^ by) for i in range(col_parts)])]
    all_to_all x2, waiting for transfers between devices: 11.8 us -> 0.01 us  [row_plan(): dealt = lax.all_to_all(key_value, 'wa', 0, 0)]
    ppermute x4 -> x3, waiting for transfers between devices: 24.4 us -> 15.4 us  [row_plan(): share = lax.ppermute(share, 'ta', shift_perm(frame_parts, by))]
    ppermute x4 -> x13, starting transfers between devices: 3.28 us -> 11.4 us  [the longest x6 5.12 us: row_plan(): lax.ppermute(block, 'wa', [(i, i ^ by) for i in range(col_parts)])]
    pallas_call x1 -> x2, Pallas kernels: 6.89 us -> 14.3 us  [mix(): pl.pallas_call(functools.partial(mix_kernel, final), grid_spec=pltpu.Pref...]
    all_to_all x3 -> x2, starting transfers between devices: 11.3 us -> 7.55 us  [row_plan(): got = lax.all_to_all(sent, ('ta', 'wa'), 0, 0, tiled=True)]
    unnamed x8 -> x26, local copies, waits for them, and re-layouts: 4.11 us -> 0.84 us
    ppermute x4, waiting for transfers between devices: 2.51 us -> 0.01 us  [row_plan(): other = lax.ppermute(share, 'wa', swap)]
  transfers between devices with their start and end apart: 18 -> 25, of which waited for: 7 -> 8; matrix products, arithmetic and copies ran while one was open for 18% -> 19% of each run, Pallas kernels for 21% -> 26%
where the time goes in v6:
time: 172 us; the launch traced here: 170 us
  waiting for transfers between devices  52.4 us (30%)
  Pallas kernels  51.4 us (30%)
  starting transfers between devices  32.4 us (19%)
  matrix products  19.4 us (11%)
  local copies, waits for them, and re-layouts  7.36 us (4%)
  other arithmetic  7.06 us (4%)
    pallas_call x4, Pallas kernels, attend(): pl.pallas_call(functools.partial(attention_kernel, len(queries), columns,...  37.1 us
    dot_general x2, matrix products, project(): jnp.einsum('cfhwd,dsne->cfhwsne', chunk, input_weight, preferred_element_...  19.4 us
    ppermute x6, waiting for transfers between devices, row_plan(): lax.ppermute(block, 'wa', [(i, i ^ by) for i in range(col_parts)])  18.9 us
    ppermute x1, waiting for transfers between devices, row_plan(): chunks.append(lax.ppermute(latents, 'ta', shift_perm(frame_parts, by)))  16.1 us
    ppermute x3, waiting for transfers between devices, row_plan(): share = lax.ppermute(share, 'ta', shift_perm(frame_parts, by))  15.4 us
    pallas_call x2, Pallas kernels, mix(): pl.pallas_call(functools.partial(mix_kernel, final), grid_spec=pltpu.Pref...  14.3 us
    all_to_all x2, starting transfers between devices, row_plan(): got = lax.all_to_all(sent, ('ta', 'wa'), 0, 0, tiled=True)  7.55 us
    all_to_all x2, starting transfers between devices, row_plan(): dealt = lax.all_to_all(key_value, 'wa', 0, 0)  7.21 us
  transfers between devices with their start and end apart: 25, of which 8 were waited for; matrix products, arithmetic and copies ran while one was open for 19% of the time, Pallas kernels for 26%

profile of v6, /device:TPU:16, one launch (start us, length us, event | category | flops | bytes accessed | tf_op | source)
XLA Modules:
  0.0 170.4 jit_solution(4174678497050828976)
XLA Ops:
  0.0 1.5 collective-permute-start.3
  1.5 9.7 %fusion.7 = f32[1,4,8,8,3,8,128]{6,3,5,4,2,1,0:T(8,128)S(1)} fusion(bf16[3072,3,8,128,1,1]{3,2,1,0,5,4:T(8,128)(2,1)} %bitcast.127, bf16[1,4,8,8,3072]{4,3,2,1,0:T(8,128)(2,1)} %param.4), kind=kOutput, calls=%fused_computation.5 | convolution fusion | flops 4831838208 | bytes 23592960 | tf_op jit(solution)/shard_map/cfhwd,dsne->cfhwsne/dot_general | solution.py:355
  11.5 0.6 multiply_reduce_fusion.2
  12.2 0.7 fusion.13
  13.1 1.1 pad_maximum_fusion
  14.2 3.5 %all-to-all-start = ((bf16[4,2,2,256,128]{4,3,2,1,0:T(8,128)(2,1)}), bf16[4,2,2,256,128]{4,3,2,1,0:T(8,128)(2,1)S(1)}, u32[]{:S(2)}, u32[]{:S(2)}) async-start(bf16[4,2,2,256,128]{4,3,2,1,0:T(8,128)(2,1)} %pad_maximum_fusion), calls=%async_computation | async-start | bytes 2097152 | tf_op jit(solution)/shard_map/all_to_all | solution.py:382
  17.7 3.1 %constant_dynamic-slice_fusion = (bf16[1,128,3072]{2,1,0:T(8,128)(2,1)}, bf16[1,128,3072]{2,1,0:T(8,128)(2,1)}, bf16[1,128,3072]{2,1,0:T(8,128)(2,1)}) fusion(bf16[8,128,3072]{2,1,0:T(8,128)(2,1)} %param.7, s32[]{:T(128)S(6)} %select_n.32, s32[]{:T(128)S(6)} %select_n.30, s32[]{:T(128)S(6)} %select_n.31), kind=kLoop, calls=%fused_computation.42 | loop fusion | bytes 4718604 | tf_op jit(solution)/shard_map/dynamic_slice | solution.py:344
  20.8 0.5 collective-permute-start.11
  21.5 16.1 %collective-permute-done.3 = bf16[1,4,8,8,3072]{4,3,2,1,0:T(8,128)(2,1)} collective-permute-done((bf16[1,4,8,8,3072]{4,3,2,1,0:T(8,128)(2,1)}, bf16[1,4,8,8,3072]{4,3,2,1,0:T(8,128)(2,1)}, u32[]{:S(2)}, u32[]{:S(2)}) %collective-permute-start.3) | collective-permute-done | bytes 1572896 | tf_op jit(solution)/shard_map/ppermute | solution.py:335
  37.6 9.7 %fusion.4 = f32[1,4,8,8,3,8,128]{6,3,5,2,1,4,0:T(8,128)S(1)} fusion(bf16[3072,3,8,128,1,1]{3,2,1,0,5,4:T(8,128)(2,1)} %bitcast.128, bf16[1,4,8,8,3072]{4,3,2,1,0:T(8,128)(2,1)} %collective-permute-done.3), kind=kOutput, calls=%fused_computation.4 | convolution fusion | flops 4831838208 | bytes 23592960 | tf_op jit(solution)/shard_map/cfhwd,dsne->cfhwsne/dot_general | solution.py:355
  47.3 0.6 multiply_reduce_fusion
  48.2 0.7 fusion.15
  49.1 1.1 pad_maximum_fusion.1
  50.2 3.7 %all-to-all-start.1 = ((bf16[4,2,2,256,128]{4,3,2,1,0:T(8,128)(2,1)}), bf16[4,2,2,256,128]{4,3,2,1,0:T(8,128)(2,1)S(1)}, u32[]{:S(2)}, u32[]{:S(2)}) async-start(bf16[4,2,2,256,128]{4,3,2,1,0:T(8,128)(2,1)} %pad_maximum_fusion.1), calls=%async_computation.1 | async-start | bytes 2097152 | tf_op jit(solution)/shard_map/all_to_all | solution.py:382
  53.9 1.6 collective-permute-start.7
  55.5 1.3 collective-permute-start.2
  56.8 0.6 collective-permute-start.1
  57.4 12.9 %collective-permute-done.2 = bf16[2,256,128]{2,1,0:T(8,128)(2,1)S(1)} collective-permute-done((bf16[2,256,128]{2,1,0:T(8,128)(2,1)S(1)}, bf16[2,256,128]{2,1,0:T(8,128)(2,1)S(1)}, u32[]{:S(2)}, u32[]{:S(2)}) %collective-permute-start.2) | collective-permute-done | bytes 131104 | tf_op jit(solution)/shard_map/ppermute | solution.py:387
  70.3 1.4 collective-permute-start
  71.8 0.7 constant_dynamic-slice_fusion.3
  72.6 1.2 collective-permute-done.1
  73.8 1.2 collective-permute-start.5
  75.0 0.7 collective-permute-start.4
  75.7 4.1 %collective-permute-done.6 = bf16[2,256,128]{2,1,0:T(8,128)(2,1)S(1)} collective-permute-done((bf16[2,256,128]{2,1,0:T(8,128)(2,1)}, bf16[2,256,128]{2,1,0:T(8,128)(2,1)S(1)}, u32[]{:S(2)}, u32[]{:S(2)}) %collective-permute-start.6) | collective-permute-done | bytes 131104 | tf_op jit(solution)/shard_map/ppermute | solution.py:387
  79.8 1.5 collective-permute-start.17
  81.3 0.7 collective-permute-done.5
  82.1 1.5 collective-permute-start.19
  83.6 1.0 pad_maximum_fusion.2.refs_0_
  84.6 1.0 collective-permute-start.13
  85.7 1.0 pad_maximum_fusion.3.refs_0_.refs_1_
  86.7 1.0 fusion.18
  87.7 1.6 collective-permute-start.15
  89.3 9.8 %tile_attention.4.refs_2_ = f32[4,2,256,256]{3,2,1,0:T(8,128)S(1)} custom-call(s32[4]{0:T(128)S(1)} %pad_add_fusion.scalar_ref, bf16[4,2,256,128]{3,2,1,0:T(8,128)(2,1)S(1)} %pad_maximum_fusion.2.refs_0_, bf16[4,2,2,256,128]{4,3,2,1,0:T(8,128)(2,1)S(1)} %all-to-all-done.refs_1_, bf16[4,2,2,256,128]{4,3,2,1,0:T(8,128)(2,1)} %collective-permute-done.7.refs_2_, ...), custom_call_target="tpu_custom_call" | custom-call | flops 4026531840 | bytes 15728640 | tf_op jit(solution)/shard_map/tile_attention/pallas_call | solution.py:261
  99.1 1.5 collective-permute-done.17.refs_1_
  100.5 1.6 collective-permute-start.9
  102.1 14.0 %collective-permute-done.19.refs_3_ = bf16[1,128,3072]{2,1,0:T(8,128)(2,1)} collective-permute-done((bf16[1,128,3072]{2,1,0:T(8,128)(2,1)}, bf16[1,128,3072]{2,1,0:T(8,128)(2,1)}, u32[]{:S(2)}, u32[]{:S(2)}) %collective-permute-start.19) | collective-permute-done | bytes 786464 | tf_op jit(solution)/shard_map/ppermute | solution.py:345
  116.1 0.4 collective-permute-start.10
  116.5 9.8 %tile_attention.5.refs_3_ = f32[4,2,256,256]{3,2,1,0:T(8,128)S(1)} custom-call(s32[4]{0:T(128)S(1)} %pad_add_fusion.scalar_ref, bf16[4,2,256,128]{3,2,1,0:T(8,128)(2,1)S(1)} %pad_maximum_fusion.3.refs_0_.refs_1_, bf16[4,2,2,256,128]{4,3,2,1,0:T(8,128)(2,1)S(1)} %all-to-all-done.refs_1_, bf16[4,2,2,256,128]{4,3,2,1,0:T(8,128)(2,1)} %collective-permute-done.7.refs_2_, ...), custom_call_target="tpu_custom_call" | custom-call | flops 4026531840 | bytes 15728640 | tf_op jit(solution)/shard_map/tile_attention/pallas_call | solution.py:261
  126.4 0.5 collective-permute-start.20
  126.9 8.0 %tile_attention.7 = bf16[2,4,1,256,128]{4,3,2,1,0:T(8,128)(2,1)} custom-call(s32[4]{0:T(128)S(1)} %pad_add_fusion.scalar_ref, bf16[4,2,256,128]{3,2,1,0:T(8,128)(2,1)S(1)} %pad_maximum_fusion.2.refs_0_, bf16[4,2,256,128]{3,2,1,0:T(8,128)(2,1)S(1)} %pad_maximum_fusion.3.refs_0_.refs_1_, f32[4,2,256,256]{3,2,1,0:T(8,128)S(1)} %tile_attention.4.refs_2_, ...), custom_call_target="tpu_custom_call" | custom-call | flops 4026531840 | bytes 15728640 | tf_op jit(solution)/shard_map/tile_attention/pallas_call | solution.py:261
  134.9 3.5 %all-to-all-start.3 = ((bf16[8,256,128]{2,1,0:T(8,128)(2,1)}), bf16[8,256,128]{2,1,0:T(8,128)(2,1)S(1)}, u32[]{:S(2)}, u32[]{:S(2)}) async-start(bf16[8,256,128]{2,1,0:T(8,128)(2,1)} %bitcast.56), calls=%async_computation.3 | async-start | bytes 1048576 | tf_op jit(solution)/shard_map/all_to_all | solution.py:432
  139.0 9.6 %tile_attention.6 = bf16[2,4,1,256,128]{4,3,2,1,0:T(8,128)(2,1)} custom-call(s32[4]{0:T(128)} %copy-done.3, bf16[4,2,256,128]{3,2,1,0:T(8,128)(2,1)} %copy-done.1, bf16[4,2,256,128]{3,2,1,0:T(8,128)(2,1)} %copy-done.2, f32[4,2,256,256]{3,2,1,0:T(8,128)} %copy-done.4, f32[4,2,256,256]{3,2,1,0:T(8,128)} %copy-done.5, bf16[4,2,2,256,128]{4,3,2,1,0:T(8,128)(2,1)} %copy-done, ...), custom_call_target="tpu_custom_call" | custom-call | flops 4026531840 | bytes 15728640 | tf_op jit(solution)/shard_map/tile_attention/pallas_call | solution.py:261
  148.6 4.1 %all-to-all-start.2 = ((bf16[8,256,128]{2,1,0:T(8,128)(2,1)}), bf16[8,256,128]{2,1,0:T(8,128)(2,1)S(1)}, u32[]{:S(2)}, u32[]{:S(2)}) async-start(bf16[8,256,128]{2,1,0:T(8,128)(2,1)} %bitcast.122), calls=%async_computation.2 | async-start | bytes 1048576 | tf_op jit(solution)/shard_map/all_to_all | solution.py:432
  152.7 0.7 stack.88.at_ref
  153.4 7.1 %mix_heads.2.refs_5_ = f32[256,3072]{1,0:T(8,128)} custom-call(s32[8]{0:T(128)} %stack.88.at_ref, bf16[8,256,128]{2,1,0:T(8,128)(2,1)} %copy-done.6, bf16[4,2,128,3072]{3,2,1,0:T(8,128)(2,1)} %bitcast.114, bf16[1,128,3072]{2,1,0:T(8,128)(2,1)} %collective-permute-done.17.refs_1_, bf16[1,128,3072]{2,1,0:T(8,128)(2,1)} %collective-permute-done.18.refs_2_, ...), custom_call_target="tpu_custom_call" | custom-call | flops 1610612736 | bytes 6291456 | tf_op jit(solution)/shard_map/mix_heads/pallas_call | solution.py:302
  160.5 1.9 %all-to-all-done.2.attended_ref = bf16[8,256,128]{2,1,0:T(8,128)(2,1)S(1)} async-done(((bf16[8,256,128]{2,1,0:T(8,128)(2,1)}), bf16[8,256,128]{2,1,0:T(8,128)(2,1)S(1)}, u32[]{:S(2)}, u32[]{:S(2)}) %all-to-all-start.2) | async-done | bytes 524320 | tf_op jit(solution)/shard_map/all_to_all | solution.py:432
  162.4 0.8 copy-done.7
  163.2 7.2 %mix_heads.3 = bf16[256,3072]{1,0:T(8,128)(2,1)} custom-call(s32[8]{0:T(128)} %stack.88.at_ref, bf16[8,256,128]{2,1,0:T(8,128)(2,1)} %copy-done.7, bf16[4,2,128,3072]{3,2,1,0:T(8,128)(2,1)} %bitcast.115, bf16[1,128,3072]{2,1,0:T(8,128)(2,1)} %collective-permute-done.11.refs_1_, bf16[1,128,3072]{2,1,0:T(8,128)(2,1)} %copy-done.8, ...), custom_call_target="tpu_custom_call" | custom-call | flops 1610612736 | bytes 6291456 | tf_op jit(solution)/shard_map/mix_heads/pallas_call | solution.py:302
  (62 shorter events, 1.9 us)
Async XLA Ops:
  0.0 37.6 %collective-permute-start.3 = (bf16[1,4,8,8,3072]{4,3,2,1,0:T(8,128)(2,1)}, bf16[1,4,8,8,3072]{4,3,2,1,0:T(8,128)(2,1)}, u32[]{:S(2)}, u32[]{:S(2)}) collective-permute-start(bf16[1,4,8,8,3072]{4,3,2,1,0:T(8,128)(2,1)} %param.4), channel_id=1, source_target_pairs={{0,16},{16,0},{1,17},{17,1},{2,18},{18,2},{3,19},{19,3},{4,20},{20... | collective-permute-start | bytes 4718600 | tf_op jit(solution)/shard_map/ppermute | solution.py:335
  11.3 0.9 copy-start.12
  14.2 36.0 %all-to-all-start = ((bf16[4,2,2,256,128]{4,3,2,1,0:T(8,128)(2,1)}), bf16[4,2,2,256,128]{4,3,2,1,0:T(8,128)(2,1)S(1)}, u32[]{:S(2)}, u32[]{:S(2)}) async-start(bf16[4,2,2,256,128]{4,3,2,1,0:T(8,128)(2,1)} %pad_maximum_fusion), calls=%async_computation | async-start | bytes 2097152 | tf_op jit(solution)/shard_map/all_to_all | solution.py:382
  20.8 54.1 %collective-permute-start.11 = (bf16[1,128,3072]{2,1,0:T(8,128)(2,1)}, bf16[1,128,3072]{2,1,0:T(8,128)(2,1)}, u32[]{:S(2)}, u32[]{:S(2)}) collective-permute-start(bf16[1,128,3072]{2,1,0:T(8,128)(2,1)} %get-tuple-element.16), channel_id=1, source_target_pairs={{0,16},{16,0},{1,17},{17,1},{2,18},{18,2},{3,19},{19,3},{4,20},{20... | collective-permute-start | bytes 2359304 | tf_op jit(solution)/shard_map/ppermute | solution.py:345
  50.2 36.6 %all-to-all-start.1 = ((bf16[4,2,2,256,128]{4,3,2,1,0:T(8,128)(2,1)}), bf16[4,2,2,256,128]{4,3,2,1,0:T(8,128)(2,1)S(1)}, u32[]{:S(2)}, u32[]{:S(2)}) async-start(bf16[4,2,2,256,128]{4,3,2,1,0:T(8,128)(2,1)} %pad_maximum_fusion.1), calls=%async_computation.1 | async-start | bytes 2097152 | tf_op jit(solution)/shard_map/all_to_all | solution.py:382
  53.9 33.8 %collective-permute-start.7 = (bf16[4,2,2,256,128]{4,3,2,1,0:T(8,128)(2,1)S(1)}, bf16[4,2,2,256,128]{4,3,2,1,0:T(8,128)(2,1)}, u32[]{:S(2)}, u32[]{:S(2)}) collective-permute-start(bf16[4,2,2,256,128]{4,3,2,1,0:T(8,128)(2,1)S(1)} %all-to-all-done.refs_1_), channel_id=1, source_target_pairs={{0,4},{4,0},{8,12},{12,8},{1,5},{5,1},{9,13},{13,9},{2,6},{6,2},{1... | collective-permute-start | bytes 3145736 | tf_op jit(solution)/shard_map/ppermute | solution.py:405
  55.5 33.8 %collective-permute-start.8 = (bf16[4,2,2,256,128]{4,3,2,1,0:T(8,128)(2,1)S(1)}, bf16[4,2,2,256,128]{4,3,2,1,0:T(8,128)(2,1)}, u32[]{:S(2)}, u32[]{:S(2)}) collective-permute-start(bf16[4,2,2,256,128]{4,3,2,1,0:T(8,128)(2,1)S(1)} %all-to-all-done.refs_1_), channel_id=1, source_target_pairs={{0,1},{1,0},{2,3},{3,2},{4,8},{5,9},{6,10},{7,11},{8,4},{9,5},{10,... | collective-permute-start | bytes 3145736 | tf_op jit(solution)/shard_map/ppermute | solution.py:406
  55.5 14.8 %collective-permute-start.2 = (bf16[2,256,128]{2,1,0:T(8,128)(2,1)S(1)}, bf16[2,256,128]{2,1,0:T(8,128)(2,1)S(1)}, u32[]{:S(2)}, u32[]{:S(2)}) collective-permute-start(bf16[2,256,128]{2,1,0:T(8,128)(2,1)S(1)} %get-tuple-element.29), channel_id=1, source_target_pairs={{0,3},{1,2},{2,1},{3,0},{4,7},{5,6},{6,5},{7,4},{8,11},{9,10},{10,... | collective-permute-start | bytes 393224 | tf_op jit(solution)/shard_map/ppermute | solution.py:387
  56.8 17.0 %collective-permute-start.1 = (bf16[2,256,128]{2,1,0:T(8,128)(2,1)S(1)}, bf16[2,256,128]{2,1,0:T(8,128)(2,1)}, u32[]{:S(2)}, u32[]{:S(2)}) collective-permute-start(bf16[2,256,128]{2,1,0:T(8,128)(2,1)S(1)} %get-tuple-element.30), channel_id=1, source_target_pairs={{0,2},{1,3},{2,0},{3,1},{4,6},{5,7},{6,4},{7,5},{8,10},{9,11},{10,... | collective-permute-start | bytes 393224 | tf_op jit(solution)/shard_map/ppermute | solution.py:387
  70.3 3.5 %collective-permute-start = (bf16[2,256,128]{2,1,0:T(8,128)(2,1)S(1)}, bf16[2,256,128]{2,1,0:T(8,128)(2,1)}, u32[]{:S(2)}, u32[]{:S(2)}) collective-permute-start(bf16[2,256,128]{2,1,0:T(8,128)(2,1)S(1)} %get-tuple-element.31), channel_id=1, source_target_pairs={{0,1},{1,0},{2,3},{3,2},{4,5},{5,4},{6,7},{7,6},{8,9},{9,8},{10,11... | collective-permute-start | bytes 393224 | tf_op jit(solution)/shard_map/ppermute | solution.py:387
  73.8 6.0 %collective-permute-start.6 = (bf16[2,256,128]{2,1,0:T(8,128)(2,1)}, bf16[2,256,128]{2,1,0:T(8,128)(2,1)S(1)}, u32[]{:S(2)}, u32[]{:S(2)}) collective-permute-start(bf16[2,256,128]{2,1,0:T(8,128)(2,1)} %get-tuple-element.25), channel_id=1, source_target_pairs={{0,3},{1,2},{2,1},{3,0},{4,7},{5,6},{6,5},{7,4},{8,11},{9,10},{10,... | collective-permute-start | bytes 393224 | tf_op jit(solution)/shard_map/ppermute | solution.py:387
  73.8 8.2 %collective-permute-start.5 = (bf16[2,256,128]{2,1,0:T(8,128)(2,1)}, bf16[2,256,128]{2,1,0:T(8,128)(2,1)S(1)}, u32[]{:S(2)}, u32[]{:S(2)}) collective-permute-start(bf16[2,256,128]{2,1,0:T(8,128)(2,1)} %get-tuple-element.26), channel_id=1, source_target_pairs={{0,2},{1,3},{2,0},{3,1},{4,6},{5,7},{6,4},{7,5},{8,10},{9,11},{10,... | collective-permute-start | bytes 393224 | tf_op jit(solution)/shard_map/ppermute | solution.py:387
  75.0 9.6 %collective-permute-start.4 = (bf16[2,256,128]{2,1,0:T(8,128)(2,1)S(1)}, bf16[2,256,128]{2,1,0:T(8,128)(2,1)S(1)}, u32[]{:S(2)}, u32[]{:S(2)}) collective-permute-start(bf16[2,256,128]{2,1,0:T(8,128)(2,1)S(1)} %get-tuple-element.27), channel_id=1, source_target_pairs={{0,1},{1,0},{2,3},{3,2},{4,5},{5,4},{6,7},{7,6},{8,9},{9,8},{10,11... | collective-permute-start | bytes 393224 | tf_op jit(solution)/shard_map/ppermute | solution.py:387
  75.7 51.2 %copy-start.3 = (s32[4]{0:T(128)}, s32[4]{0:T(128)S(1)}, u32[]{:S(2)}) copy-start(s32[4]{0:T(128)S(1)} %pad_add_fusion.scalar_ref) | copy-start | bytes 52
  79.8 5.8 %copy-start.10 = (bf16[2,256,128]{2,1,0:T(8,128)(2,1)}, bf16[2,256,128]{2,1,0:T(8,128)(2,1)S(1)}, u32[]{:S(2)}) copy-start(bf16[2,256,128]{2,1,0:T(8,128)(2,1)S(1)} %collective-permute-done.6) | copy-start | bytes 393220
  79.8 20.7 %collective-permute-start.17 = (bf16[1,128,3072]{2,1,0:T(8,128)(2,1)}, bf16[1,128,3072]{2,1,0:T(8,128)(2,1)}, u32[]{:S(2)}, u32[]{:S(2)}) collective-permute-start(bf16[1,128,3072]{2,1,0:T(8,128)(2,1)} %get-tuple-element.17), channel_id=1, source_target_pairs={{0,16},{16,0},{1,17},{17,1},{2,18},{18,2},{3,19},{19,3},{4,20},{20... | collective-permute-start | bytes 2359304 | tf_op jit(solution)/shard_map/ppermute | solution.py:345
  82.0 3.6 %copy-start.11 = (bf16[2,256,128]{2,1,0:T(8,128)(2,1)}, bf16[2,256,128]{2,1,0:T(8,128)(2,1)S(1)}, u32[]{:S(2)}) copy-start(bf16[2,256,128]{2,1,0:T(8,128)(2,1)S(1)} %collective-permute-done.5) | copy-start | bytes 393220
  82.1 34.0 %collective-permute-start.19 = (bf16[1,128,3072]{2,1,0:T(8,128)(2,1)}, bf16[1,128,3072]{2,1,0:T(8,128)(2,1)}, u32[]{:S(2)}, u32[]{:S(2)}) collective-permute-start(bf16[1,128,3072]{2,1,0:T(8,128)(2,1)} %get-tuple-element.15), channel_id=1, source_target_pairs={{0,16},{16,0},{1,17},{17,1},{2,18},{18,2},{3,19},{19,3},{4,20},{20... | collective-permute-start | bytes 2359304 | tf_op jit(solution)/shard_map/ppermute | solution.py:345
  84.6 42.3 %copy-start.1 = (bf16[4,2,256,128]{3,2,1,0:T(8,128)(2,1)}, bf16[4,2,256,128]{3,2,1,0:T(8,128)(2,1)S(1)}, u32[]{:S(2)}) copy-start(bf16[4,2,256,128]{3,2,1,0:T(8,128)(2,1)S(1)} %pad_maximum_fusion.2.refs_0_) | copy-start | bytes 1572868
  84.6 53.8 %collective-permute-start.13 = (bf16[1,128,3072]{2,1,0:T(8,128)(2,1)}, bf16[1,128,3072]{2,1,0:T(8,128)(2,1)}, u32[]{:S(2)}, u32[]{:S(2)}) collective-permute-start(bf16[1,128,3072]{2,1,0:T(8,128)(2,1)} %collective-permute-done.11.refs_1_), channel_id=1, source_target_pairs={{0,2},{1,3},{2,0},{3,1},{4,6},{5,7},{6,4},{7,5},{8,10},{9,11},{10,... | collective-permute-start | bytes 2359304 | tf_op jit(solution)/shard_map/ppermute | solution.py:351
  86.7 40.2 %copy-start.2 = (bf16[4,2,256,128]{3,2,1,0:T(8,128)(2,1)}, bf16[4,2,256,128]{3,2,1,0:T(8,128)(2,1)S(1)}, u32[]{:S(2)}) copy-start(bf16[4,2,256,128]{3,2,1,0:T(8,128)(2,1)S(1)} %pad_maximum_fusion.3.refs_0_.refs_1_) | copy-start | bytes 1572868
  86.7 40.2 %copy-start = (bf16[4,2,2,256,128]{4,3,2,1,0:T(8,128)(2,1)}, bf16[4,2,2,256,128]{4,3,2,1,0:T(8,128)(2,1)S(1)}, u32[]{:S(2)}) copy-start(bf16[4,2,2,256,128]{4,3,2,1,0:T(8,128)(2,1)S(1)} %all-to-all-done.1.refs_4_) | copy-start | bytes 3145732
  87.7 38.6 %collective-permute-start.15 = (bf16[4,1,2,256,128]{4,3,2,1,0:T(8,128)(2,1)S(1)}, bf16[4,1,2,256,128]{4,3,2,1,0:T(8,128)(2,1)S(1)}, u32[]{:S(2)}, u32[]{:S(2)}) collective-permute-start(bf16[4,1,2,256,128]{4,3,2,1,0:T(8,128)(2,1)S(1)} %get-tuple-element.22), channel_id=1, source_target_pairs={{0,4},{4,0},{8,12},{12,8},{1,5},{5,1},{9,13},{13,9},{2,6},{6,2},{1... | collective-permute-start | bytes 1572872 | tf_op jit(solution)/shard_map/ppermute | solution.py:405
  89.3 37.1 %collective-permute-start.16 = (bf16[4,1,2,256,128]{4,3,2,1,0:T(8,128)(2,1)S(1)}, bf16[4,1,2,256,128]{4,3,2,1,0:T(8,128)(2,1)S(1)}, u32[]{:S(2)}, u32[]{:S(2)}) collective-permute-start(bf16[4,1,2,256,128]{4,3,2,1,0:T(8,128)(2,1)S(1)} %get-tuple-element.22), channel_id=1, source_target_pairs={{0,1},{1,0},{2,3},{3,2},{4,8},{5,9},{6,10},{7,11},{8,4},{9,5},{10,... | collective-permute-start | bytes 1572872 | tf_op jit(solution)/shard_map/ppermute | solution.py:406
  99.0 27.9 %copy-start.4 = (f32[4,2,256,256]{3,2,1,0:T(8,128)}, f32[4,2,256,256]{3,2,1,0:T(8,128)S(1)}, u32[]{:S(2)}) copy-start(f32[4,2,256,256]{3,2,1,0:T(8,128)S(1)} %tile_attention.4.refs_2_) | copy-start | bytes 6291460
  100.5 38.3 %collective-permute-start.9 = (bf16[4,1,2,256,128]{4,3,2,1,0:T(8,128)(2,1)}, bf16[4,1,2,256,128]{4,3,2,1,0:T(8,128)(2,1)}, u32[]{:S(2)}, u32[]{:S(2)}) collective-permute-start(bf16[4,1,2,256,128]{4,3,2,1,0:T(8,128)(2,1)} %get-tuple-element.23), channel_id=1, source_target_pairs={{0,4},{4,0},{8,12},{12,8},{1,5},{5,1},{9,13},{13,9},{2,6},{6,2},{1... | collective-permute-start | bytes 1572872 | tf_op jit(solution)/shard_map/ppermute | solution.py:405
  116.1 22.9 %collective-permute-start.10 = (bf16[4,1,2,256,128]{4,3,2,1,0:T(8,128)(2,1)}, bf16[4,1,2,256,128]{4,3,2,1,0:T(8,128)(2,1)}, u32[]{:S(2)}, u32[]{:S(2)}) collective-permute-start(bf16[4,1,2,256,128]{4,3,2,1,0:T(8,128)(2,1)} %get-tuple-element.23), channel_id=1, source_target_pairs={{0,1},{1,0},{2,3},{3,2},{4,8},{5,9},{6,10},{7,11},{8,4},{9,5},{10,... | collective-permute-start | bytes 1572872 | tf_op jit(solution)/shard_map/ppermute | solution.py:406
  126.3 8.6 %copy-start.5 = (f32[4,2,256,256]{3,2,1,0:T(8,128)}, f32[4,2,256,256]{3,2,1,0:T(8,128)S(1)}, u32[]{:S(2)}) copy-start(f32[4,2,256,256]{3,2,1,0:T(8,128)S(1)} %tile_attention.5.refs_3_) | copy-start | bytes 6291460
  126.3 27.0 %collective-permute-start.18 = (bf16[1,128,3072]{2,1,0:T(8,128)(2,1)}, bf16[1,128,3072]{2,1,0:T(8,128)(2,1)}, u32[]{:S(2)}, u32[]{:S(2)}) collective-permute-start(bf16[1,128,3072]{2,1,0:T(8,128)(2,1)} %collective-permute-done.17.refs_1_), channel_id=1, source_target_pairs={{0,1},{1,0},{2,3},{3,2},{4,5},{5,4},{6,7},{7,6},{8,9},{9,8},{10,11... | collective-permute-start | bytes 2359304 | tf_op jit(solution)/shard_map/ppermute | solution.py:422
  126.4 26.9 %collective-permute-start.20 = (bf16[1,128,3072]{2,1,0:T(8,128)(2,1)}, bf16[1,128,3072]{2,1,0:T(8,128)(2,1)}, u32[]{:S(2)}, u32[]{:S(2)}) collective-permute-start(bf16[1,128,3072]{2,1,0:T(8,128)(2,1)} %collective-permute-done.19.refs_3_), channel_id=1, source_target_pairs={{0,1},{1,0},{2,3},{3,2},{4,5},{5,4},{6,7},{7,6},{8,9},{9,8},{10,11... | collective-permute-start | bytes 2359304 | tf_op jit(solution)/shard_map/ppermute | solution.py:422
  134.9 13.7 %all-to-all-start.3 = ((bf16[8,256,128]{2,1,0:T(8,128)(2,1)}), bf16[8,256,128]{2,1,0:T(8,128)(2,1)S(1)}, u32[]{:S(2)}, u32[]{:S(2)}) async-start(bf16[8,256,128]{2,1,0:T(8,128)(2,1)} %bitcast.56), calls=%async_computation.3 | async-start | bytes 1048576 | tf_op jit(solution)/shard_map/all_to_all | solution.py:432
  138.4 22.0 %collective-permute-start.12 = (bf16[1,128,3072]{2,1,0:T(8,128)(2,1)}, bf16[1,128,3072]{2,1,0:T(8,128)(2,1)S(1)}, u32[]{:S(2)}, u32[]{:S(2)}) collective-permute-start(bf16[1,128,3072]{2,1,0:T(8,128)(2,1)} %collective-permute-done.11.refs_1_), channel_id=1, source_target_pairs={{0,1},{1,0},{2,3},{3,2},{4,5},{5,4},{6,7},{7,6},{8,9},{9,8},{10,11... | collective-permute-start | bytes 2359304 | tf_op jit(solution)/shard_map/ppermute | solution.py:422
  138.8 21.6 %collective-permute-start.14 = (bf16[1,128,3072]{2,1,0:T(8,128)(2,1)}, bf16[1,128,3072]{2,1,0:T(8,128)(2,1)S(1)}, u32[]{:S(2)}, u32[]{:S(2)}) collective-permute-start(bf16[1,128,3072]{2,1,0:T(8,128)(2,1)} %collective-permute-done.13.refs_3_), channel_id=1, source_target_pairs={{0,1},{1,0},{2,3},{3,2},{4,5},{5,4},{6,7},{7,6},{8,9},{9,8},{10,11... | collective-permute-start | bytes 2359304 | tf_op jit(solution)/shard_map/ppermute | solution.py:422
  148.6 4.7 %copy-start.6 = (bf16[8,256,128]{2,1,0:T(8,128)(2,1)}, bf16[8,256,128]{2,1,0:T(8,128)(2,1)S(1)}, u32[]{:S(2)}) copy-start(bf16[8,256,128]{2,1,0:T(8,128)(2,1)S(1)} %all-to-all-done.3.attended_ref) | copy-start | bytes 1572868
  148.6 13.8 %all-to-all-start.2 = ((bf16[8,256,128]{2,1,0:T(8,128)(2,1)}), bf16[8,256,128]{2,1,0:T(8,128)(2,1)S(1)}, u32[]{:S(2)}, u32[]{:S(2)}) async-start(bf16[8,256,128]{2,1,0:T(8,128)(2,1)} %bitcast.122), calls=%async_computation.2 | async-start | bytes 1048576 | tf_op jit(solution)/shard_map/all_to_all | solution.py:432
  160.5 1.9 %copy-start.8 = (bf16[1,128,3072]{2,1,0:T(8,128)(2,1)}, bf16[1,128,3072]{2,1,0:T(8,128)(2,1)S(1)}, u32[]{:S(2)}) copy-start(bf16[1,128,3072]{2,1,0:T(8,128)(2,1)S(1)} %collective-permute-done.12.refs_2_) | copy-start | bytes 2359300
  160.5 1.9 %copy-start.9 = (bf16[1,128,3072]{2,1,0:T(8,128)(2,1)}, bf16[1,128,3072]{2,1,0:T(8,128)(2,1)S(1)}, u32[]{:S(2)}) copy-start(bf16[1,128,3072]{2,1,0:T(8,128)(2,1)S(1)} %collective-permute-done.14.refs_4_) | copy-start | bytes 2359300
  162.4 0.8 copy-start.7
